TPU v7x, 256 devices: a whole 4x4x8 slice. The times are simulated.
256 devices in a mesh: lat: 16 (over x, y_hi, core), lon: 16 (over y_lo, z).
Axes of the slice: x: 4, y: 4 (y_hi: 2, y_lo: 2; y = y_hi * 2 + y_lo), z: 8, core: 2. Of those that a mesh axis runs over, the one named last changes fastest.
Arguments:
- feature: bfloat16 [512, 512, 384], P('lat', 'lon'), may hold values from -6 to 6
- coverage: int32 [512, 512], P('lat', 'lon'), may hold values 0 or 1
- band_rows: int32 [16], replicated, may hold values from 3 to 32, as said below
- depth_weight: bfloat16 [7, 7, 384], replicated, may hold values from -0.875 to 0.875
- norm_gain: float32 [384], replicated, may hold values from 0.25 to 1.75
- norm_shift: float32 [384], replicated, may hold values from -3 to 3
- up_weight: bfloat16 [384, 1536], P('lon'), may hold values from -0.3125 to 0.3125
- up_bias: float32 [1536], replicated, may hold values from -3 to 3
- down_weight: bfloat16 [1536, 384], P('lon'), may hold values from -0.15625 to 0.15625
- down_bias: float32 [384], replicated, may hold values from -3 to 3
- layer_scale: float32 [384], replicated, may hold values from 0.3 to 1.5
- cotangent: bfloat16 [512, 512, 384], P('lat', 'lon'), may hold values from -6 to 6
Outputs:
- block_out: bfloat16 [512, 512, 384], P('lat', 'lon')
- grad_in: bfloat16 [512, 512, 384], P('lat', 'lon')
- grad_up: float32 [384, 1536], P('lon')
- grad_down: float32 [1536, 384], P('lon')
- grad_depth: float32 [7, 7, 384], replicated
Inputs may be any that keep to these rules, and one draw needn't show every extreme that they name: `band_rows`: every band has 3 or more rows, the bands' rows sum to 256, and one band has exactly 32.
All inputs are finite; a program needn't handle non-finite values. No bound on the sum of `coverage` on one device may be relied on, other than what follows from the above.
Results may differ from a plain program's by a relative error of at most 0.0066.
Values may be sent and summed in bfloat16 or wider, within the bound.
A program may use at most 64 MiB of HBM per device.

v0:
```python
import math

import jax
import jax.numpy as jnp
from jax import lax
from jax.sharding import PartitionSpec as P

BAND_MEAN = 16


SQRT_TWO_PI = 0.7978845608028654
CUBIC = 0.044715
EPSILON = 1e-06


def padded(array, sides, width):
    for axis, dim in sides:
        size, length = (lax.axis_size(axis), array.shape[dim])
        up = [(i, (i + 1) % size) for i in range(size)]
        down = [(j, i) for i, j in up]
        last = lax.slice_in_dim(array, length - width, length, axis=dim)
        initial = lax.slice_in_dim(array, 0, width, axis=dim)
        before = lax.ppermute(last, axis, up)
        after = lax.ppermute(initial, axis, down)
        array = jnp.concatenate([before, array, after], axis=dim)
    return array


def shifted(block, axis, distance):
    devices = range(lax.axis_size(axis))
    route = [(i - distance, i) for i in devices if i - distance in devices]
    return lax.ppermute(block, axis, route)


def smooth_gate(pre_act):
    argument = SQRT_TWO_PI * (pre_act + CUBIC * pre_act * pre_act * pre_act)
    return 0.5 * pre_act * (1.0 + jnp.tanh(argument))


def smooth_slope(pre_act):
    argument = SQRT_TWO_PI * (pre_act + CUBIC * pre_act * pre_act * pre_act)
    tangent = jnp.tanh(argument)
    return 0.5 * (1.0 + tangent) + 0.5 * pre_act * (1.0 - tangent * tangent) * SQRT_TWO_PI * (
        1.0 + 3.0 * CUBIC * pre_act * pre_act
    )


def extend(field, live_rows):
    widened = padded(field, (("lon", 1),), 3)
    last_rows = lax.dynamic_slice_in_dim(widened, live_rows - 3, 3, 0)
    from_above = shifted(last_rows, "lat", 1)
    from_below = shifted(widened[:3], "lat", -1)
    zero_rows = jnp.zeros((3,) + widened.shape[1:], widened.dtype)
    stacked = jnp.concatenate([from_above, widened, zero_rows], axis=0)
    return lax.dynamic_update_slice_in_dim(stacked, from_below, live_rows + 3, 0)


def shards(
    feature,
    coverage,
    band_rows,
    depth_weight,
    norm_gain,
    norm_shift,
    up_weight,
    up_bias,
    down_weight,
    down_bias,
    layer_scale,
    cotangent,
):
    rows_max, tile_cols, channels = feature.shape
    kernel = depth_weight.shape[0]
    live_rows = lax.dynamic_index_in_dim(band_rows, lax.axis_index("lat"), 0, keepdims=False)
    inside = jnp.arange(rows_max, dtype=jnp.int32) < live_rows
    covered = jnp.where(inside[:, None], coverage, 0).astype(jnp.bfloat16)
    masked = feature * covered[:, :, None]
    framed = extend(masked, live_rows)
    depth_out = jnp.zeros((rows_max, tile_cols, channels), jnp.float32)
    for row_off in range(kernel):
        for col_off in range(kernel):
            depth_out = depth_out + framed[
                row_off : row_off + rows_max, col_off : col_off + tile_cols
            ].astype(jnp.float32) * depth_weight[row_off, col_off].astype(jnp.float32)
    full_up, full_down = (
        lax.all_gather(up_weight, "lon", axis=0, tiled=True),
        lax.all_gather(down_weight, "lon", axis=0, tiled=True),
    )
    depth_rows = depth_out.reshape(-1, channels)
    center = jnp.mean(depth_rows, axis=-1, keepdims=True)
    offset = depth_rows - center
    scale_inv = lax.rsqrt(jnp.mean(offset * offset, axis=-1, keepdims=True) + EPSILON)
    standard = offset * scale_inv
    normed = (standard * norm_gain + norm_shift).astype(jnp.bfloat16)
    before = jnp.dot(normed, full_up, preferred_element_type=jnp.float32) + up_bias
    active = smooth_gate(before).astype(jnp.bfloat16)
    branch = jnp.dot(active, full_down, preferred_element_type=jnp.float32) + down_bias
    result = (feature.reshape(-1, channels).astype(jnp.float32) + layer_scale * branch).astype(
        jnp.bfloat16
    )
    cot_live = jnp.where(inside[:, None, None], cotangent, jnp.zeros_like(cotangent)).reshape(
        -1, channels
    )
    upstream = (layer_scale * cot_live.astype(jnp.float32)).astype(jnp.bfloat16)
    sum_down = lax.dot_general(
        active, upstream, (((0,), (0,)), ((), ())), preferred_element_type=jnp.float32
    )
    back_active = lax.dot_general(
        upstream, full_down, (((1,), (1,)), ((), ())), preferred_element_type=jnp.float32
    )
    back_before = (back_active * smooth_slope(before)).astype(jnp.bfloat16)
    sum_up = lax.dot_general(
        normed, back_before, (((0,), (0,)), ((), ())), preferred_element_type=jnp.float32
    )
    back_normed = lax.dot_general(
        back_before, full_up, (((1,), (1,)), ((), ())), preferred_element_type=jnp.float32
    )
    back_unit = back_normed * norm_gain
    back_depth = scale_inv * (
        back_unit
        - jnp.mean(back_unit, axis=-1, keepdims=True)
        - standard * jnp.mean(back_unit * standard, axis=-1, keepdims=True)
    )
    back_depth = back_depth.astype(jnp.bfloat16).reshape(rows_max, tile_cols, channels)
    framed_back = extend(back_depth, live_rows)
    spread = jnp.zeros((rows_max, tile_cols, channels), jnp.float32)
    tap_list = []
    for row_off in range(kernel):
        for col_off in range(kernel):
            spread = spread + framed_back[
                6 - row_off : 6 - row_off + rows_max, 6 - col_off : 6 - col_off + tile_cols
            ].astype(jnp.float32) * depth_weight[row_off, col_off].astype(jnp.float32)
            tap_list.append(
                jnp.sum(
                    framed[row_off : row_off + rows_max, col_off : col_off + tile_cols].astype(
                        jnp.float32
                    )
                    * back_depth.astype(jnp.float32),
                    axis=(0, 1),
                )
            )
    grad_local = (
        cotangent.astype(jnp.float32) + covered.astype(jnp.float32)[:, :, None] * spread
    ).astype(jnp.bfloat16)
    grad_in = jnp.where(inside[:, None, None], grad_local, jnp.zeros_like(grad_local))
    block_out = jnp.where(
        inside[:, None, None],
        result.reshape(rows_max, tile_cols, channels),
        jnp.zeros_like(feature),
    )
    rscale = 1.0 / math.sqrt(BAND_MEAN * lax.axis_size("lat") * tile_cols * lax.axis_size("lon"))
    tap_terms = jnp.stack(tap_list, axis=0).reshape(kernel, kernel, channels)
    grad_depth = lax.psum(tap_terms, ("lat", "lon")) * rscale
    up_part, down_part = (
        lax.psum_scatter(sum_up, "lon", scatter_dimension=0, tiled=True),
        lax.psum_scatter(sum_down, "lon", scatter_dimension=0, tiled=True),
    )
    up_part, down_part = lax.psum((up_part, down_part), "lat")
    return (block_out, grad_in, up_part * rscale, down_part * rscale, grad_depth)


def solution(mesh):
    placed = (
        P("lat", "lon", None),
        P("lat", "lon"),
        P(),
        P(),
        P(),
        P(),
        P("lon", None),
        P(),
        P("lon", None),
        P(),
        P(),
        P("lat", "lon", None),
    )
    return jax.shard_map(
        shards,
        mesh=mesh,
        in_specs=placed,
        out_specs=(
            P("lat", "lon", None),
            P("lat", "lon", None),
            P("lon", None),
            P("lon", None),
            P(),
        ),
        check_vma=False,
    )
```

profile of v0, /device:TPU:1, one launch (start us, length us, event | category | flops | bytes accessed | tf_op | source)
XLA Modules:
  0.0 711.0 jit_solution(1951065629706237876)
XLA Ops:
  8.0 1.2 dynamic_slice.10
  10.7 1.3 broadcast_multiply_fusion
  12.1 2.5 collective-permute-start
  14.6 5.0 collective-permute-start.1
  24.2 5.4 collective-permute-start.2
  30.3 1.9 collective-permute-start.3
  33.3 5.1 collective-permute-done.3
  38.8 12.5 %fusion.109 = (f32[32,32]{1,0:T(8,128)S(1)}, f32[32,32,384]{2,1,0:T(8,128)S(1)}) fusion(f32[384]{0:T(512)} %get-tuple-element.103, bf16[38,38,384]{2,1,0:T(8,128)(2,1)S(1)} %constant_dynamic-update-slice_fusion.1, f32[384]{0:T(512)} %get-tuple-element.104, f32[384]{0:T(512)S(1)} %get-tuple-element.57, f32[384]{0:T(512)S(1)} %get-tuple-element.58, ...), kind=kLoop, calls=%fused_computation.289 | loop fusion | flops 57801728 | bytes 40187392 | tf_op jit(solution)/shard_map/reduce_sum | solution.py:90
  53.3 19.7 %all-gather.3.cloned.1.call-done = bf16[384,1536]{1,0:T(8,128)(2,1)} async-done(((bf16[24,1536]{1,0:T(8,128)(2,1)}), bf16[384,1536]{1,0:T(8,128)(2,1)}) %all-gather.3.cloned.1.call-update) | async-done | bytes 1179664 | tf_op jit(solution)/shard_map/all_gather | solution.py:86
  73.1 7.8 %multiply_convert_fusion = (bf16[1024,1536]{1,0:T(8,128)(2,1)}, f32[1024,1536]{1,0:T(8,128)}) fusion(f32[1536]{0:T(1024)} %param.19, bf16[1024,384]{1,0:T(8,128)(2,1)} %add_convert_fusion.1, bf16[384,1536]{1,0:T(8,128)(2,1)} %all-gather.3.cloned.1.call-done), kind=kOutput, calls=%fused_computation.58 | convolution fusion | flops 1223688192 | bytes 11409408 | tf_op jit(solution)/shard_map/dot_general | solution.py:95
  80.9 61.0 %all-gather.5.cloned.1.call-done = bf16[1536,384]{1,0:T(8,128)(2,1)} async-done(((bf16[96,384]{1,0:T(8,128)(2,1)}), bf16[1536,384]{1,0:T(8,128)(2,1)}) %all-gather.5.cloned.1.call-update) | async-done | bytes 1179664 | tf_op jit(solution)/shard_map/all_gather | solution.py:87
  141.9 4.2 fusion.105
  148.8 5.4 fusion.6
  154.2 2.0 fusion.107
  156.2 5.0 fusion.103
  161.2 3.0 fusion.67
  164.2 4.0 fusion.85
  169.7 5.2 fusion.116
  176.0 4.7 fusion.115
  181.4 3.1 collective-permute-start.5
  184.5 2.0 collective-permute-done.4
  187.5 16.5 %collective-permute-start.6 = (bf16[3,38,384]{2,1,0:T(8,128)(2,1)S(1)}, bf16[3,38,384]{2,1,0:T(8,128)(2,1)S(1)}, u32[]{:S(2)}, u32[]{:S(2)}) collective-permute-start(bf16[3,38,384]{2,1,0:T(8,128)(2,1)S(1)} %get-tuple-element.113), channel_id=1, source_target_pairs={{0,16},{16,32},{32,48},{48,64},{64,80},{80,96},{96,112},{112,128},... | collective-permute-start | bytes 262664 | tf_op jit(solution)/shard_map/ppermute | solution.py:32
  204.0 214.4 %all-reduce.4.cloned.1.call-done = f32[7,7,384]{2,1,0:T(8,128)} async-done(((f32[7,7,384]{2,1,0:T(8,128)}), f32[7,7,384]{2,1,0:T(8,128)}) %all-reduce.4.cloned.1.call-update) | async-done | bytes 75280 | tf_op jit(solution)/shard_map/psum | solution.py:153
  418.4 1.5 broadcast_multiply_fusion.3
  420.0 1.9 collective-permute-start.7
  423.0 4.3 collective-permute-done.7
  427.4 53.8 %reduce-scatter.5.cloned.1.call-done = f32[96,384]{1,0:T(8,128)} async-done(((f32[1536,384]{1,0:T(8,128)}), f32[96,384]{1,0:T(8,128)}) %reduce-scatter.5.cloned.1.call-update) | async-done | bytes 147472 | tf_op jit(solution)/shard_map/reduce_scatter | solution.py:156
  481.1 73.6 %reduce-scatter.3.cloned.1.call-done = f32[24,1536]{1,0:T(8,128)} async-done(((f32[384,1536]{1,0:T(8,128)}), f32[24,1536]{1,0:T(8,128)}) %reduce-scatter.3.cloned.1.call-update) | async-done | bytes 147472 | tf_op jit(solution)/shard_map/reduce_scatter | solution.py:155
  555.1 12.6 %broadcast_select_fusion = bf16[32,32,384]{2,1,0:T(8,128)(2,1)} fusion(pred[32]{0:T(512)(128)(4,1)} %copy-done.85, f32[384]{0:T(512)} %get-tuple-element.103, bf16[38,38,384]{2,1,0:T(8,128)(2,1)S(1)} %constant_dynamic-update-slice_fusion, f32[384]{0:T(512)} %get-tuple-element.104, f32[384]{0:T(512)S(1)} %copy-done.46, f32[384]{0:T(512)S(1)} %copy-done.48, ...), kind=kLoop, calls=%fused_computation.221 | loop fusion | flops 59375616 | bytes 40187424 | tf_op jit(solution)/shard_map/jit(_where)/select_n | solution.py:145
  567.7 133.3 %all-reduce.6.cloned.1.call-done = (f32[24,1536]{1,0:T(8,128)}, f32[96,384]{1,0:T(8,128)}) async-done(((f32[24,1536]{1,0:T(8,128)}, f32[96,384]{1,0:T(8,128)}), (f32[24,1536]{1,0:T(8,128)}, f32[96,384]{1,0:T(8,128)})) %all-reduce.6.cloned.1.call-update) | async-done | bytes 294928 | tf_op jit(solution)/shard_map/psum | solution.py:158
  701.0 1.6 broadcast_multiply_fusion.2
  702.5 1.6 broadcast_multiply_fusion.1
  (287 shorter events, 15.0 us)
Async XLA Ops:
  7.2 65.9 %all-gather.3.cloned.1.call-start = ((), (), s32[]{:S(2)}) async-start(), calls=%async_computation.2 | async-start | bytes 1253376 | tf_op jit(solution)/shard_map/all_gather | solution.py:86
  7.9 134.0 %all-gather.5.cloned.1.call-start = ((), (), s32[]{:S(2)}) async-start(), calls=%async_computation.3 | async-start | bytes 1253376 | tf_op jit(solution)/shard_map/all_gather | solution.py:87
  12.1 11.5 %collective-permute-start = (bf16[32,3,384]{2,1,0:T(4,128)(2,1)S(1)}, bf16[32,3,384]{2,1,0:T(4,128)(2,1)S(1)}, u32[]{:S(2)}, u32[]{:S(2)}) collective-permute-start(bf16[32,3,384]{2,1,0:T(4,128)(2,1)S(1)} %get-tuple-element.118), channel_id=1, source_target_pairs={{0,1},{1,2},{2,3},{3,4},{4,5},{5,6},{6,7},{7,8},{8,9},{9,10},{10,1... | collective-permute-start | bytes 221192 | tf_op jit(solution)/shard_map/ppermute | solution.py:23
  14.6 9.0 %collective-permute-start.1 = (bf16[32,3,384]{2,1,0:T(4,128)(2,1)S(1)}, bf16[32,3,384]{2,1,0:T(4,128)(2,1)S(1)}, u32[]{:S(2)}, u32[]{:S(2)}) collective-permute-start(bf16[32,3,384]{2,1,0:T(4,128)(2,1)S(1)} %get-tuple-element.119), channel_id=1, source_target_pairs={{1,0},{2,1},{3,2},{4,3},{5,4},{6,5},{7,6},{8,7},{9,8},{10,9},{11,1... | collective-permute-start | bytes 221192 | tf_op jit(solution)/shard_map/ppermute | solution.py:24
  19.7 398.7 %all-reduce.4.cloned.1.call-start = ((), (), s32[]{:S(2)}) async-start(), calls=%async_computation.6 | async-start | bytes 172032 | tf_op jit(solution)/shard_map/psum | solution.py:153
  24.2 8.0 %collective-permute-start.2 = (bf16[3,38,384]{2,1,0:T(8,128)(2,1)S(1)}, bf16[3,38,384]{2,1,0:T(8,128)(2,1)S(1)}, u32[]{:S(2)}, u32[]{:S(2)}) collective-permute-start(bf16[3,38,384]{2,1,0:T(8,128)(2,1)S(1)} %get-tuple-element.115), channel_id=1, source_target_pairs={{0,16},{16,32},{32,48},{48,64},{64,80},{80,96},{96,112},{112,128},... | collective-permute-start | bytes 262664 | tf_op jit(solution)/shard_map/ppermute | solution.py:32
  30.3 8.2 %collective-permute-start.3 = (bf16[3,38,384]{2,1,0:T(8,128)(2,1)S(1)}, bf16[3,38,384]{2,1,0:T(8,128)(2,1)S(1)}, u32[]{:S(2)}, u32[]{:S(2)}) collective-permute-start(bf16[3,38,384]{2,1,0:T(8,128)(2,1)S(1)} %get-tuple-element.114), channel_id=1, source_target_pairs={{16,0},{32,16},{48,32},{64,48},{80,64},{96,80},{112,96},{128,112},... | collective-permute-start | bytes 262664 | tf_op jit(solution)/shard_map/ppermute | solution.py:32
  169.6 311.5 %reduce-scatter.5.cloned.1.call-start = ((), (), s32[]{:S(2)}) async-start(), calls=%async_computation.5 | async-start | bytes 2506752 | tf_op jit(solution)/shard_map/reduce_scatter | solution.py:156
  174.9 379.8 %reduce-scatter.3.cloned.1.call-start = ((), (), s32[]{:S(2)}) async-start(), calls=%async_computation.4 | async-start | bytes 2506752 | tf_op jit(solution)/shard_map/reduce_scatter | solution.py:155
  180.7 520.2 %all-reduce.6.cloned.1.call-start = ((), (), s32[]{:S(2)}) async-start(), calls=%async_computation.7 | async-start | bytes 589824 | tf_op jit(solution)/shard_map/psum | solution.py:158
  180.9 5.7 collective-permute-start.4
  181.4 5.1 collective-permute-start.5
  187.1 367.6 %copy-start.1 = (bf16[32,32,384]{2,1,0:T(8,128)(2,1)S(1)}, bf16[32,32,384]{2,1,0:T(8,128)(2,1)}, u32[]{:S(2)}) copy-start(bf16[32,32,384]{2,1,0:T(8,128)(2,1)} %param.23) | copy-start | bytes 2359300
  187.1 367.6 %copy-start.8 = (f32[384]{0:T(512)S(1)}, f32[384]{0:T(512)}, u32[]{:S(2)}) copy-start(f32[384]{0:T(512)} %copy-done.7) | copy-start | bytes 4612
  187.1 367.6 %copy-start.10 = (f32[384]{0:T(512)S(1)}, f32[384]{0:T(512)}, u32[]{:S(2)}) copy-start(f32[384]{0:T(512)} %copy-done.9) | copy-start | bytes 4612
  187.1 367.6 %copy-start.12 = (f32[384]{0:T(512)S(1)}, f32[384]{0:T(512)}, u32[]{:S(2)}) copy-start(f32[384]{0:T(512)} %copy-done.11) | copy-start | bytes 4612
  187.1 367.6 %copy-start.14 = (f32[384]{0:T(512)S(1)}, f32[384]{0:T(512)}, u32[]{:S(2)}) copy-start(f32[384]{0:T(512)} %copy-done.13) | copy-start | bytes 4612
  187.1 367.6 %copy-start.16 = (f32[384]{0:T(512)S(1)}, f32[384]{0:T(512)}, u32[]{:S(2)}) copy-start(f32[384]{0:T(512)} %copy-done.15) | copy-start | bytes 4612
  187.1 367.6 %copy-start.18 = (f32[384]{0:T(512)S(1)}, f32[384]{0:T(512)}, u32[]{:S(2)}) copy-start(f32[384]{0:T(512)} %copy-done.17) | copy-start | bytes 4612
  187.2 367.6 %copy-start.20 = (f32[384]{0:T(512)S(1)}, f32[384]{0:T(512)}, u32[]{:S(2)}) copy-start(f32[384]{0:T(512)} %copy-done.19) | copy-start | bytes 4612
  187.2 367.6 %copy-start.22 = (f32[384]{0:T(512)S(1)}, f32[384]{0:T(512)}, u32[]{:S(2)}) copy-start(f32[384]{0:T(512)} %copy-done.21) | copy-start | bytes 4612
  187.2 367.6 %copy-start.24 = (f32[384]{0:T(512)S(1)}, f32[384]{0:T(512)}, u32[]{:S(2)}) copy-start(f32[384]{0:T(512)} %copy-done.23) | copy-start | bytes 4612
  187.2 367.6 %copy-start.26 = (f32[384]{0:T(512)S(1)}, f32[384]{0:T(512)}, u32[]{:S(2)}) copy-start(f32[384]{0:T(512)} %copy-done.25) | copy-start | bytes 4612
  187.2 367.6 %copy-start.28 = (f32[384]{0:T(512)S(1)}, f32[384]{0:T(512)}, u32[]{:S(2)}) copy-start(f32[384]{0:T(512)} %copy-done.27) | copy-start | bytes 4612
  187.2 367.6 %copy-start.30 = (f32[384]{0:T(512)S(1)}, f32[384]{0:T(512)}, u32[]{:S(2)}) copy-start(f32[384]{0:T(512)} %copy-done.29) | copy-start | bytes 4612
  187.2 367.6 %copy-start.32 = (f32[384]{0:T(512)S(1)}, f32[384]{0:T(512)}, u32[]{:S(2)}) copy-start(f32[384]{0:T(512)} %copy-done.31) | copy-start | bytes 4612
  187.2 367.6 %copy-start.34 = (f32[384]{0:T(512)S(1)}, f32[384]{0:T(512)}, u32[]{:S(2)}) copy-start(f32[384]{0:T(512)} %copy-done.33) | copy-start | bytes 4612
  187.2 367.6 %copy-start.36 = (f32[384]{0:T(512)S(1)}, f32[384]{0:T(512)}, u32[]{:S(2)}) copy-start(f32[384]{0:T(512)} %copy-done.35) | copy-start | bytes 4612
  187.2 367.6 %copy-start.38 = (f32[384]{0:T(512)S(1)}, f32[384]{0:T(512)}, u32[]{:S(2)}) copy-start(f32[384]{0:T(512)} %copy-done.37) | copy-start | bytes 4612
  187.3 367.6 %copy-start.40 = (f32[384]{0:T(512)S(1)}, f32[384]{0:T(512)}, u32[]{:S(2)}) copy-start(f32[384]{0:T(512)} %copy-done.39) | copy-start | bytes 4612
  187.5 234.4 %collective-permute-start.6 = (bf16[3,38,384]{2,1,0:T(8,128)(2,1)S(1)}, bf16[3,38,384]{2,1,0:T(8,128)(2,1)S(1)}, u32[]{:S(2)}, u32[]{:S(2)}) collective-permute-start(bf16[3,38,384]{2,1,0:T(8,128)(2,1)S(1)} %get-tuple-element.113), channel_id=1, source_target_pairs={{0,16},{16,32},{32,48},{48,64},{64,80},{80,96},{96,112},{112,128},... | collective-permute-start | bytes 262664 | tf_op jit(solution)/shard_map/ppermute | solution.py:32
  420.0 7.4 %collective-permute-start.7 = (bf16[3,38,384]{2,1,0:T(8,128)(2,1)S(1)}, bf16[3,38,384]{2,1,0:T(8,128)(2,1)S(1)}, u32[]{:S(2)}, u32[]{:S(2)}) collective-permute-start(bf16[3,38,384]{2,1,0:T(8,128)(2,1)S(1)} %get-tuple-element.112), channel_id=1, source_target_pairs={{16,0},{32,16},{48,32},{64,48},{80,64},{96,80},{112,96},{128,112},... | collective-permute-start | bytes 262664 | tf_op jit(solution)/shard_map/ppermute | solution.py:32
  (78 other events, 8857.2 us)
Sparse Core Ops, SparseCore 0:
  9.8 63.2 all-gather.2
  74.8 67.0 all-gather.4
  169.7 248.6 all-reduce.3
  420.8 60.2 reduce-scatter.4
  483.5 71.1 reduce-scatter.2
  557.3 143.6 all-reduce.5
where the time goes:
time: 712 us; the launch traced here: 711 us
  waiting for transfers between devices  568 us (80%)
  other arithmetic  51.7 us (7%)
  starting transfers between devices  37.2 us (5%)
  matrix products  29.3 us (4%)
  between operations  18.7 us (3%)
    psum x1, waiting for transfers between devices, shards(): grad_depth = lax.psum(tap_terms, ('lat', 'lon')) * rscale  214 us
    psum x1, waiting for transfers between devices, shards(): up_part, down_part = lax.psum((up_part, down_part), 'lat')  133 us
    reduce_scatter x1, waiting for transfers between devices, shards(): lax.psum_scatter(sum_up, 'lon', scatter_dimension=0, tiled=True)  73.6 us
    all_gather x1, waiting for transfers between devices, shards(): lax.all_gather(down_weight, 'lon', axis=0, tiled=True)  61 us
    reduce_scatter x1, waiting for transfers between devices, shards(): lax.psum_scatter(sum_down, 'lon', scatter_dimension=0, tiled=True)  53.8 us
    ppermute x4, starting transfers between devices, shifted(): return lax.ppermute(block, axis, route)  25.7 us
    all_gather x1, waiting for transfers between devices, shards(): lax.all_gather(up_weight, 'lon', axis=0, tiled=True)  19.7 us
  transfers between devices with their start and end apart: 14, of which 9 were waited for; matrix products, arithmetic and copies ran while one was open for 8% of the time, Pallas kernels for 0%

commit v1 on v0

--- a/solution.py
+++ b/solution.py
@@ -1,8 +1,11 @@
+import functools
 import math
 
 import jax
 import jax.numpy as jnp
 from jax import lax
+from jax.experimental import pallas as pl
+from jax.experimental.pallas import tpu as pltpu
 from jax.sharding import PartitionSpec as P
 
 BAND_MEAN = 16
@@ -53,6 +56,335 @@
     zero_rows = jnp.zeros((3,) + widened.shape[1:], widened.dtype)
     stacked = jnp.concatenate([from_above, widened, zero_rows], axis=0)
     return lax.dynamic_update_slice_in_dim(stacked, from_below, live_rows + 3, 0)
+
+
+def places():
+    lat, lon = lax.axis_index("lat"), lax.axis_index("lon")
+    return lat, lon, lat // 4, (lat // 2) % 2, lat % 2, lon // 8, lon % 8
+
+
+def remote(src, dst, sends, recvs, slot, device):
+    return pltpu.make_async_remote_copy(
+        src_ref=src,
+        dst_ref=dst,
+        send_sem=sends.at[slot],
+        recv_sem=recvs.at[slot],
+        device_id=device,
+        device_id_type=pl.DeviceIdType.MESH,
+    )
+
+
+def greet(peers):
+    barrier = pltpu.get_barrier_semaphore()
+    for peer in peers:
+        pl.semaphore_signal(barrier, inc=1, device_id=peer, device_id_type=pl.DeviceIdType.MESH)
+    pl.semaphore_wait(barrier, len(peers))
+
+
+def gather_kernel(up_ref, down_ref, full_up, full_down, sends, recvs):
+    lat, lon, x, yh, c, yl, z = places()
+    loop = [(lat, yl * 8 + (z + k) % 8) for k in range(1, 8)]
+    across = (lat, (1 - yl) * 8 + z)
+    twin = (lat + 1 - 2 * c, lon)
+    greet(loop + [across, twin])
+
+    def parts(up, down, block, half):
+        lanes = pl.ds(pl.multiple_of(half * 768, 768), 768)
+        return (
+            up.at[pl.ds(block * 3, 3), :, lanes],
+            down.at[pl.ds(block * 12 + half * 6, 6)],
+        )
+
+    def copies(block, half, base, device, own=False):
+        sources = parts(up_ref, down_ref, 0, half) if own else parts(full_up, full_down, block, half)
+        targets = parts(full_up, full_down, block, half)
+        return [
+            remote(sources[i], targets[i], sends, recvs, base * 2 + i, device) for i in range(2)
+        ]
+
+    started = []
+
+    def launch(pair):
+        for copy in pair:
+            copy.start()
+        started.extend(pair)
+
+    for k in (4, 3, 5, 2, 6, 1, 7):
+        launch(copies(lon, c, k - 1, loop[k - 1], own=True))
+    launch(copies(lon, c, 7, across, own=True))
+    full_up[pl.ds(lon * 3, 3)] = up_ref[...]
+    full_down[pl.ds(lon * 12, 12)] = down_ref[...]
+    for k in (1, 7, 2, 6, 3, 5, 4):
+        block = yl * 8 + (z + 8 - k) % 8
+        for copy in copies(block, c, k - 1, across):
+            copy.wait_recv()
+        launch(copies(block, c, 7 + k, across))
+        launch(copies(block, c, 14 + k, twin))
+    for k in (0, 1, 7, 2, 6, 3, 5, 4):
+        block = (1 - yl) * 8 + (z + 8 - k) % 8
+        for copy in copies(block, c, 7 + k, across):
+            copy.wait_recv()
+        launch(copies(block, c, 22 + k, twin))
+    for k in range(1, 8):
+        block = yl * 8 + (z + 8 - k) % 8
+        for copy in copies(block, 1 - c, 14 + k, twin):
+            copy.wait_recv()
+    for k in range(8):
+        block = (1 - yl) * 8 + (z + 8 - k) % 8
+        for copy in copies(block, 1 - c, 22 + k, twin):
+            copy.wait_recv()
+    for copy in started:
+        copy.wait_send()
+
+
+def gather_weights(up_weight, down_weight):
+    vmem = pl.BlockSpec(memory_space=pltpu.VMEM)
+    full_up, full_down = pl.pallas_call(
+        gather_kernel,
+        out_shape=(
+            jax.ShapeDtypeStruct((48, 8, 1536), jnp.bfloat16),
+            jax.ShapeDtypeStruct((192, 8, 384), jnp.bfloat16),
+        ),
+        in_specs=[vmem, vmem],
+        out_specs=(vmem, vmem),
+        scratch_shapes=[pltpu.SemaphoreType.DMA((60,)), pltpu.SemaphoreType.DMA((60,))],
+        compiler_params=pltpu.CompilerParams(collective_id=1, has_side_effects=True),
+        name="gather_weights",
+    )(up_weight.reshape(3, 8, 1536), down_weight.reshape(12, 8, 384))
+    return full_up.reshape(384, 1536), full_down.reshape(1536, 384)
+
+
+def sum_kernel(
+    rscale, up_ref, down_ref, up_out, down_out, twin_send, twin_recv, x_send, x_recv,
+    total, y_send, y_recv, z_send, z_recv, h_send, h_recv, pieces, others, sends, recvs,
+):
+    lat, lon, x, yh, c, yl, z = places()
+    f32, bf16 = jnp.float32, jnp.bfloat16
+    twin = (lat + 1 - 2 * c, lon)
+    column = [(((x + k) % 4) * 4 + yh * 2 + c, lon) for k in range(1, 4)]
+    across = (lat, (1 - yl) * 8 + z)
+    loop = [(lat, yl * 8 + (z + k) % 8) for k in range(1, 8)]
+    far = (lat + 2 - 4 * yh, lon)
+    greet([twin] + column + [across] + loop + [far])
+    started = []
+
+    def launch(copy):
+        copy.start()
+        started.append(copy)
+        return copy
+
+    order = (2, 1, 3, 0)
+
+    def chunk_of(k):
+        return (x + k) % 4
+
+    def up_part(part):
+        return up_ref[:, :, pl.ds(pl.multiple_of(part * 384, 384), 384)]
+
+    twin_copies = {}
+    for k in order:
+        part = chunk_of(k)
+
+        @pl.when(c == 1)
+        def _():
+            twin_send[k] = up_part(part).astype(bf16)
+
+        @pl.when(c == 0)
+        def _():
+            @pl.loop(0, 16)
+            def _(block):
+                twin_send[k, pl.ds(block * 3, 3)] = down_ref[
+                    pl.ds(block * 12 + part * 3, 3)
+                ].astype(bf16)
+
+        twin_copies[k] = launch(
+            remote(twin_send.at[k], twin_recv.at[k], sends, recvs, k, twin)
+        )
+    for k in order:
+        part = chunk_of(k)
+        twin_copies[k].wait_recv()
+
+        @pl.when(c == 0)
+        def _():
+            total[...] = up_part(part) + twin_recv[k].astype(f32)
+
+        @pl.when(c == 1)
+        def _():
+            @pl.loop(0, 16)
+            def _(block):
+                total[pl.ds(block * 3, 3)] = down_ref[
+                    pl.ds(block * 12 + part * 3, 3)
+                ] + twin_recv[k, pl.ds(block * 3, 3)].astype(f32)
+
+        if k:
+            x_send[k - 1] = total[...].astype(bf16)
+            launch(
+                remote(x_send.at[k - 1], x_recv.at[k - 1], sends, recvs, 3 + k, column[k - 1])
+            )
+    for k in (1, 3, 2):
+        remote(x_send.at[k - 1], x_recv.at[k - 1], sends, recvs, 3 + k, column[k - 1]).wait_recv()
+    far_half = pl.ds((1 - yl) * 24, 24)
+    near_half = pl.ds(yl * 24, 24)
+
+    def summed(rows):
+        return total[rows] + (
+            x_recv[0, rows].astype(f32) + x_recv[1, rows].astype(f32) + x_recv[2, rows].astype(f32)
+        )
+
+    y_send[...] = summed(far_half).astype(bf16)
+    y_copy = launch(remote(y_send, y_recv, sends, recvs, 7, across))
+    total[near_half] = summed(near_half)
+    y_copy.wait_recv()
+    for k in (4, 3, 5, 2, 6, 1, 7):
+        zk = (z + k) % 8
+        z_send[k - 1] = (
+            total[pl.ds(yl * 24 + zk * 3, 3)] + y_recv[pl.ds(zk * 3, 3)].astype(f32)
+        ).astype(bf16)
+        launch(remote(z_send.at[k - 1], z_recv.at[k - 1], sends, recvs, 7 + k, loop[k - 1]))
+    piece = total[pl.ds(yl * 24 + z * 3, 3)] + y_recv[pl.ds(z * 3, 3)].astype(f32)
+    for k in (1, 7, 2, 6, 3, 5, 4):
+        remote(z_send.at[k - 1], z_recv.at[k - 1], sends, recvs, 7 + k, loop[k - 1]).wait_recv()
+        piece = piece + z_recv[k - 1].astype(f32)
+    h_send[...] = piece
+    far_copy = launch(remote(h_send, h_recv, sends, recvs, 15, far))
+    far_copy.wait_recv()
+    pieces[x] = (piece + h_recv[...]) * rscale
+    for k in range(1, 4):
+        launch(remote(pieces.at[x], pieces.at[x], sends, recvs, 15 + k, column[k - 1]))
+    for k in range(1, 4):
+        owner = (x + 4 - k) % 4
+        remote(
+            pieces.at[owner], pieces.at[owner], sends, recvs, 15 + k, column[k - 1]
+        ).wait_recv()
+    last = launch(remote(pieces, others, sends, recvs, 19, twin))
+    last.wait_recv()
+
+    def place(ups, downs):
+        for part in range(4):
+            up_out[:, :, part * 384 : part * 384 + 384] = ups[part]
+            down_out[part * 3 : part * 3 + 3] = downs[part]
+
+    @pl.when(c == 0)
+    def _():
+        place(pieces, others)
+
+    @pl.when(c == 1)
+    def _():
+        place(others, pieces)
+
+    for copy in started:
+        copy.wait_send()
+
+
+def sum_weights(sum_up, sum_down, rscale):
+    vmem = pl.BlockSpec(memory_space=pltpu.VMEM)
+    f32, bf16 = jnp.float32, jnp.bfloat16
+    up_part, down_part = pl.pallas_call(
+        functools.partial(sum_kernel, rscale),
+        out_shape=(
+            jax.ShapeDtypeStruct((3, 8, 1536), f32),
+            jax.ShapeDtypeStruct((12, 8, 384), f32),
+        ),
+        in_specs=[vmem, vmem],
+        out_specs=(vmem, vmem),
+        scratch_shapes=[
+            pltpu.VMEM((4, 48, 8, 384), bf16),
+            pltpu.VMEM((4, 48, 8, 384), bf16),
+            pltpu.VMEM((3, 48, 8, 384), bf16),
+            pltpu.VMEM((3, 48, 8, 384), bf16),
+            pltpu.VMEM((48, 8, 384), f32),
+            pltpu.VMEM((24, 8, 384), bf16),
+            pltpu.VMEM((24, 8, 384), bf16),
+            pltpu.VMEM((7, 3, 8, 384), bf16),
+            pltpu.VMEM((7, 3, 8, 384), bf16),
+            pltpu.VMEM((3, 8, 384), f32),
+            pltpu.VMEM((3, 8, 384), f32),
+            pltpu.VMEM((4, 3, 8, 384), f32),
+            pltpu.VMEM((4, 3, 8, 384), f32),
+            pltpu.SemaphoreType.DMA((20,)),
+            pltpu.SemaphoreType.DMA((20,)),
+        ],
+        compiler_params=pltpu.CompilerParams(collective_id=2, has_side_effects=True),
+        name="sum_weights",
+    )(sum_up.reshape(48, 8, 1536), sum_down.reshape(192, 8, 384))
+    return up_part.reshape(24, 1536), down_part.reshape(96, 384)
+
+
+def taps_kernel(
+    rscale, taps_ref, out_ref, first, twin_recv, columns, h_send, h_recv, y_send, y_recv,
+    z_send, z_recv, gathered, sends, recvs,
+):
+    lat, lon, x, yh, c, yl, z = places()
+    twin = (lat + 1 - 2 * c, lon)
+    column = [(((x + k) % 4) * 4 + yh * 2 + c, lon) for k in range(1, 4)]
+    across = (lat, (1 - yl) * 8 + z)
+    loop = [(lat, yl * 8 + (z + k) % 8) for k in range(1, 8)]
+    far = (lat + 2 - 4 * yh, lon)
+    greet([twin] + column + [across] + loop + [far])
+    started = []
+
+    def launch(copy):
+        copy.start()
+        started.append(copy)
+        return copy
+
+    launch(remote(taps_ref, twin_recv, sends, recvs, 0, twin)).wait_recv()
+    columns[x] = taps_ref[...] + twin_recv[...]
+    for k in range(1, 4):
+        launch(remote(columns.at[x], columns.at[x], sends, recvs, k, column[k - 1]))
+    for k in (1, 3, 2):
+        owner = (x + 4 - k) % 4
+        remote(columns.at[owner], columns.at[owner], sends, recvs, k, column[k - 1]).wait_recv()
+    h_send[...] = (columns[0] + columns[1]) + (columns[2] + columns[3])
+    launch(remote(h_send, h_recv, sends, recvs, 4, far)).wait_recv()
+    y_send[...] = h_send[...] + h_recv[...]
+    launch(remote(y_send, y_recv, sends, recvs, 5, across)).wait_recv()
+    z_send[...] = y_send[...] + y_recv[...]
+    for k in (4, 3, 5, 2, 6, 1, 7):
+        launch(
+            remote(z_send.at[(z + k) % 8], z_recv.at[k - 1], sends, recvs, 5 + k, loop[k - 1])
+        )
+    block = z_send[z]
+    for k in (1, 7, 2, 6, 3, 5, 4):
+        remote(z_send.at[z], z_recv.at[k - 1], sends, recvs, 5 + k, loop[k - 1]).wait_recv()
+        block = block + z_recv[k - 1]
+    gathered[z] = block * rscale
+    for k in (4, 3, 5, 2, 6, 1, 7):
+        launch(remote(gathered.at[z], gathered.at[z], sends, recvs, 12 + k, loop[k - 1]))
+    for k in (1, 7, 2, 6, 3, 5, 4):
+        owner = (z + 8 - k) % 8
+        remote(gathered.at[owner], gathered.at[owner], sends, recvs, 12 + k, loop[k - 1]).wait_recv()
+    out_ref[...] = gathered[...]
+    for copy in started:
+        copy.wait_send()
+
+
+def sum_taps(taps, rscale):
+    vmem = pl.BlockSpec(memory_space=pltpu.VMEM)
+    f32 = jnp.float32
+    whole = pltpu.VMEM((8, 8, 384), f32)
+    return pl.pallas_call(
+        functools.partial(taps_kernel, rscale),
+        out_shape=jax.ShapeDtypeStruct((8, 8, 384), f32),
+        in_specs=[vmem],
+        out_specs=vmem,
+        scratch_shapes=[
+            whole,
+            whole,
+            pltpu.VMEM((4, 8, 8, 384), f32),
+            whole,
+            whole,
+            whole,
+            whole,
+            whole,
+            pltpu.VMEM((7, 8, 384), f32),
+            whole,
+            pltpu.SemaphoreType.DMA((20,)),
+            pltpu.SemaphoreType.DMA((20,)),
+        ],
+        compiler_params=pltpu.CompilerParams(collective_id=3, has_side_effects=True),
+        name="sum_taps",
+    )(taps)
 
 
 def shards(
@@ -82,10 +414,7 @@
             depth_out = depth_out + framed[
                 row_off : row_off + rows_max, col_off : col_off + tile_cols
             ].astype(jnp.float32) * depth_weight[row_off, col_off].astype(jnp.float32)
-    full_up, full_down = (
-        lax.all_gather(up_weight, "lon", axis=0, tiled=True),
-        lax.all_gather(down_weight, "lon", axis=0, tiled=True),
-    )
+    full_up, full_down = gather_weights(up_weight, down_weight)
     depth_rows = depth_out.reshape(-1, channels)
     center = jnp.mean(depth_rows, axis=-1, keepdims=True)
     offset = depth_rows - center
@@ -149,14 +478,11 @@
         jnp.zeros_like(feature),
     )
     rscale = 1.0 / math.sqrt(BAND_MEAN * lax.axis_size("lat") * tile_cols * lax.axis_size("lon"))
-    tap_terms = jnp.stack(tap_list, axis=0).reshape(kernel, kernel, channels)
-    grad_depth = lax.psum(tap_terms, ("lat", "lon")) * rscale
-    up_part, down_part = (
-        lax.psum_scatter(sum_up, "lon", scatter_dimension=0, tiled=True),
-        lax.psum_scatter(sum_down, "lon", scatter_dimension=0, tiled=True),
-    )
-    up_part, down_part = lax.psum((up_part, down_part), "lat")
-    return (block_out, grad_in, up_part * rscale, down_part * rscale, grad_depth)
+    tap_list.extend([jnp.zeros_like(tap_list[0])] * (64 - kernel * kernel))
+    tap_terms = jnp.stack(tap_list, axis=0).reshape(8, 8, channels)
+    grad_depth = sum_taps(tap_terms, rscale).reshape(64, channels)[: kernel * kernel]
+    up_part, down_part = sum_weights(sum_up, sum_down, rscale)
+    return (block_out, grad_in, up_part, down_part, grad_depth.reshape(kernel, kernel, channels))
 
 
 def solution(mesh):

time: 712 us -> 237 us (0.33)
  waiting for transfers between devices: 568 us -> 9.67 us
  Pallas kernels: 0 us -> 108 us
  starting transfers between devices: 37.2 us -> 22.6 us
  between operations: 18.7 us -> 5.66 us
  local copies, waits for them, and re-layouts: 6.1 us -> 19 us
    psum x2 -> x0, waiting for transfers between devices: 348 us -> none  [the longest x1 214 us: shards(): grad_depth = lax.psum(tap_terms, ('lat', 'lon')) * rscale]
    reduce_scatter x2 -> x0, waiting for transfers between devices: 127 us -> none  [the longest x1 73.6 us: shards(): lax.psum_scatter(sum_up, 'lon', scatter_dimension=0, tiled=True)]
    pallas_call x0 -> x3, Pallas kernels: none -> 108 us  [the longest x1 46 us: sum_weights(): pl.pallas_call(functools.partial(sum_kernel, rscale), out_shape=(jax.Shap...]
    all_gather x2 -> x0, waiting for transfers between devices: 80.8 us -> none  [the longest x1 61 us: shards(): lax.all_gather(down_weight, 'lon', axis=0, tiled=True)]
    ppermute x4, starting transfers between devices: 25.7 us -> 11.2 us  [shifted(): return lax.ppermute(block, axis, route)]
  transfers between devices with their start and end apart: 14 -> 8, of which waited for: 9 -> 2; matrix products, arithmetic and copies ran while one was open for 8% -> 10% of each run, Pallas kernels for 0% -> 46%
where the time goes in v1:
time: 237 us
  Pallas kernels  108 us (46%)
  other arithmetic  46.3 us (20%)
  matrix products  25.6 us (11%)
  starting transfers between devices  22.6 us (10%)
  local copies, waits for them, and re-layouts  19 us (8%)
  waiting for transfers between devices  9.67 us (4%)
  between operations  5.66 us (2%)
    pallas_call x1, Pallas kernels, sum_weights(): pl.pallas_call(functools.partial(sum_kernel, rscale), out_shape=(jax.Shap...  46 us
    pallas_call x1, Pallas kernels, gather_weights(): pl.pallas_call(gather_kernel, out_shape=(jax.ShapeDtypeStruct((48, 8, 153...  35.1 us
    pallas_call x1, Pallas kernels, sum_taps(): pl.pallas_call(functools.partial(taps_kernel, rscale), out_shape=jax.Shap...  26.7 us
    reduce_sum x3, other arithmetic, shards(): jnp.sum(framed[row_off:row_off + rows_max, col_off:col_off + tile_cols].a...  13.2 us
    select_n x1, other arithmetic, shards(): jnp.where(inside[:, None, None], grad_local, jnp.zeros_like(grad_local))  12.8 us
    reduce_sum x1, other arithmetic, shards(): center = jnp.mean(depth_rows, axis=-1, keepdims=True)  11.8 us
    ppermute x4, starting transfers between devices, shifted(): return lax.ppermute(block, axis, route)  11.2 us
    ppermute x4, waiting for transfers between devices, shifted(): return lax.ppermute(block, axis, route)  9.66 us
  transfers between devices with their start and end apart: 8, of which 2 were waited for; matrix products, arithmetic and copies ran while one was open for 10% of the time, Pallas kernels for 46%

profile of v1, /device:TPU:1, one launch (start us, length us, event | category | flops | bytes accessed | tf_op | source)
XLA Modules:
  0.0 236.7 jit_solution(15798812659894592796)
XLA Ops:
  0.7 1.3 dynamic_slice.10
  3.4 1.3 broadcast_multiply_fusion
  4.9 2.5 %collective-permute-start = (bf16[32,3,384]{2,1,0:T(4,128)(2,1)S(1)}, bf16[32,3,384]{2,1,0:T(4,128)(2,1)S(1)}, u32[]{:S(2)}, u32[]{:S(2)}) collective-permute-start(bf16[32,3,384]{2,1,0:T(4,128)(2,1)S(1)} %get-tuple-element.125), channel_id=1, source_target_pairs={{0,1},{1,2},{2,3},{3,4},{4,5},{5,6},{6,7},{7,8},{8,9},{9,10},{10,1... | collective-permute-start | bytes 221192 | tf_op jit(solution)/shard_map/ppermute | solution.py:26
  7.4 5.0 %collective-permute-start.1 = (bf16[32,3,384]{2,1,0:T(4,128)(2,1)S(1)}, bf16[32,3,384]{2,1,0:T(4,128)(2,1)S(1)}, u32[]{:S(2)}, u32[]{:S(2)}) collective-permute-start(bf16[32,3,384]{2,1,0:T(4,128)(2,1)S(1)} %get-tuple-element.126), channel_id=1, source_target_pairs={{1,0},{2,1},{3,2},{4,3},{5,4},{6,5},{7,6},{8,7},{9,8},{10,9},{11,1... | collective-permute-start | bytes 221192 | tf_op jit(solution)/shard_map/ppermute | solution.py:27
  15.8 1.1 multiply_convert_fusion.3
  17.0 35.1 %gather_weights.1 = (bf16[48,8,1536]{2,1,0:T(8,128)(2,1)}, bf16[192,8,384]{2,1,0:T(8,128)(2,1)}) custom-call(bf16[3,8,1536]{2,1,0:T(8,128)(2,1)} %bitcast.121, bf16[12,8,384]{2,1,0:T(8,128)(2,1)} %bitcast.122), custom_call_target="tpu_custom_call" | custom-call | tf_op jit(solution)/shard_map/gather_weights/pallas_call | solution.py:142
  53.1 4.5 %collective-permute-start.2 = (bf16[3,38,384]{2,1,0:T(8,128)(2,1)S(1)}, bf16[3,38,384]{2,1,0:T(8,128)(2,1)S(1)}, u32[]{:S(2)}, u32[]{:S(2)}) collective-permute-start(bf16[3,38,384]{2,1,0:T(8,128)(2,1)S(1)} %get-tuple-element.122), channel_id=1, source_target_pairs={{0,16},{16,32},{32,48},{48,64},{64,80},{80,96},{96,112},{112,128},... | collective-permute-start | bytes 262664 | tf_op jit(solution)/shard_map/ppermute | solution.py:35
  57.8 1.9 collective-permute-start.3
  60.2 5.0 %collective-permute-done.3 = bf16[3,38,384]{2,1,0:T(8,128)(2,1)S(1)} collective-permute-done((bf16[3,38,384]{2,1,0:T(8,128)(2,1)S(1)}, bf16[3,38,384]{2,1,0:T(8,128)(2,1)S(1)}, u32[]{:S(2)}, u32[]{:S(2)}) %collective-permute-start.3) | collective-permute-done | bytes 87584 | tf_op jit(solution)/shard_map/ppermute | solution.py:35
  65.5 11.8 %fusion.128 = (f32[32,32]{1,0:T(8,128)S(1)}, f32[32,32,384]{2,1,0:T(8,128)S(1)}) fusion(f32[384]{0:T(512)S(1)} %get-tuple-element.111, bf16[38,38,384]{2,1,0:T(8,128)(2,1)S(1)} %constant_dynamic-update-slice_fusion.1, f32[384]{0:T(512)S(1)} %get-tuple-element.112, f32[384]{0:T(512)S(1)} %get-tuple-element.65, f32[384]{0:T(512)S(1)} %get-tuple-element.66, ...), kind=kLoop, calls=%fused_computation.307 | loop fusion | flops 57801728 | bytes 40187392 | tf_op jit(solution)/shard_map/reduce_sum | solution.py:419
  79.4 4.1 %fusion.11 = (bf16[1536,1024]{0,1:T(8,128)(2,1)}, f32[1024,1536]{1,0:T(8,128)S(1)}) fusion(f32[1536]{0:T(1024)S(1)} %copy-done.124, bf16[1024,384]{1,0:T(8,128)(2,1)S(1)} %bitcast.116, bf16[48,8,1536]{2,1,0:T(8,128)(2,1)S(1)} %copy-done.123), kind=kOutput, calls=%fused_computation.63 | convolution fusion | flops 1223688192 | bytes 11409408 | tf_op jit(solution)/shard_map/dot_general | solution.py:424
  83.5 2.7 %copy-done.128 = f32[1024,1536]{1,0:T(8,128)} copy-done((f32[1024,1536]{1,0:T(8,128)}, f32[1024,1536]{1,0:T(8,128)S(1)}, u32[]{:S(2)}) %copy-start.128) | copy-done | bytes 6291480
  86.2 5.4 %fusion.6 = bf16[1024,1536]{1,0:T(8,128)(2,1)S(1)} fusion(f32[1024,1536]{1,0:T(8,128)S(1)} %get-tuple-element.129, bf16[1024,384]{1,0:T(8,128)(2,1)S(1)} %bitcast.112, f32[1536]{0:T(1024)S(1)} %copy-done.124, bf16[192,8,384]{2,1,0:T(8,128)(2,1)S(1)} %copy-done.121), kind=kOutput, calls=%fused_computation.58 | convolution fusion | flops 1239416832 | bytes 11409408 | tf_op jit(solution)/shard_map/dot_general | solution.py:437
  91.6 2.5 %fusion.126 = (f32[1024]{0:T(1024)S(1)}, f32[1024]{0:T(1024)S(1)}, bf16[1024,384]{1,0:T(8,128)(2,1)}, f32[1024,384]{1,0:T(8,128)S(1)}) fusion(f32[1024]{0:T(1024)S(1)} %rsqrt.13, f32[1024]{0:T(1024)S(1)} %div.17, f32[32,32,384]{2,1,0:T(8,128)S(1)} %get-tuple-element.117, f32[384]{0:T(512)S(1)} %copy-done.115, f32[384]{0:T(512)S(1)} %copy-done.116, ...), kind=kOutput, calls=%fused_computation.305 | convolution fusion | flops 1211496448 | bytes 8276992 | tf_op jit(solution)/shard_map/dot_general | solution.py:444
  94.1 6.5 %fusion.113 = (f32[384]{0:T(512)}, f32[384]{0:T(512)}, f32[384]{0:T(512)}, f32[384]{0:T(512)}, f32[384]{0:T(512)}, /*index=5*/f32[384]{0:T(512)}, f32[384]{0:T(5...) fusion(bf16[38,38,384]{2,1,0:T(8,128)(2,1)S(1)} %constant_dynam, ...), kind=kLoop, calls=%fused_computation.216 | loop fusion | flops 24372480 | bytes 18131968 | tf_op jit(solution)/shard_map/reduce_sum | solution.py:463
  100.7 2.8 %fusion.77 = (f32[384]{0:T(512)S(1)}, f32[384]{0:T(512)S(1)}, f32[384]{0:T(512)S(1)}, f32[384]{0:T(512)S(1)}, f32[384]{0:T(512)S(1)}, /*index=5*/f32[384]{0:T(51...) fusion(bf16[38,38,384]{2,1,0:T(8,128)(2,1)S(1)} %constant_dynam, ...), kind=kLoop, calls=%fused_computation.180 | loop fusion | flops 15723648 | bytes 11030016 | tf_op jit(solution)/shard_map/reduce_sum | solution.py:463
  103.5 3.9 %fusion.95 = (f32[384]{0:T(512)S(1)}, f32[384]{0:T(512)S(1)}, f32[384]{0:T(512)S(1)}, f32[384]{0:T(512)S(1)}, f32[384]{0:T(512)S(1)}, /*index=5*/f32[384]{0:T(51...) fusion(bf16[38,38,384]{2,1,0:T(8,128)(2,1)S(1)} %constant_dynam, ...), kind=kLoop, calls=%fused_computation.198 | loop fusion | flops 21619968 | bytes 14969856 | tf_op jit(solution)/shard_map/reduce_sum | solution.py:463
  107.4 4.8 %copy.20 = bf16[1536,1024]{1,0:T(8,128)(2,1)} copy(bf16[1536,1024]{0,1:T(8,128)(2,1)} %get-tuple-element.128) | data formatting | bytes 6291456 | tf_op jit(solution)/shard_map/convert_element_type | solution.py:425
  112.3 0.8 collective-permute-start.4
  113.1 3.0 %collective-permute-start.5 = (bf16[32,3,384]{2,1,0:T(4,128)(2,1)S(1)}, bf16[32,3,384]{2,1,0:T(4,128)(2,1)S(1)}, u32[]{:S(2)}, u32[]{:S(2)}) collective-permute-start(bf16[32,3,384]{2,1,0:T(4,128)(2,1)S(1)} %get-tuple-element.124), channel_id=1, source_target_pairs={{1,0},{2,1},{3,2},{4,3},{5,4},{6,5},{7,6},{8,7},{9,8},{10,9},{11,1... | collective-permute-start | bytes 221192 | tf_op jit(solution)/shard_map/ppermute | solution.py:27
  116.5 4.8 %fusion.14.up_ref = f32[48,8,1536]{2,1,0:T(8,128)} fusion(bf16[1024,1536]{1,0:T(8,128)(2,1)} %copy-done.127, bf16[384,1024]{1,0:T(8,128)(2,1)S(1)} %copy.19), kind=kOutput, calls=%fused_computation.68 | convolution fusion | flops 1207959552 | bytes 6291456 | tf_op jit(solution)/shard_map/dot_general | solution.py:441
  121.4 5.5 %fusion.114 = bf16[1024,384]{1,0:T(8,128)(2,1)S(1)} fusion(bf16[1024,384]{1,0:T(8,128)(2,1)S(1)} %bitcast.111, f32[1024,1536]{1,0:T(8,128)} %copy-done.128, f32[1536]{0:T(1024)S(1)} %copy-done.125, bf16[192,8,384]{2,1,0:T(8,128)(2,1)S(1)} %copy-done.122, f32[384]{0:T(512)S(1)} %copy-done.126, f32[384]{0:T(512)S(1)} %copy-done.118), kind=kOutput, calls=%fused_computation.218 | convolution fusion | flops 1225654272 | bytes 9053184 | tf_op jit(solution)/shard_map/dot_general | solution.py:426
  126.9 3.2 %fusion.12.down_ref = f32[192,8,384]{2,1,0:T(8,128)} fusion(bf16[1024,384,1]{1,0,2:T(8,128)(2,1)S(1)} %bitcast.113, bf16[1536,1024]{1,0:T(8,128)(2,1)S(1)} %copy-done), kind=kOutput, calls=%fused_computation.66 | convolution fusion | flops 1207959552 | bytes 6291456 | tf_op jit(solution)/shard_map/dot_general | solution.py:434
  130.9 2.4 %collective-permute-start.6 = (bf16[3,38,384]{2,1,0:T(8,128)(2,1)S(1)}, bf16[3,38,384]{2,1,0:T(8,128)(2,1)S(1)}, u32[]{:S(2)}, u32[]{:S(2)}) collective-permute-start(bf16[3,38,384]{2,1,0:T(8,128)(2,1)S(1)} %get-tuple-element.120), channel_id=1, source_target_pairs={{0,16},{16,32},{32,48},{48,64},{64,80},{80,96},{96,112},{112,128},... | collective-permute-start | bytes 262664 | tf_op jit(solution)/shard_map/ppermute | solution.py:35
  133.3 1.0 broadcast_select_fusion.1
  135.1 5.0 %stack.211 = f32[64,384]{1,0:T(8,128)} concatenate(f32[1,384]{1,0:T(1,128)S(1)} %stack.159, f32[1,384]{1,0:T(1,128)S(1)} %stack.160, f32[1,384]{1,0:T(1,128)S(1)} %stack.161, f32[1,384]{1,0:T(1,128)S(1)} %stack.162, f32[1,384]{1,0:T(1,128)S(1)} %stack.163, f32[1,384]{1,0:T(1,128)S(1)} %stack.164, f32[1,384]{1,0:T(1,128)S(1)} %stack.165, f32[1,384]{1,0:T(1,128)S(1)} %stack.166, ...), dimensions={0} | concatenate | bytes 196608 | tf_op jit(solution)/shard_map/stack | solution.py:482
  140.0 26.7 %sum_taps.1 = f32[8,8,384]{2,1,0:T(8,128)} custom-call(f32[8,8,384]{2,1,0:T(8,128)} %bitcast.117), custom_call_target="tpu_custom_call" | custom-call | tf_op jit(solution)/shard_map/sum_taps/pallas_call | solution.py:366
  166.7 0.9 slice.818
  168.3 46.0 %sum_weights.1 = (f32[3,8,1536]{2,1,0:T(8,128)}, f32[12,8,384]{2,1,0:T(8,128)}) custom-call(f32[48,8,1536]{2,1,0:T(8,128)} %fusion.14.up_ref, f32[192,8,384]{2,1,0:T(8,128)} %fusion.12.down_ref), custom_call_target="tpu_custom_call" | custom-call | tf_op jit(solution)/shard_map/sum_weights/pallas_call | solution.py:282
  214.7 2.4 %collective-permute-start.7 = (bf16[3,38,384]{2,1,0:T(8,128)(2,1)S(1)}, bf16[3,38,384]{2,1,0:T(8,128)(2,1)S(1)}, u32[]{:S(2)}, u32[]{:S(2)}) collective-permute-start(bf16[3,38,384]{2,1,0:T(8,128)(2,1)S(1)} %get-tuple-element.119), channel_id=1, source_target_pairs={{16,0},{32,16},{48,32},{64,48},{80,64},{96,80},{112,96},{128,112},... | collective-permute-start | bytes 262664 | tf_op jit(solution)/shard_map/ppermute | solution.py:35
  217.5 4.7 %collective-permute-done.7 = bf16[3,38,384]{2,1,0:T(8,128)(2,1)S(1)} collective-permute-done((bf16[3,38,384]{2,1,0:T(8,128)(2,1)S(1)}, bf16[3,38,384]{2,1,0:T(8,128)(2,1)S(1)}, u32[]{:S(2)}, u32[]{:S(2)}) %collective-permute-start.7) | collective-permute-done | bytes 87584 | tf_op jit(solution)/shard_map/ppermute | solution.py:35
  222.6 12.8 %broadcast_select_fusion = bf16[32,32,384]{2,1,0:T(8,128)(2,1)} fusion(pred[32]{0:T(512)(128)(4,1)S(1)} %copy-done.96, f32[384]{0:T(512)} %copy-done.91, bf16[38,38,384]{2,1,0:T(8,128)(2,1)S(1)} %constant_dynamic-update-slice_fusion, f32[384]{0:T(512)} %copy-done.92, f32[384]{0:T(512)S(1)} %copy-done.45, f32[384]{0:T(512)S(1)} %copy-done.47, ...), kind=kLoop, calls=%fused_computation.239 | loop fusion | flops 59375616 | bytes 40187424 | tf_op jit(solution)/shard_map/jit(_where)/select_n | solution.py:474
  (344 shorter events, 9.5 us)
Async XLA Ops:
  0.6 14.4 %copy-start.9 = (bf16[7,7,384]{2,1,0:T(8,128)(2,1)S(1)}, bf16[7,7,384]{2,1,0:T(8,128)(2,1)}, u32[]{:S(2)}) copy-start(bf16[7,7,384]{2,1,0:T(8,128)(2,1)} %param.15) | copy-start | bytes 112900
  0.6 15.2 %copy-start.1 = (bf16[32,32,384]{2,1,0:T(8,128)(2,1)S(1)}, bf16[32,32,384]{2,1,0:T(8,128)(2,1)}, u32[]{:S(2)}) copy-start(bf16[32,32,384]{2,1,0:T(8,128)(2,1)} %param.23) | copy-start | bytes 2359300
  0.7 15.2 %copy-start.117 = (f32[384]{0:T(512)S(1)}, f32[384]{0:T(512)}, u32[]{:S(2)}) copy-start(f32[384]{0:T(512)} %param.22) | copy-start | bytes 4612
  2.6 14.4 %copy-start.95 = (pred[32]{0:T(512)(128)(4,1)}, pred[32]{0:T(512)(128)(4,1)S(1)}, u32[]{:S(2)}) copy-start(pred[32]{0:T(512)(128)(4,1)S(1)} %iota_compare_fusion) | copy-start | bytes 100
  4.9 47.5 %collective-permute-start = (bf16[32,3,384]{2,1,0:T(4,128)(2,1)S(1)}, bf16[32,3,384]{2,1,0:T(4,128)(2,1)S(1)}, u32[]{:S(2)}, u32[]{:S(2)}) collective-permute-start(bf16[32,3,384]{2,1,0:T(4,128)(2,1)S(1)} %get-tuple-element.125), channel_id=1, source_target_pairs={{0,1},{1,2},{2,3},{3,4},{4,5},{5,6},{6,7},{7,8},{8,9},{9,10},{10,1... | collective-permute-start | bytes 221192 | tf_op jit(solution)/shard_map/ppermute | solution.py:26
  7.4 45.0 %collective-permute-start.1 = (bf16[32,3,384]{2,1,0:T(4,128)(2,1)S(1)}, bf16[32,3,384]{2,1,0:T(4,128)(2,1)S(1)}, u32[]{:S(2)}, u32[]{:S(2)}) collective-permute-start(bf16[32,3,384]{2,1,0:T(4,128)(2,1)S(1)} %get-tuple-element.126), channel_id=1, source_target_pairs={{1,0},{2,1},{3,2},{4,3},{5,4},{6,5},{7,6},{8,7},{9,8},{10,9},{11,1... | collective-permute-start | bytes 221192 | tf_op jit(solution)/shard_map/ppermute | solution.py:27
  15.8 43.9 %copy-start.119 = (bf16[38]{0:T(256)(128)(2,1)}, bf16[38]{0:T(256)(128)(2,1)S(1)}, u32[]{:S(2)}) copy-start(bf16[38]{0:T(256)(128)(2,1)S(1)} %pad.12.clone) | copy-start | bytes 232
  52.2 13.0 %copy-start.44 = (f32[384]{0:T(512)}, f32[384]{0:T(512)S(1)}, u32[]{:S(2)}) copy-start(f32[384]{0:T(512)S(1)} %get-tuple-element.65) | copy-start | bytes 4612
  52.2 13.0 %copy-start.46 = (f32[384]{0:T(512)}, f32[384]{0:T(512)S(1)}, u32[]{:S(2)}) copy-start(f32[384]{0:T(512)S(1)} %get-tuple-element.66) | copy-start | bytes 4612
  52.2 13.0 %copy-start.48 = (f32[384]{0:T(512)}, f32[384]{0:T(512)S(1)}, u32[]{:S(2)}) copy-start(f32[384]{0:T(512)S(1)} %get-tuple-element.67) | copy-start | bytes 4612
  52.2 13.0 %copy-start.50 = (f32[384]{0:T(512)}, f32[384]{0:T(512)S(1)}, u32[]{:S(2)}) copy-start(f32[384]{0:T(512)S(1)} %get-tuple-element.68) | copy-start | bytes 4612
  53.1 6.6 %collective-permute-start.2 = (bf16[3,38,384]{2,1,0:T(8,128)(2,1)S(1)}, bf16[3,38,384]{2,1,0:T(8,128)(2,1)S(1)}, u32[]{:S(2)}, u32[]{:S(2)}) collective-permute-start(bf16[3,38,384]{2,1,0:T(8,128)(2,1)S(1)} %get-tuple-element.122), channel_id=1, source_target_pairs={{0,16},{16,32},{32,48},{48,64},{64,80},{80,96},{96,112},{112,128},... | collective-permute-start | bytes 262664 | tf_op jit(solution)/shard_map/ppermute | solution.py:35
  57.7 19.6 %copy-start.80 = (f32[384]{0:T(512)}, f32[384]{0:T(512)S(1)}, u32[]{:S(2)}) copy-start(f32[384]{0:T(512)S(1)} %get-tuple-element.102) | copy-start | bytes 4612
  57.7 19.6 %copy-start.82 = (f32[384]{0:T(512)}, f32[384]{0:T(512)S(1)}, u32[]{:S(2)}) copy-start(f32[384]{0:T(512)S(1)} %get-tuple-element.103) | copy-start | bytes 4612
  57.7 19.6 %copy-start.84 = (f32[384]{0:T(512)}, f32[384]{0:T(512)S(1)}, u32[]{:S(2)}) copy-start(f32[384]{0:T(512)S(1)} %get-tuple-element.104) | copy-start | bytes 4612
  57.7 19.6 %copy-start.85 = (f32[384]{0:T(512)}, f32[384]{0:T(512)S(1)}, u32[]{:S(2)}) copy-start(f32[384]{0:T(512)S(1)} %get-tuple-element.105) | copy-start | bytes 4612
  57.7 19.6 %copy-start.86 = (f32[384]{0:T(512)}, f32[384]{0:T(512)S(1)}, u32[]{:S(2)}) copy-start(f32[384]{0:T(512)S(1)} %get-tuple-element.106) | copy-start | bytes 4612
  57.7 19.6 %copy-start.87 = (f32[384]{0:T(512)}, f32[384]{0:T(512)S(1)}, u32[]{:S(2)}) copy-start(f32[384]{0:T(512)S(1)} %get-tuple-element.107) | copy-start | bytes 4612
  57.7 19.6 %copy-start.88 = (f32[384]{0:T(512)}, f32[384]{0:T(512)S(1)}, u32[]{:S(2)}) copy-start(f32[384]{0:T(512)S(1)} %get-tuple-element.108) | copy-start | bytes 4612
  57.8 19.6 %copy-start.89 = (f32[384]{0:T(512)}, f32[384]{0:T(512)S(1)}, u32[]{:S(2)}) copy-start(f32[384]{0:T(512)S(1)} %get-tuple-element.109) | copy-start | bytes 4612
  57.8 19.6 %copy-start.90 = (f32[384]{0:T(512)}, f32[384]{0:T(512)S(1)}, u32[]{:S(2)}) copy-start(f32[384]{0:T(512)S(1)} %get-tuple-element.110) | copy-start | bytes 4612
  57.8 19.6 %copy-start.91 = (f32[384]{0:T(512)}, f32[384]{0:T(512)S(1)}, u32[]{:S(2)}) copy-start(f32[384]{0:T(512)S(1)} %get-tuple-element.111) | copy-start | bytes 4612
  57.8 19.6 %copy-start.92 = (f32[384]{0:T(512)}, f32[384]{0:T(512)S(1)}, u32[]{:S(2)}) copy-start(f32[384]{0:T(512)S(1)} %get-tuple-element.112) | copy-start | bytes 4612
  57.8 7.4 %collective-permute-start.3 = (bf16[3,38,384]{2,1,0:T(8,128)(2,1)S(1)}, bf16[3,38,384]{2,1,0:T(8,128)(2,1)S(1)}, u32[]{:S(2)}, u32[]{:S(2)}) collective-permute-start(bf16[3,38,384]{2,1,0:T(8,128)(2,1)S(1)} %get-tuple-element.121), channel_id=1, source_target_pairs={{16,0},{32,16},{48,32},{64,48},{80,64},{96,80},{112,96},{128,112},... | collective-permute-start | bytes 262664 | tf_op jit(solution)/shard_map/ppermute | solution.py:35
  77.5 14.1 %copy-start.93 = (f32[1024]{0:T(1024)}, f32[1024]{0:T(1024)S(1)}, u32[]{:S(2)}) copy-start(f32[1024]{0:T(1024)S(1)} %div.17) | copy-start | bytes 12292
  78.1 13.5 %copy-start.94 = (f32[1024]{0:T(1024)}, f32[1024]{0:T(1024)S(1)}, u32[]{:S(2)}) copy-start(f32[1024]{0:T(1024)S(1)} %rsqrt.13) | copy-start | bytes 12292
  112.3 18.0 %collective-permute-start.4 = (bf16[32,3,384]{2,1,0:T(4,128)(2,1)S(1)}, bf16[32,3,384]{2,1,0:T(4,128)(2,1)S(1)}, u32[]{:S(2)}, u32[]{:S(2)}) collective-permute-start(bf16[32,3,384]{2,1,0:T(4,128)(2,1)S(1)} %get-tuple-element.123), channel_id=1, source_target_pairs={{0,1},{1,2},{2,3},{3,4},{4,5},{5,6},{6,7},{7,8},{8,9},{9,10},{10,1... | collective-permute-start | bytes 221192 | tf_op jit(solution)/shard_map/ppermute | solution.py:26
  113.1 17.2 %collective-permute-start.5 = (bf16[32,3,384]{2,1,0:T(4,128)(2,1)S(1)}, bf16[32,3,384]{2,1,0:T(4,128)(2,1)S(1)}, u32[]{:S(2)}, u32[]{:S(2)}) collective-permute-start(bf16[32,3,384]{2,1,0:T(4,128)(2,1)S(1)} %get-tuple-element.124), channel_id=1, source_target_pairs={{1,0},{2,1},{3,2},{4,3},{5,4},{6,5},{7,6},{8,7},{9,8},{10,9},{11,1... | collective-permute-start | bytes 221192 | tf_op jit(solution)/shard_map/ppermute | solution.py:27
  130.9 86.2 %collective-permute-start.6 = (bf16[3,38,384]{2,1,0:T(8,128)(2,1)S(1)}, bf16[3,38,384]{2,1,0:T(8,128)(2,1)S(1)}, u32[]{:S(2)}, u32[]{:S(2)}) collective-permute-start(bf16[3,38,384]{2,1,0:T(8,128)(2,1)S(1)} %get-tuple-element.120), channel_id=1, source_target_pairs={{0,16},{16,32},{32,48},{48,64},{64,80},{80,96},{96,112},{112,128},... | collective-permute-start | bytes 262664 | tf_op jit(solution)/shard_map/ppermute | solution.py:35
  168.3 48.8 %copy-start.120 = (bf16[38]{0:T(256)(128)(2,1)S(1)}, bf16[38]{0:T(256)(128)(2,1)}, u32[]{:S(2)}) copy-start(bf16[38]{0:T(256)(128)(2,1)} %copy-done.119) | copy-start | bytes 232
  214.7 7.5 %collective-permute-start.7 = (bf16[3,38,384]{2,1,0:T(8,128)(2,1)S(1)}, bf16[3,38,384]{2,1,0:T(8,128)(2,1)S(1)}, u32[]{:S(2)}, u32[]{:S(2)}) collective-permute-start(bf16[3,38,384]{2,1,0:T(8,128)(2,1)S(1)} %get-tuple-element.119), channel_id=1, source_target_pairs={{16,0},{32,16},{48,32},{64,48},{80,64},{96,80},{112,96},{128,112},... | collective-permute-start | bytes 262664 | tf_op jit(solution)/shard_map/ppermute | solution.py:35
  222.6 13.5 %copy-start.7 = (f32[12,8,384]{2,1,0:T(8,128)S(1)}, f32[12,8,384]{2,1,0:T(8,128)}, u32[]{:S(2)}) copy-start(f32[12,8,384]{2,1,0:T(8,128)} %get-tuple-element.12) | copy-start | bytes 442372
  (105 other events, 854.1 us)

commit v2 on v1

v2 whole, which is shorter than its diff:
```python
import functools
import math

import jax
import jax.numpy as jnp
from jax import lax
from jax.experimental import pallas as pl
from jax.experimental.pallas import tpu as pltpu
from jax.sharding import PartitionSpec as P

BAND_MEAN = 16


SQRT_TWO_PI = 0.7978845608028654
CUBIC = 0.044715
EPSILON = 1e-06


def smooth_gate(pre_act):
    argument = SQRT_TWO_PI * (pre_act + CUBIC * pre_act * pre_act * pre_act)
    return 0.5 * pre_act * (1.0 + jnp.tanh(argument))


def smooth_slope(pre_act):
    argument = SQRT_TWO_PI * (pre_act + CUBIC * pre_act * pre_act * pre_act)
    tangent = jnp.tanh(argument)
    return 0.5 * (1.0 + tangent) + 0.5 * pre_act * (1.0 - tangent * tangent) * SQRT_TWO_PI * (
        1.0 + 3.0 * CUBIC * pre_act * pre_act
    )


def places():
    lat, lon = lax.axis_index("lat"), lax.axis_index("lon")
    return lat, lon, lat // 4, (lat // 2) % 2, lat % 2, lon // 8, lon % 8


def remote(src, dst, sends, recvs, slot, device):
    return pltpu.make_async_remote_copy(
        src_ref=src,
        dst_ref=dst,
        send_sem=sends.at[slot],
        recv_sem=recvs.at[slot],
        device_id=device,
        device_id_type=pl.DeviceIdType.MESH,
    )


def greet(peers):
    barrier = pltpu.get_barrier_semaphore()
    for peer in peers:
        pl.semaphore_signal(barrier, inc=1, device_id=peer, device_id_type=pl.DeviceIdType.MESH)
    pl.semaphore_wait(barrier, len(peers))


def halo_peers(lat, lon):
    north, south = (lat + 15) % 16, (lat + 1) % 16
    west, east = (lon + 15) % 16, (lon + 1) % 16
    return [
        (lat, east), (lat, west), (south, lon), (north, lon),
        (south, east), (south, west), (north, east), (north, west),
    ]


def halo_copies(edges, arrivals, sends, recvs, base, peers):
    return [
        remote(edges[i], arrivals[i], sends, recvs, base + i, peers[i]) for i in range(8)
    ]


def halo_edges(field, live_rows):
    final = lax.dynamic_slice_in_dim(field, live_rows - 3, 3, 0)
    first = field[:3]
    return [
        field[:, -3:], field[:, :3], final, first,
        final[:, -3:], final[:, :3], first[:, -3:], first[:, :3],
    ]


def halo_shapes(rows, cols, channels):
    tall = jax.ShapeDtypeStruct((rows, 3, channels), jnp.bfloat16)
    wide = jax.ShapeDtypeStruct((3, cols, channels), jnp.bfloat16)
    corner = jax.ShapeDtypeStruct((3, 3, channels), jnp.bfloat16)
    return [tall, tall, wide, wide, corner, corner, corner, corner]


def framed_by(field, arrivals, live_rows):
    west, east, north, south, nw, ne, sw, se = arrivals
    lat = lax.axis_index("lat")
    above = jnp.concatenate([nw, north, ne], axis=1)
    below = jnp.concatenate([sw, south, se], axis=1)
    above = jnp.where(lat > 0, above, jnp.zeros_like(above))
    below = jnp.where(lat < lax.axis_size("lat") - 1, below, jnp.zeros_like(below))
    widened = jnp.concatenate([west, field, east], axis=1)
    stacked = jnp.concatenate([above, widened, jnp.zeros_like(above)], axis=0)
    return lax.dynamic_update_slice_in_dim(stacked, below, live_rows + 3, 0)


def gather_kernel(*refs):
    up_ref, down_ref = refs[:2]
    edges = refs[2:10]
    full_up, full_down = refs[10:12]
    arrivals = refs[12:20]
    sends, recvs = refs[20:]
    lat, lon, x, yh, c, yl, z = places()
    after = (lat, yl * 8 + (z + 1) % 8)
    ahead = (lat, yl * 8 + (z + 7) % 8)
    across = (lat, (1 - yl) * 8 + z)
    twin = (lat + 1 - 2 * c, lon)
    around = halo_peers(lat, lon)
    greet([after, ahead, across, twin] + around)
    started = []

    def parts(up, down, block, half):
        lanes = pl.ds(pl.multiple_of(half * 768, 768), 768)
        return (
            up.at[pl.ds(block * 3, 3), :, lanes],
            down.at[pl.ds(block * 12 + half * 6, 6)],
        )

    def copies(block, half, slot, device, own=False, which=(0, 1)):
        sources = parts(up_ref, down_ref, 0, half) if own else parts(full_up, full_down, block, half)
        targets = parts(full_up, full_down, block, half)
        return [
            remote(sources[i], targets[i], sends, recvs, slot * 2 + i, device) for i in which
        ]

    def mine(k):
        return yl * 8 + (z + 8 + k) % 8

    def theirs(k):
        return (1 - yl) * 8 + (z + 8 + k) % 8

    def send(block, slot, device, own=False, which=(0, 1)):
        for copy in copies(block, c, slot, device, own, which):
            copy.start()
            started.append(copy)

    def wait(block, slot, device, half=c, which=(0, 1)):
        for copy in copies(block, half, slot, device, False, which):
            copy.wait_recv()

    send(lon, 0, after, own=True)
    send(lon, 4, ahead, own=True)
    send(lon, 8, across, own=True)
    halos = halo_copies(edges, arrivals, sends, recvs, 64, around)
    for copy in halos:
        copy.start()
        started.append(copy)
    full_up[pl.ds(lon * 3, 3)] = up_ref[...]
    full_down[pl.ds(lon * 12, 12)] = down_ref[...]
    for k in (1, 2, 3):
        wait(mine(-k), k - 1, after)
        wait(mine(k), 3 + k, ahead)
        if k < 3:
            send(mine(-k), k, after)
            send(mine(k), 4 + k, ahead)
        else:
            send(mine(-3), 3, after, which=(0,))
            send(mine(3), 7, ahead, which=(1,))
        if k > 1:
            send(mine(-k), 7 + k, across)
            send(mine(k), 9 + k, across)
        send(mine(-k), 15 + k, twin)
        send(mine(k), 18 + k, twin)
        if k == 1:
            wait(theirs(0), 8, across)
            send(theirs(0), 14, after)
            send(theirs(0), 15, ahead)
            send(theirs(0), 23, twin)
    wait(theirs(-1), 14, after)
    wait(theirs(1), 15, ahead)
    send(theirs(-1), 24, twin)
    send(theirs(1), 25, twin)
    wait(mine(4), 3, after, which=(0,))
    wait(mine(4), 7, ahead, which=(1,))
    send(mine(4), 13, across)
    send(mine(4), 22, twin)
    for k in (2, 3):
        wait(theirs(-k), 7 + k, across)
        wait(theirs(k), 9 + k, across)
        send(theirs(-k), 24 + k, twin)
        send(theirs(k), 26 + k, twin)
    wait(theirs(4), 13, across)
    send(theirs(4), 30, twin)
    for k in (1, 2, 3):
        wait(mine(-k), 15 + k, twin, 1 - c)
        wait(mine(k), 18 + k, twin, 1 - c)
    wait(theirs(0), 23, twin, 1 - c)
    wait(theirs(-1), 24, twin, 1 - c)
    wait(theirs(1), 25, twin, 1 - c)
    wait(mine(4), 22, twin, 1 - c)
    for k in (2, 3):
        wait(theirs(-k), 24 + k, twin, 1 - c)
        wait(theirs(k), 26 + k, twin, 1 - c)
    wait(theirs(4), 30, twin, 1 - c)
    for copy in halos:
        copy.wait_recv()
    for copy in started:
        copy.wait_send()


def gather_weights(up_weight, down_weight, edges):
    vmem = pl.BlockSpec(memory_space=pltpu.VMEM)
    rows, cols, channels = edges[0].shape[0], edges[2].shape[1], edges[0].shape[2]
    full_up, full_down, *arrivals = pl.pallas_call(
        gather_kernel,
        out_shape=(
            jax.ShapeDtypeStruct((48, 8, 1536), jnp.bfloat16),
            jax.ShapeDtypeStruct((192, 8, 384), jnp.bfloat16),
            *halo_shapes(rows, cols, channels),
        ),
        in_specs=[vmem] * 10,
        out_specs=(vmem,) * 10,
        scratch_shapes=[pltpu.SemaphoreType.DMA((72,)), pltpu.SemaphoreType.DMA((72,))],
        compiler_params=pltpu.CompilerParams(collective_id=1, has_side_effects=True),
        name="gather_weights",
    )(up_weight.reshape(3, 8, 1536), down_weight.reshape(12, 8, 384), *edges)
    return full_up.reshape(384, 1536), full_down.reshape(1536, 384), arrivals


def sum_kernel(rscale, *refs):
    up_ref, down_ref, taps_ref = refs[:3]
    edges = refs[3:11]
    up_out, down_out, taps_out = refs[11:14]
    arrivals = refs[14:22]
    (
        twin_send, twin_recv, x_send, x_recv, d_send, d_recv, total, y_send, y_recv, z_send, z_recv,
        h_send, h_recv, pieces, others, tap_twin, tap_sum, tap_x, tap_ys, tap_yr, tap_z,
        tap_hs, tap_hr, sends, recvs,
    ) = refs[22:]
    lat, lon, x, yh, c, yl, z = places()
    f32, bf16 = jnp.float32, jnp.bfloat16
    twin = (lat + 1 - 2 * c, lon)
    column = [(((x + k) % 4) * 4 + yh * 2 + c, lon) for k in range(1, 4)]
    across = (lat, (1 - yl) * 8 + z)
    loop = [(lat, yl * 8 + (z + k) % 8) for k in range(1, 8)]
    far = (lat + 2 - 4 * yh, lon)
    around = halo_peers(lat, lon)
    greet([twin] + column + [across] + loop + [far] + around)
    started = []

    def launch(copy):
        copy.start()
        started.append(copy)
        return copy

    halos = [launch(copy) for copy in halo_copies(edges, arrivals, sends, recvs, 50, around)]
    tap_half = launch(
        remote(taps_ref.at[pl.ds((1 - c) * 4, 4)], tap_twin, sends, recvs, 22, twin)
    )
    order = (2, 1, 3, 0)

    def chunk_of(k):
        return (x + k) % 4

    def up_part(part):
        return up_ref[:, :, pl.ds(pl.multiple_of(part * 384, 384), 384)]

    twin_copies = {}
    for k in order:
        part = chunk_of(k)

        @pl.when(c == 1)
        def _():
            twin_send[k] = up_part(part).astype(bf16)

        @pl.when(c == 0)
        def _():
            @pl.loop(0, 16)
            def _(block):
                twin_send[k, pl.ds(block * 3, 3)] = down_ref[
                    pl.ds(block * 12 + part * 3, 3)
                ].astype(bf16)

        twin_copies[k] = launch(
            remote(twin_send.at[k], twin_recv.at[k], sends, recvs, k, twin)
        )
    upper, lower = pl.ds(0, 24), pl.ds(24, 24)
    for k in order:
        part = chunk_of(k)
        twin_copies[k].wait_recv()

        @pl.when(c == 0)
        def _():
            total[...] = up_part(part) + twin_recv[k].astype(f32)

        @pl.when(c == 1)
        def _():
            @pl.loop(0, 16)
            def _(block):
                total[pl.ds(block * 3, 3)] = down_ref[
                    pl.ds(block * 12 + part * 3, 3)
                ] + twin_recv[k, pl.ds(block * 3, 3)].astype(f32)

        if k == 2:
            d_send[...] = total[...].astype(bf16)
            via_next = launch(remote(d_send.at[upper], d_recv.at[0], sends, recvs, 20, column[0]))
            via_last = launch(remote(d_send.at[lower], d_recv.at[1], sends, recvs, 21, column[2]))
            tap_half.wait_recv()
            tap_sum[...] = taps_ref[pl.ds(c * 4, 4)] + tap_twin[...]
            for j in range(1, 4):
                launch(
                    remote(
                        tap_sum.at[(x + j) % 4], tap_x.at[j - 1], sends, recvs, 22 + j, column[j - 1]
                    )
                )
        elif k == 1:
            x_send[0, lower] = total[lower].astype(bf16)
            launch(remote(x_send.at[0, lower], x_recv.at[0, lower], sends, recvs, 4, column[0]))
            via_next.wait_recv()
            x_send[0, upper] = (total[upper] + d_recv[0].astype(f32)).astype(bf16)
            launch(remote(x_send.at[0, upper], x_recv.at[0, upper], sends, recvs, 5, column[0]))
        elif k == 3:
            x_send[1, upper] = total[upper].astype(bf16)
            launch(remote(x_send.at[1, upper], x_recv.at[1, upper], sends, recvs, 6, column[2]))
            via_last.wait_recv()
            x_send[1, lower] = (total[lower] + d_recv[1].astype(f32)).astype(bf16)
            launch(remote(x_send.at[1, lower], x_recv.at[1, lower], sends, recvs, 19, column[2]))
    for j in (1, 3, 2):
        remote(
            tap_sum.at[x], tap_x.at[j - 1], sends, recvs, 22 + j, column[j - 1]
        ).wait_recv()
    tap_ys[...] = (tap_sum[x] + tap_x[0]) + (tap_x[1] + tap_x[2])
    tap_y = launch(remote(tap_ys, tap_yr, sends, recvs, 26, across))
    tap_y.wait_recv()
    tap_z[z] = tap_ys[...] + tap_yr[...]
    for k in (4, 3, 5, 2, 6, 1, 7):
        launch(remote(tap_z.at[z], tap_z.at[z], sends, recvs, 26 + k, loop[k - 1]))
    remote(x_send.at[0, lower], x_recv.at[0, lower], sends, recvs, 4, column[0]).wait_recv()
    remote(x_send.at[0, upper], x_recv.at[0, upper], sends, recvs, 5, column[0]).wait_recv()
    remote(x_send.at[1, upper], x_recv.at[1, upper], sends, recvs, 6, column[2]).wait_recv()
    remote(x_send.at[1, lower], x_recv.at[1, lower], sends, recvs, 19, column[2]).wait_recv()
    far_half = pl.ds((1 - yl) * 24, 24)
    near_half = pl.ds(yl * 24, 24)

    def summed(rows):
        return total[rows] + (x_recv[0, rows].astype(f32) + x_recv[1, rows].astype(f32))

    y_send[...] = summed(far_half).astype(bf16)
    y_copy = launch(remote(y_send, y_recv, sends, recvs, 7, across))
    total[near_half] = summed(near_half)
    for k in (1, 7, 2, 6, 3, 5, 4):
        owner = (z + 8 - k) % 8
        remote(tap_z.at[owner], tap_z.at[owner], sends, recvs, 26 + k, loop[k - 1]).wait_recv()
    tap_hs[...] = ((tap_z[0] + tap_z[1]) + (tap_z[2] + tap_z[3])) + (
        (tap_z[4] + tap_z[5]) + (tap_z[6] + tap_z[7])
    )
    tap_h = launch(remote(tap_hs, tap_hr, sends, recvs, 34, far))
    y_copy.wait_recv()
    for k in (4, 3, 5, 2, 6, 1, 7):
        zk = (z + k) % 8
        z_send[k - 1] = (
            total[pl.ds(yl * 24 + zk * 3, 3)] + y_recv[pl.ds(zk * 3, 3)].astype(f32)
        ).astype(bf16)
        launch(remote(z_send.at[k - 1], z_recv.at[k - 1], sends, recvs, 7 + k, loop[k - 1]))
    piece = total[pl.ds(yl * 24 + z * 3, 3)] + y_recv[pl.ds(z * 3, 3)].astype(f32)
    tap_h.wait_recv()
    taps_out[c * 4 + x] = (tap_hs[...] + tap_hr[...]) * rscale
    for k in range(1, 4):
        launch(
            remote(
                taps_out.at[c * 4 + x], taps_out.at[c * 4 + x], sends, recvs, 34 + k, column[k - 1]
            )
        )
    for k in (1, 7, 2, 6, 3, 5, 4):
        remote(z_send.at[k - 1], z_recv.at[k - 1], sends, recvs, 7 + k, loop[k - 1]).wait_recv()
        piece = piece + z_recv[k - 1].astype(f32)
    h_send[...] = piece
    far_copy = launch(remote(h_send, h_recv, sends, recvs, 15, far))
    for k in range(1, 4):
        owner = c * 4 + (x + 4 - k) % 4
        remote(
            taps_out.at[owner], taps_out.at[owner], sends, recvs, 34 + k, column[k - 1]
        ).wait_recv()
    here, there = pl.ds(c * 4, 4), pl.ds((1 - c) * 4, 4)
    launch(remote(taps_out.at[here], taps_out.at[here], sends, recvs, 38, twin))
    far_copy.wait_recv()
    pieces[x] = (h_send[...] + h_recv[...]) * rscale
    for k in range(1, 4):
        launch(remote(pieces.at[x], pieces.at[x], sends, recvs, 15 + k, column[k - 1]))
    for k in range(1, 4):
        owner = (x + 4 - k) % 4
        remote(
            pieces.at[owner], pieces.at[owner], sends, recvs, 15 + k, column[k - 1]
        ).wait_recv()
    last = launch(remote(pieces, others, sends, recvs, 39, twin))
    remote(taps_out.at[there], taps_out.at[there], sends, recvs, 38, twin).wait_recv()
    for copy in halos:
        copy.wait_recv()
    last.wait_recv()

    def place(ups, downs):
        for part in range(4):
            up_out[:, :, part * 384 : part * 384 + 384] = ups[part]
            down_out[part * 3 : part * 3 + 3] = downs[part]

    @pl.when(c == 0)
    def _():
        place(pieces, others)

    @pl.when(c == 1)
    def _():
        place(others, pieces)

    for copy in started:
        copy.wait_send()


def sum_weights(sum_up, sum_down, taps, edges, rscale):
    vmem = pl.BlockSpec(memory_space=pltpu.VMEM)
    f32, bf16 = jnp.float32, jnp.bfloat16
    rows, cols, channels = edges[0].shape[0], edges[2].shape[1], edges[0].shape[2]
    up_part, down_part, taps, *arrivals = pl.pallas_call(
        functools.partial(sum_kernel, rscale),
        out_shape=(
            jax.ShapeDtypeStruct((3, 8, 1536), f32),
            jax.ShapeDtypeStruct((12, 8, 384), f32),
            jax.ShapeDtypeStruct((8, 8, 384), f32),
            *halo_shapes(rows, cols, channels),
        ),
        in_specs=[vmem] * 11,
        out_specs=(vmem,) * 11,
        scratch_shapes=[
            pltpu.VMEM((4, 48, 8, 384), bf16),
            pltpu.VMEM((4, 48, 8, 384), bf16),
            pltpu.VMEM((2, 48, 8, 384), bf16),
            pltpu.VMEM((2, 48, 8, 384), bf16),
            pltpu.VMEM((48, 8, 384), bf16),
            pltpu.VMEM((2, 24, 8, 384), bf16),
            pltpu.VMEM((48, 8, 384), f32),
            pltpu.VMEM((24, 8, 384), bf16),
            pltpu.VMEM((24, 8, 384), bf16),
            pltpu.VMEM((7, 3, 8, 384), bf16),
            pltpu.VMEM((7, 3, 8, 384), bf16),
            pltpu.VMEM((3, 8, 384), f32),
            pltpu.VMEM((3, 8, 384), f32),
            pltpu.VMEM((4, 3, 8, 384), f32),
            pltpu.VMEM((4, 3, 8, 384), f32),
            pltpu.VMEM((4, 8, 384), f32),
            pltpu.VMEM((4, 8, 384), f32),
            pltpu.VMEM((3, 8, 384), f32),
            pltpu.VMEM((8, 384), f32),
            pltpu.VMEM((8, 384), f32),
            pltpu.VMEM((8, 8, 384), f32),
            pltpu.VMEM((8, 384), f32),
            pltpu.VMEM((8, 384), f32),
            pltpu.SemaphoreType.DMA((58,)),
            pltpu.SemaphoreType.DMA((58,)),
        ],
        compiler_params=pltpu.CompilerParams(collective_id=2, has_side_effects=True),
        name="sum_weights",
    )(sum_up.reshape(48, 8, 1536), sum_down.reshape(192, 8, 384), taps, *edges)
    return up_part.reshape(24, 1536), down_part.reshape(96, 384), taps, arrivals


def shards(
    feature,
    coverage,
    band_rows,
    depth_weight,
    norm_gain,
    norm_shift,
    up_weight,
    up_bias,
    down_weight,
    down_bias,
    layer_scale,
    cotangent,
):
    rows_max, tile_cols, channels = feature.shape
    kernel = depth_weight.shape[0]
    live_rows = lax.dynamic_index_in_dim(band_rows, lax.axis_index("lat"), 0, keepdims=False)
    inside = jnp.arange(rows_max, dtype=jnp.int32) < live_rows
    covered = jnp.where(inside[:, None], coverage, 0).astype(jnp.bfloat16)
    masked = feature * covered[:, :, None]
    full_up, full_down, arrivals = gather_weights(
        up_weight, down_weight, halo_edges(masked, live_rows)
    )
    framed = framed_by(masked, arrivals, live_rows)
    depth_out = jnp.zeros((rows_max, tile_cols, channels), jnp.float32)
    for row_off in range(kernel):
        for col_off in range(kernel):
            depth_out = depth_out + framed[
                row_off : row_off + rows_max, col_off : col_off + tile_cols
            ].astype(jnp.float32) * depth_weight[row_off, col_off].astype(jnp.float32)
    depth_rows = depth_out.reshape(-1, channels)
    center = jnp.mean(depth_rows, axis=-1, keepdims=True)
    offset = depth_rows - center
    scale_inv = lax.rsqrt(jnp.mean(offset * offset, axis=-1, keepdims=True) + EPSILON)
    standard = offset * scale_inv
    normed = (standard * norm_gain + norm_shift).astype(jnp.bfloat16)
    before = jnp.dot(normed, full_up, preferred_element_type=jnp.float32) + up_bias
    active = smooth_gate(before).astype(jnp.bfloat16)
    branch = jnp.dot(active, full_down, preferred_element_type=jnp.float32) + down_bias
    result = (feature.reshape(-1, channels).astype(jnp.float32) + layer_scale * branch).astype(
        jnp.bfloat16
    )
    cot_live = jnp.where(inside[:, None, None], cotangent, jnp.zeros_like(cotangent)).reshape(
        -1, channels
    )
    upstream = (layer_scale * cot_live.astype(jnp.float32)).astype(jnp.bfloat16)
    sum_down = lax.dot_general(
        active, upstream, (((0,), (0,)), ((), ())), preferred_element_type=jnp.float32
    )
    back_active = lax.dot_general(
        upstream, full_down, (((1,), (1,)), ((), ())), preferred_element_type=jnp.float32
    )
    back_before = (back_active * smooth_slope(before)).astype(jnp.bfloat16)
    sum_up = lax.dot_general(
        normed, back_before, (((0,), (0,)), ((), ())), preferred_element_type=jnp.float32
    )
    back_normed = lax.dot_general(
        back_before, full_up, (((1,), (1,)), ((), ())), preferred_element_type=jnp.float32
    )
    back_unit = back_normed * norm_gain
    back_depth = scale_inv * (
        back_unit
        - jnp.mean(back_unit, axis=-1, keepdims=True)
        - standard * jnp.mean(back_unit * standard, axis=-1, keepdims=True)
    )
    back_depth = back_depth.astype(jnp.bfloat16).reshape(rows_max, tile_cols, channels)
    tap_list = []
    for row_off in range(kernel):
        for col_off in range(kernel):
            tap_list.append(
                jnp.sum(
                    framed[row_off : row_off + rows_max, col_off : col_off + tile_cols].astype(
                        jnp.float32
                    )
                    * back_depth.astype(jnp.float32),
                    axis=(0, 1),
                )
            )
    tap_list.extend([jnp.zeros_like(tap_list[0])] * (64 - kernel * kernel))
    tap_terms = jnp.stack(tap_list, axis=0).reshape(8, 8, channels)
    rscale = 1.0 / math.sqrt(BAND_MEAN * lax.axis_size("lat") * tile_cols * lax.axis_size("lon"))
    up_part, down_part, grad_depth, arrivals = sum_weights(
        sum_up, sum_down, tap_terms, halo_edges(back_depth, live_rows), rscale
    )
    grad_depth = grad_depth.reshape(64, channels)[: kernel * kernel]
    framed_back = framed_by(back_depth, arrivals, live_rows)
    spread = jnp.zeros((rows_max, tile_cols, channels), jnp.float32)
    for row_off in range(kernel):
        for col_off in range(kernel):
            spread = spread + framed_back[
                6 - row_off : 6 - row_off + rows_max, 6 - col_off : 6 - col_off + tile_cols
            ].astype(jnp.float32) * depth_weight[row_off, col_off].astype(jnp.float32)
    grad_local = (
        cotangent.astype(jnp.float32) + covered.astype(jnp.float32)[:, :, None] * spread
    ).astype(jnp.bfloat16)
    grad_in = jnp.where(inside[:, None, None], grad_local, jnp.zeros_like(grad_local))
    block_out = jnp.where(
        inside[:, None, None],
        result.reshape(rows_max, tile_cols, channels),
        jnp.zeros_like(feature),
    )
    return (block_out, grad_in, up_part, down_part, grad_depth.reshape(kernel, kernel, channels))


def solution(mesh):
    placed = (
        P("lat", "lon", None),
        P("lat", "lon"),
        P(),
        P(),
        P(),
        P(),
        P("lon", None),
        P(),
        P("lon", None),
        P(),
        P(),
        P("lat", "lon", None),
    )
    return jax.shard_map(
        shards,
        mesh=mesh,
        in_specs=placed,
        out_specs=(
            P("lat", "lon", None),
            P("lat", "lon", None),
            P("lon", None),
            P("lon", None),
            P(),
        ),
        check_vma=False,
    )
```

time: 237 us -> 188 us (0.79)
  Pallas kernels: 108 us -> 77.9 us
  starting transfers between devices: 22.6 us -> 0 us
  waiting for transfers between devices: 9.67 us -> 0 us
  other arithmetic: 46.3 us -> 53.7 us
  matrix products: 25.6 us -> 28.6 us
  local copies, waits for them, and re-layouts: 19 us -> 22 us
    pallas_call x1 -> x0, Pallas kernels: 26.7 us -> none  [sum_taps(): pl.pallas_call(functools.partial(taps_kernel, rscale), out_shape=jax.Shap...]
    ppermute x8 -> x0, starting transfers between devices: 22.6 us -> none  [the longest x4 11.2 us: shifted(): return lax.ppermute(block, axis, route)]
    ppermute x8 -> x0, waiting for transfers between devices: 9.67 us -> none  [the longest x4 9.66 us: shifted(): return lax.ppermute(block, axis, route)]
    mul x3, other arithmetic: 0.87 us -> 5.11 us  [shards(): framed[row_off:row_off + rows_max, col_off:col_off + tile_cols]]
    slice x5 -> x8, local copies, waits for them, and re-layouts: 1.1 us -> 4.06 us  [the longest x2 1.49 us: halo_edges(): field[:, :3]]
    pallas_call x1, Pallas kernels: 46 us -> 43.5 us  [sum_weights(): pl.pallas_call(functools.partial(sum_kernel, rscale), out_shape=(jax.Shap...]
    unnamed x260 -> x216, local copies, waits for them, and re-layouts: 5.54 us -> 3.94 us
  transfers between devices with their start and end apart: 8 -> 0, of which waited for: 2 -> 0; matrix products, arithmetic and copies ran while one was open for 10% -> 0% of each run, Pallas kernels for 46% -> 0%
where the time goes in v2:
time: 188 us; the launch traced here: 187 us
  Pallas kernels  77.9 us (41%)
  other arithmetic  53.7 us (29%)
  matrix products  28.6 us (15%)
  local copies, waits for them, and re-layouts  22 us (12%)
  between operations  5.29 us (3%)
    pallas_call x1, Pallas kernels, sum_weights(): pl.pallas_call(functools.partial(sum_kernel, rscale), out_shape=(jax.Shap...  43.5 us
    pallas_call x1, Pallas kernels, gather_weights(): pl.pallas_call(gather_kernel, out_shape=(jax.ShapeDtypeStruct((48, 8, 153...  34.4 us
    select_n x1, other arithmetic, shards(): jnp.where(inside[:, None, None], grad_local, jnp.zeros_like(grad_local))  12.6 us
    reduce_sum x1, other arithmetic, shards(): center = jnp.mean(depth_rows, axis=-1, keepdims=True)  12.5 us
    reduce_sum x3, other arithmetic, shards(): jnp.sum(framed[row_off:row_off + rows_max, col_off:col_off + tile_cols].a...  11.9 us
    dot_general x1, matrix products, shards(): jnp.dot(active, full_down, preferred_element_type=jnp.float32) + down_bias  5.52 us
    dot_general x1, matrix products, shards(): lax.dot_general(active, upstream, (((0,), (0,)), ((), ())), preferred_ele...  5.44 us
    dot_general x1, matrix products, shards(): lax.dot_general(upstream, full_down, (((1,), (1,)), ((), ())), preferred_...  5.39 us

profile of v2, /device:TPU:1, one launch (start us, length us, event | category | flops | bytes accessed | tf_op | source)
XLA Modules:
  0.0 187.5 jit_solution(451289088394394580)
XLA Ops:
  0.7 1.3 dynamic_slice.10
  5.2 1.6 convert_reduce_fusion.46
  6.8 0.8 fusion.129
  7.6 1.8 convert_reduce_fusion.48
  9.4 1.7 convert_reduce_fusion.47
  11.1 1.3 broadcast_multiply_fusion
  13.8 0.8 fusion.135
  14.5 1.1 multiply_convert_fusion.3
  16.1 34.4 %gather_weights.1 = (bf16[48,8,1536]{2,1,0:T(8,128)(2,1)}, bf16[192,8,384]{2,1,0:T(8,128)(2,1)}, bf16[32,3,384]{2,1,0:T(4,128)(2,1)}, bf16[32,3,384]{2,1,0:T(4,1...) custom-call(bf16[3,8,1536]{2,1,0:T(8,128)(2,1)} %bitcast.125, ...), custom_call_target="tpu_custom_call" | custom-call | tf_op jit(solution)/shard_map/gather_weights/pallas_call | solution.py:205
  50.5 1.0 maximum_select_fusion
  51.5 1.6 pad_maximum_fusion.1
  53.0 0.8 fusion.122
  54.2 12.5 %fusion.130 = (f32[32,32]{1,0:T(8,128)S(1)}, f32[32,32,384]{2,1,0:T(8,128)S(1)}) fusion(f32[384]{0:T(512)S(1)} %copy-done.25, bf16[38,38,384]{2,1,0:T(8,128)(2,1)S(1)} %fusion.122, f32[384]{0:T(512)S(1)} %copy-done.27, f32[384]{0:T(512)S(1)} %copy-done.31, f32[384]{0:T(512)S(1)} %copy-done.33, f32[384]{0:T(512)S(1)} %copy-done.35, f32[384]{0:T(512)S(1)} %copy-done.37, ...), kind=kLoop, calls=%fused_computation.313 | loop fusion | flops 57801728 | bytes 40187392 | tf_op jit(solution)/shard_map/reduce_sum | solution.py:487
  68.9 0.9 copy-done.98
  69.8 5.0 %fusion.11 = (bf16[1536,1024]{0,1:T(8,128)(2,1)}, f32[1024,1536]{1,0:T(8,128)}) fusion(f32[1536]{0:T(1024)S(1)} %copy-done.101, bf16[1024,384]{1,0:T(8,128)(2,1)S(1)} %bitcast.118, bf16[48,8,1536]{2,1,0:T(8,128)(2,1)S(1)} %copy-done.98), kind=kOutput, calls=%fused_computation.63 | convolution fusion | flops 1223688192 | bytes 11409408 | tf_op jit(solution)/shard_map/dot_general | solution.py:492
  74.8 4.6 %copy.20 = bf16[1536,1024]{1,0:T(8,128)(2,1)} copy(bf16[1536,1024]{0,1:T(8,128)(2,1)} %get-tuple-element.168) | data formatting | bytes 6291456 | tf_op jit(solution)/shard_map/convert_element_type | solution.py:493
  79.5 5.4 %fusion.12.refs_1_ = f32[192,8,384]{2,1,0:T(8,128)} fusion(bf16[1024,384,1]{1,0,2:T(8,128)(2,1)} %bitcast.115, bf16[1536,1024]{1,0:T(8,128)(2,1)} %copy.20), kind=kOutput, calls=%fused_computation.66 | convolution fusion | flops 1207959552 | bytes 6291456 | tf_op jit(solution)/shard_map/dot_general | solution.py:502
  85.0 5.5 %fusion.114 = bf16[1024,384]{1,0:T(8,128)(2,1)S(1)} fusion(bf16[1024,384]{1,0:T(8,128)(2,1)S(1)} %bitcast.113, f32[1024,1536]{1,0:T(8,128)} %get-tuple-element.169, f32[1536]{0:T(1024)S(1)} %copy-done.102, bf16[192,8,384]{2,1,0:T(8,128)(2,1)S(1)} %copy-done.100, f32[384]{0:T(512)S(1)} %copy-done.103, f32[384]{0:T(512)S(1)} %copy-done.93), kind=kOutput, calls=%fused_computation.220 | convolution fusion | flops 1225654272 | bytes 9053184 | tf_op jit(solution)/shard_map/dot_general | solution.py:494
  90.5 5.4 %fusion.6 = bf16[1024,1536]{1,0:T(8,128)(2,1)S(1)} fusion(f32[1024,1536]{1,0:T(8,128)S(1)} %bitcast.128, bf16[1024,384]{1,0:T(8,128)(2,1)S(1)} %bitcast.116, f32[1536]{0:T(1024)S(1)} %copy-done.102, bf16[192,8,384]{2,1,0:T(8,128)(2,1)S(1)} %copy-done.100), kind=kOutput, calls=%fused_computation.58 | convolution fusion | flops 1239416832 | bytes 11409408 | tf_op jit(solution)/shard_map/dot_general | solution.py:505
  96.0 1.0 broadcast_select_fusion.1
  97.1 1.3 copy-done.99
  98.3 2.5 %fusion.128 = (f32[1024]{0:T(1024)S(1)}, f32[1024]{0:T(1024)S(1)}, bf16[1024,384]{1,0:T(8,128)(2,1)}, f32[1024,384]{1,0:T(8,128)S(1)}) fusion(f32[1024]{0:T(1024)S(1)} %copy-done.87, f32[1024]{0:T(1024)S(1)} %copy-done.86, f32[32,32,384]{2,1,0:T(8,128)S(1)} %get-tuple-element.151, f32[384]{0:T(512)S(1)} %copy-done.95, f32[384]{0:T(512)S(1)} %copy-done.97, ...), kind=kOutput, calls=%fused_computation.311 | convolution fusion | flops 1211496448 | bytes 8276992 | tf_op jit(solution)/shard_map/dot_general | solution.py:512
  100.8 5.2 %fusion.113 = (f32[384]{0:T(512)S(1)}, f32[384]{0:T(512)S(1)}, f32[384]{0:T(512)S(1)}, f32[384]{0:T(512)S(1)}, f32[384]{0:T(512)S(1)}, /*index=5*/f32[384]{0:T(5...) fusion(bf16[38,38,384]{2,1,0:T(8,128)(2,1)S(1)} %fusion.122, ...), kind=kLoop, calls=%fused_computation.218 | loop fusion | flops 24372480 | bytes 18131968 | tf_op jit(solution)/shard_map/reduce_sum | solution.py:526
  106.8 2.8 %fusion.77 = (f32[384]{0:T(512)S(1)}, f32[384]{0:T(512)S(1)}, f32[384]{0:T(512)S(1)}, f32[384]{0:T(512)S(1)}, f32[384]{0:T(512)S(1)}, /*index=5*/f32[384]{0:T(51...) fusion(bf16[38,38,384]{2,1,0:T(8,128)(2,1)S(1)} %fusion.122, ...), kind=kLoop, calls=%fused_computation.182 | loop fusion | flops 15723648 | bytes 11030016 | tf_op jit(solution)/shard_map/reduce_sum | solution.py:526
  109.6 3.9 %fusion.95 = (f32[384]{0:T(512)S(1)}, f32[384]{0:T(512)S(1)}, f32[384]{0:T(512)S(1)}, f32[384]{0:T(512)S(1)}, f32[384]{0:T(512)S(1)}, /*index=5*/f32[384]{0:T(51...) fusion(bf16[38,38,384]{2,1,0:T(8,128)(2,1)S(1)} %fusion.122, ...), kind=kLoop, calls=%fused_computation.200 | loop fusion | flops 21619968 | bytes 14969856 | tf_op jit(solution)/shard_map/reduce_sum | solution.py:526
  114.0 5.0 %stack.211 = f32[64,384]{1,0:T(8,128)} concatenate(f32[1,384]{1,0:T(1,128)S(1)} %stack.159, f32[1,384]{1,0:T(1,128)S(1)} %stack.160, f32[1,384]{1,0:T(1,128)S(1)} %stack.161, f32[1,384]{1,0:T(1,128)S(1)} %stack.162, f32[1,384]{1,0:T(1,128)S(1)} %stack.163, f32[1,384]{1,0:T(1,128)S(1)} %stack.164, f32[1,384]{1,0:T(1,128)S(1)} %stack.165, f32[1,384]{1,0:T(1,128)S(1)} %stack.166, ...), dimensions={0} | concatenate | bytes 196608 | tf_op jit(solution)/shard_map/stack | solution.py:535
  120.2 0.7 fusion.132
  121.3 4.7 %fusion.14.refs_0_ = f32[48,8,1536]{2,1,0:T(8,128)} fusion(bf16[1024,1536]{1,0:T(8,128)(2,1)} %copy-done.104, bf16[384,1024]{1,0:T(8,128)(2,1)S(1)} %copy.19), kind=kOutput, calls=%fused_computation.68 | convolution fusion | flops 1207959552 | bytes 6291456 | tf_op jit(solution)/shard_map/dot_general | solution.py:509
  126.0 43.5 %sum_weights.1 = (f32[3,8,1536]{2,1,0:T(8,128)}, f32[12,8,384]{2,1,0:T(8,128)}, f32[8,8,384]{2,1,0:T(8,128)}, bf16[32,3,384]{2,1,0:T(4,128)(2,1)}, bf16[32,3,384...) custom-call(f32[48,8,1536]{2,1,0:T(8,128)} %fusion.14.refs_0_, ...), custom_call_target="tpu_custom_call" | custom-call | tf_op jit(solution)/shard_map/sum_weights/pallas_call | solution.py:413
  169.8 1.0 maximum_select_fusion.2
  170.8 1.5 pad_maximum_fusion
  172.8 12.6 %broadcast_select_fusion = bf16[32,32,384]{2,1,0:T(8,128)(2,1)} fusion(pred[32]{0:T(512)(128)(4,1)} %copy-done.90, f32[384]{0:T(512)S(1)} %copy-done.26, bf16[38,38,384]{2,1,0:T(8,128)(2,1)S(1)} %fusion.123, f32[384]{0:T(512)S(1)} %copy-done.28, f32[384]{0:T(512)S(1)} %copy-done.32, f32[384]{0:T(512)S(1)} %copy-done.34, f32[384]{0:T(512)S(1)} %copy-done.36, ...), kind=kLoop, calls=%fused_computation.237 | loop fusion | flops 59375616 | bytes 40187424 | tf_op jit(solution)/shard_map/jit(_where)/select_n | solution.py:551
  (287 shorter events, 8.9 us)
Async XLA Ops:
  15.7 38.2 %copy-start.19 = (f32[384]{0:T(512)S(1)}, f32[384]{0:T(512)}, u32[]{:S(2)}) copy-start(f32[384]{0:T(512)} %get-tuple-element.142) | copy-start | bytes 4612
  15.7 38.2 %copy-start.21 = (f32[384]{0:T(512)S(1)}, f32[384]{0:T(512)}, u32[]{:S(2)}) copy-start(f32[384]{0:T(512)} %get-tuple-element.143) | copy-start | bytes 4612
  15.7 38.2 %copy-start.23 = (f32[384]{0:T(512)S(1)}, f32[384]{0:T(512)}, u32[]{:S(2)}) copy-start(f32[384]{0:T(512)} %get-tuple-element.144) | copy-start | bytes 4612
  15.7 38.2 %copy-start.25 = (f32[384]{0:T(512)S(1)}, f32[384]{0:T(512)}, u32[]{:S(2)}) copy-start(f32[384]{0:T(512)} %get-tuple-element.145) | copy-start | bytes 4612
  15.7 38.2 %copy-start.27 = (f32[384]{0:T(512)S(1)}, f32[384]{0:T(512)}, u32[]{:S(2)}) copy-start(f32[384]{0:T(512)} %get-tuple-element.146) | copy-start | bytes 4612
  15.7 38.2 %copy-start.29 = (f32[384]{0:T(512)S(1)}, f32[384]{0:T(512)}, u32[]{:S(2)}) copy-start(f32[384]{0:T(512)} %get-tuple-element.98) | copy-start | bytes 4612
  15.8 38.2 %copy-start.31 = (f32[384]{0:T(512)S(1)}, f32[384]{0:T(512)}, u32[]{:S(2)}) copy-start(f32[384]{0:T(512)} %get-tuple-element.99) | copy-start | bytes 4612
  15.8 38.2 %copy-start.33 = (f32[384]{0:T(512)S(1)}, f32[384]{0:T(512)}, u32[]{:S(2)}) copy-start(f32[384]{0:T(512)} %get-tuple-element.100) | copy-start | bytes 4612
  15.8 38.2 %copy-start.35 = (f32[384]{0:T(512)S(1)}, f32[384]{0:T(512)}, u32[]{:S(2)}) copy-start(f32[384]{0:T(512)} %get-tuple-element.101) | copy-start | bytes 4612
  15.8 38.2 %copy-start.37 = (f32[384]{0:T(512)S(1)}, f32[384]{0:T(512)}, u32[]{:S(2)}) copy-start(f32[384]{0:T(512)} %get-tuple-element.102) | copy-start | bytes 4612
  15.8 38.2 %copy-start.39 = (f32[384]{0:T(512)S(1)}, f32[384]{0:T(512)}, u32[]{:S(2)}) copy-start(f32[384]{0:T(512)} %get-tuple-element.103) | copy-start | bytes 4612
  15.8 38.2 %copy-start.41 = (f32[384]{0:T(512)S(1)}, f32[384]{0:T(512)}, u32[]{:S(2)}) copy-start(f32[384]{0:T(512)} %get-tuple-element.104) | copy-start | bytes 4612
  15.8 38.2 %copy-start.43 = (f32[384]{0:T(512)S(1)}, f32[384]{0:T(512)}, u32[]{:S(2)}) copy-start(f32[384]{0:T(512)} %get-tuple-element.105) | copy-start | bytes 4612
  15.8 38.2 %copy-start.45 = (f32[384]{0:T(512)S(1)}, f32[384]{0:T(512)}, u32[]{:S(2)}) copy-start(f32[384]{0:T(512)} %get-tuple-element.106) | copy-start | bytes 4612
  15.8 38.2 %copy-start.47 = (f32[384]{0:T(512)S(1)}, f32[384]{0:T(512)}, u32[]{:S(2)}) copy-start(f32[384]{0:T(512)} %get-tuple-element.107) | copy-start | bytes 4612
  15.8 38.2 %copy-start.49 = (f32[384]{0:T(512)S(1)}, f32[384]{0:T(512)}, u32[]{:S(2)}) copy-start(f32[384]{0:T(512)} %get-tuple-element.108) | copy-start | bytes 4612
  15.9 38.2 %copy-start.51 = (f32[384]{0:T(512)S(1)}, f32[384]{0:T(512)}, u32[]{:S(2)}) copy-start(f32[384]{0:T(512)} %get-tuple-element.109) | copy-start | bytes 4612
  15.9 38.2 %copy-start.53 = (f32[384]{0:T(512)S(1)}, f32[384]{0:T(512)}, u32[]{:S(2)}) copy-start(f32[384]{0:T(512)} %get-tuple-element.110) | copy-start | bytes 4612
  15.9 38.2 %copy-start.55 = (f32[384]{0:T(512)S(1)}, f32[384]{0:T(512)}, u32[]{:S(2)}) copy-start(f32[384]{0:T(512)} %get-tuple-element.111) | copy-start | bytes 4612
  15.9 38.2 %copy-start.57 = (f32[384]{0:T(512)S(1)}, f32[384]{0:T(512)}, u32[]{:S(2)}) copy-start(f32[384]{0:T(512)} %get-tuple-element.112) | copy-start | bytes 4612
  15.9 38.2 %copy-start.59 = (f32[384]{0:T(512)S(1)}, f32[384]{0:T(512)}, u32[]{:S(2)}) copy-start(f32[384]{0:T(512)} %get-tuple-element.113) | copy-start | bytes 4612
  15.9 38.2 %copy-start.61 = (f32[384]{0:T(512)S(1)}, f32[384]{0:T(512)}, u32[]{:S(2)}) copy-start(f32[384]{0:T(512)} %get-tuple-element.114) | copy-start | bytes 4612
  15.9 38.2 %copy-start.63 = (f32[384]{0:T(512)S(1)}, f32[384]{0:T(512)}, u32[]{:S(2)}) copy-start(f32[384]{0:T(512)} %get-tuple-element.115) | copy-start | bytes 4612
  15.9 38.2 %copy-start.65 = (f32[384]{0:T(512)S(1)}, f32[384]{0:T(512)}, u32[]{:S(2)}) copy-start(f32[384]{0:T(512)} %get-tuple-element.116) | copy-start | bytes 4612
  15.9 38.2 %copy-start.67 = (f32[384]{0:T(512)S(1)}, f32[384]{0:T(512)}, u32[]{:S(2)}) copy-start(f32[384]{0:T(512)} %get-tuple-element.117) | copy-start | bytes 4612
  15.9 38.2 %copy-start.69 = (f32[384]{0:T(512)S(1)}, f32[384]{0:T(512)}, u32[]{:S(2)}) copy-start(f32[384]{0:T(512)} %get-tuple-element.118) | copy-start | bytes 4612
  16.0 38.2 %copy-start.71 = (f32[384]{0:T(512)S(1)}, f32[384]{0:T(512)}, u32[]{:S(2)}) copy-start(f32[384]{0:T(512)} %get-tuple-element.119) | copy-start | bytes 4612
  16.0 38.2 %copy-start.73 = (f32[384]{0:T(512)S(1)}, f32[384]{0:T(512)}, u32[]{:S(2)}) copy-start(f32[384]{0:T(512)} %get-tuple-element.120) | copy-start | bytes 4612
  16.0 38.2 %copy-start.75 = (f32[384]{0:T(512)S(1)}, f32[384]{0:T(512)}, u32[]{:S(2)}) copy-start(f32[384]{0:T(512)} %get-tuple-element.121) | copy-start | bytes 4612
  16.0 38.2 %copy-start.77 = (f32[384]{0:T(512)S(1)}, f32[384]{0:T(512)}, u32[]{:S(2)}) copy-start(f32[384]{0:T(512)} %get-tuple-element.122) | copy-start | bytes 4612
  16.0 38.2 %copy-start.79 = (f32[384]{0:T(512)S(1)}, f32[384]{0:T(512)}, u32[]{:S(2)}) copy-start(f32[384]{0:T(512)} %get-tuple-element.123) | copy-start | bytes 4612
  126.0 44.9 %copy-start.3 = (bf16[3,38,384]{2,1,0:T(8,128)(2,1)S(1)}, bf16[3,38,384]{2,1,0:T(8,128)(2,1)}, u32[]{:S(2)}) copy-start(bf16[3,38,384]{2,1,0:T(8,128)(2,1)} %copy-done.2) | copy-start | bytes 262660
  (75 other events, 585.8 us)

commit v3 on v2

--- a/solution.py
+++ b/solution.py
@@ -9,24 +9,12 @@
 from jax.sharding import PartitionSpec as P
 
 BAND_MEAN = 16
+TILE = 256
 
 
 SQRT_TWO_PI = 0.7978845608028654
 CUBIC = 0.044715
 EPSILON = 1e-06
-
-
-def smooth_gate(pre_act):
-    argument = SQRT_TWO_PI * (pre_act + CUBIC * pre_act * pre_act * pre_act)
-    return 0.5 * pre_act * (1.0 + jnp.tanh(argument))
-
-
-def smooth_slope(pre_act):
-    argument = SQRT_TWO_PI * (pre_act + CUBIC * pre_act * pre_act * pre_act)
-    tangent = jnp.tanh(argument)
-    return 0.5 * (1.0 + tangent) + 0.5 * pre_act * (1.0 - tangent * tangent) * SQRT_TWO_PI * (
-        1.0 + 3.0 * CUBIC * pre_act * pre_act
-    )
 
 
 def places():
@@ -453,6 +441,99 @@
     return up_part.reshape(24, 1536), down_part.reshape(96, 384), taps, arrivals
 
 
+def token_kernel(
+    live_ref, depth_ref, feature_ref, cot_ref, gain_ref, shift_ref, up_ref, up_bias_ref,
+    down_ref, down_bias_ref, scale_ref, out_ref, back_ref, sum_up_ref, sum_down_ref,
+):
+    step = pl.program_id(0)
+    f32, bf16 = jnp.float32, jnp.bfloat16
+    rows = depth_ref.shape[0]
+
+    def dot(left, right, dims):
+        return lax.dot_general(left, right, ((dims[:1], dims[1:]), ((), ())), preferred_element_type=f32)
+
+    @pl.when(step == 0)
+    def _():
+        sum_up_ref[...] = jnp.zeros_like(sum_up_ref)
+        sum_down_ref[...] = jnp.zeros_like(sum_down_ref)
+
+    index = step * rows + lax.broadcasted_iota(jnp.int32, (rows, 1), 0)
+    inside = index < live_ref[0]
+    depth = depth_ref[...]
+    gain, layer_scale = gain_ref[...], scale_ref[...]
+    offset = depth - jnp.mean(depth, axis=-1, keepdims=True)
+    scale_inv = lax.rsqrt(jnp.mean(offset * offset, axis=-1, keepdims=True) + EPSILON)
+    standard = offset * scale_inv
+    normed = (standard * gain + shift_ref[...]).astype(bf16)
+    upstream = jnp.where(inside, layer_scale * cot_ref[...].astype(f32), 0.0).astype(bf16)
+    before = dot(normed, up_ref[...], (1, 0)) + up_bias_ref[...]
+    square = before * before
+    tangent = jnp.tanh(SQRT_TWO_PI * (before + CUBIC * square * before))
+    half = 0.5 * (1.0 + tangent)
+    active = (before * half).astype(bf16)
+    slope = half + 0.5 * before * (1.0 - tangent * tangent) * SQRT_TWO_PI * (
+        1.0 + 3.0 * CUBIC * square
+    )
+    back_active = dot(upstream, down_ref[...], (1, 1))
+    back_before = (back_active * slope).astype(bf16)
+    branch = dot(active, down_ref[...], (1, 0)) + down_bias_ref[...]
+    result = feature_ref[...].astype(f32) + layer_scale * branch
+    out_ref[...] = jnp.where(inside, result, 0.0).astype(bf16)
+    back_unit = dot(back_before, up_ref[...], (1, 1)) * gain
+    back_depth = scale_inv * (
+        back_unit
+        - jnp.mean(back_unit, axis=-1, keepdims=True)
+        - standard * jnp.mean(back_unit * standard, axis=-1, keepdims=True)
+    )
+    back_ref[...] = back_depth.astype(bf16)
+    sum_down_ref[...] += dot(active, upstream, (0, 0))
+    sum_up_ref[...] += dot(normed, back_before, (0, 0))
+
+
+def token_block(
+    live, depth_rows, feature_rows, cot_rows, gain, shift, up, up_bias, down, down_bias, scale
+):
+    pixels, channels = depth_rows.shape
+    hidden = up.shape[1]
+    tile = TILE
+    f32, bf16 = jnp.float32, jnp.bfloat16
+
+    def per_tile():
+        return pl.BlockSpec((tile, channels), lambda i: (i, 0))
+
+    def whole(*shape):
+        return pl.BlockSpec(shape, lambda i: (0, 0))
+
+    return pl.pallas_call(
+        token_kernel,
+        grid=(pixels // tile,),
+        out_shape=(
+            jax.ShapeDtypeStruct((pixels, channels), bf16),
+            jax.ShapeDtypeStruct((pixels, channels), bf16),
+            jax.ShapeDtypeStruct((channels, hidden), f32),
+            jax.ShapeDtypeStruct((hidden, channels), f32),
+        ),
+        in_specs=[
+            pl.BlockSpec(memory_space=pltpu.SMEM),
+            per_tile(),
+            per_tile(),
+            per_tile(),
+            whole(1, channels),
+            whole(1, channels),
+            whole(channels, hidden),
+            whole(1, hidden),
+            whole(hidden, channels),
+            whole(1, channels),
+            whole(1, channels),
+        ],
+        out_specs=(per_tile(), per_tile(), whole(channels, hidden), whole(hidden, channels)),
+        name="token_block",
+    )(
+        live, depth_rows, feature_rows, cot_rows, gain[None], shift[None], up, up_bias[None],
+        down, down_bias[None], scale[None],
+    )
+
+
 def shards(
     feature,
     coverage,
@@ -483,42 +564,20 @@
             depth_out = depth_out + framed[
                 row_off : row_off + rows_max, col_off : col_off + tile_cols
             ].astype(jnp.float32) * depth_weight[row_off, col_off].astype(jnp.float32)
-    depth_rows = depth_out.reshape(-1, channels)
-    center = jnp.mean(depth_rows, axis=-1, keepdims=True)
-    offset = depth_rows - center
-    scale_inv = lax.rsqrt(jnp.mean(offset * offset, axis=-1, keepdims=True) + EPSILON)
-    standard = offset * scale_inv
-    normed = (standard * norm_gain + norm_shift).astype(jnp.bfloat16)
-    before = jnp.dot(normed, full_up, preferred_element_type=jnp.float32) + up_bias
-    active = smooth_gate(before).astype(jnp.bfloat16)
-    branch = jnp.dot(active, full_down, preferred_element_type=jnp.float32) + down_bias
-    result = (feature.reshape(-1, channels).astype(jnp.float32) + layer_scale * branch).astype(
-        jnp.bfloat16
-    )
-    cot_live = jnp.where(inside[:, None, None], cotangent, jnp.zeros_like(cotangent)).reshape(
-        -1, channels
-    )
-    upstream = (layer_scale * cot_live.astype(jnp.float32)).astype(jnp.bfloat16)
-    sum_down = lax.dot_general(
-        active, upstream, (((0,), (0,)), ((), ())), preferred_element_type=jnp.float32
-    )
-    back_active = lax.dot_general(
-        upstream, full_down, (((1,), (1,)), ((), ())), preferred_element_type=jnp.float32
-    )
-    back_before = (back_active * smooth_slope(before)).astype(jnp.bfloat16)
-    sum_up = lax.dot_general(
-        normed, back_before, (((0,), (0,)), ((), ())), preferred_element_type=jnp.float32
-    )
-    back_normed = lax.dot_general(
-        back_before, full_up, (((1,), (1,)), ((), ())), preferred_element_type=jnp.float32
-    )
-    back_unit = back_normed * norm_gain
-    back_depth = scale_inv * (
-        back_unit
-        - jnp.mean(back_unit, axis=-1, keepdims=True)
-        - standard * jnp.mean(back_unit * standard, axis=-1, keepdims=True)
-    )
-    back_depth = back_depth.astype(jnp.bfloat16).reshape(rows_max, tile_cols, channels)
+    block_rows, back_rows, sum_up, sum_down = token_block(
+        (live_rows * tile_cols).reshape(1),
+        depth_out.reshape(-1, channels),
+        feature.reshape(-1, channels),
+        cotangent.reshape(-1, channels),
+        norm_gain,
+        norm_shift,
+        full_up,
+        up_bias,
+        full_down,
+        down_bias,
+        layer_scale,
+    )
+    back_depth = back_rows.reshape(rows_max, tile_cols, channels)
     tap_list = []
     for row_off in range(kernel):
         for col_off in range(kernel):
@@ -549,11 +608,7 @@
         cotangent.astype(jnp.float32) + covered.astype(jnp.float32)[:, :, None] * spread
     ).astype(jnp.bfloat16)
     grad_in = jnp.where(inside[:, None, None], grad_local, jnp.zeros_like(grad_local))
-    block_out = jnp.where(
-        inside[:, None, None],
-        result.reshape(rows_max, tile_cols, channels),
-        jnp.zeros_like(feature),
-    )
+    block_out = block_rows.reshape(rows_max, tile_cols, channels)
     return (block_out, grad_in, up_part, down_part, grad_depth.reshape(kernel, kernel, channels))
 
 

time: 188 us -> 162 us (0.86)
  matrix products: 28.6 us -> 0 us
  Pallas kernels: 77.9 us -> 94.6 us
  other arithmetic: 53.7 us -> 44.8 us
  local copies, waits for them, and re-layouts: 22 us -> 17.1 us
    dot_general x6 -> x0, matrix products: 28.6 us -> none  [the longest x1 5.52 us: shards(): jnp.dot(active, full_down, preferred_element_type=jnp.float32) + down_bias]
    pallas_call x0 -> x1, Pallas kernels: none -> 16.7 us  [token_block(): pl.pallas_call(token_kernel, grid=(pixels // tile,), out_shape=(jax.Shape...]
    reduce_sum x2 -> x0, other arithmetic: 12.9 us -> none  [the longest x1 12.5 us: shards(): center = jnp.mean(depth_rows, axis=-1, keepdims=True)]
    add x0 -> x1, other arithmetic: none -> 12.3 us  [shards(): depth_out + framed[row_off:row_off + rows_max, col_off:col_off + tile_col...]
    mul x3, other arithmetic: 5.11 us -> 0.27 us  [shards(): framed[row_off:row_off + rows_max, col_off:col_off + tile_cols]]
    convert_element_type x1 -> x0, local copies, waits for them, and re-layouts: 4.64 us -> none  [shards(): active = smooth_gate(before).astype(jnp.bfloat16)]
    broadcast_in_dim x0 -> x5, local copies, waits for them, and re-layouts: none -> 2.86 us  [the longest x1 0.6 us: token_block(): up_bias[None]]
    unnamed x216 -> x38, local copies, waits for them, and re-layouts: 3.94 us -> 1.41 us
where the time goes in v3:
time: 162 us; the launch traced here: 161 us
  Pallas kernels  94.6 us (58%)
  other arithmetic  44.8 us (28%)
  local copies, waits for them, and re-layouts  17.1 us (11%)
  between operations  4.82 us (3%)
    pallas_call x1, Pallas kernels, sum_weights(): pl.pallas_call(functools.partial(sum_kernel, rscale), out_shape=(jax.Shap...  43.7 us
    pallas_call x1, Pallas kernels, gather_weights(): pl.pallas_call(gather_kernel, out_shape=(jax.ShapeDtypeStruct((48, 8, 153...  34.2 us
    pallas_call x1, Pallas kernels, token_block(): pl.pallas_call(token_kernel, grid=(pixels // tile,), out_shape=(jax.Shape...  16.7 us
    select_n x1, other arithmetic, shards(): jnp.where(inside[:, None, None], grad_local, jnp.zeros_like(grad_local))  12.5 us
    add x1, other arithmetic, shards(): depth_out + framed[row_off:row_off + rows_max, col_off:col_off + tile_col...  12.3 us
    reduce_sum x3, other arithmetic, shards(): jnp.sum(framed[row_off:row_off + rows_max, col_off:col_off + tile_cols].a...  11.7 us
    another operation x54, local copies, waits for them, and re-layouts, shards(): tap_terms = jnp.stack(tap_list, axis=0).reshape(8, 8, channels)  5.13 us

profile of v3, /device:TPU:1, one launch (start us, length us, event | category | flops | bytes accessed | tf_op | source)
XLA Modules:
  0.0 161.4 jit_solution(12487002171693961256)
XLA Ops:
  0.6 1.3 dynamic_slice.10
  3.3 0.7 iota_compare_fusion
  4.0 0.8 fusion.99
  4.8 1.3 broadcast_multiply_fusion
  6.2 0.6 fusion.101
  6.8 0.7 fusion.102
  7.5 0.8 fusion.103
  8.2 34.2 %gather_weights.1 = (bf16[48,8,1536]{2,1,0:T(8,128)(2,1)}, bf16[192,8,384]{2,1,0:T(8,128)(2,1)}, bf16[32,3,384]{2,1,0:T(4,128)(2,1)}, bf16[32,3,384]{2,1,0:T(4,1...) custom-call(bf16[3,8,1536]{2,1,0:T(8,128)(2,1)} %bitcast.84, ...), custom_call_target="tpu_custom_call" | custom-call | tf_op jit(solution)/shard_map/gather_weights/pallas_call | solution.py:193
  42.4 1.0 maximum_select_fusion
  43.4 1.5 pad_maximum_fusion.1
  46.8 12.3 %fusion.47 = f32[32,32,384]{2,1,0:T(8,128)} fusion(f32[384]{0:T(512)S(1)} %get-tuple-element.151, f32[384]{0:T(512)S(1)} %get-tuple-element.152, f32[384]{0:T(512)S(1)} %get-tuple-element.105, f32[384]{0:T(512)S(1)} %get-tuple-element.106, f32[384]{0:T(512)S(1)} %get-tuple-element.107, f32[384]{0:T(512)S(1)} %get-tuple-element.108, ...), kind=kLoop, calls=%fused_computation.147 | loop fusion | flops 57409536 | bytes 40183296 | tf_op jit(solution)/shard_map/add | solution.py:564
  59.8 0.6 broadcast_in_dim.33.up_bias_ref
  60.4 0.6 broadcast_in_dim.31.gain_ref
  61.0 0.6 broadcast_in_dim.32.shift_ref
  61.5 0.6 broadcast_in_dim.34.down_bias_ref
  62.1 0.5 broadcast_in_dim.35.scale_ref
  62.7 16.7 %token_block.1 = (bf16[1024,384]{1,0:T(8,128)(2,1)}, bf16[1024,384]{1,0:T(8,128)(2,1)}, f32[384,1536]{1,0:T(8,128)}, f32[1536,384]{1,0:T(8,128)}) custom-call(s32[1]{0:T(128)} %bitcast.1.live_ref, f32[1024,384]{1,0:T(8,128)} %bitcast.71, bf16[1024,384]{1,0:T(8,128)(2,1)} %bitcast.72, bf16[1024,384]{1,0:T(8,128)(2,1)} %bitcast.73, ...), custom_call_target="tpu_custom_call" | custom-call | tf_op jit(solution)/shard_map/token_block/pallas_call | solution.py:507
  79.4 0.9 slice.696
  80.3 1.4 constant_dynamic-slice_fusion.1
  81.7 5.0 %fusion.96 = (f32[384]{0:T(512)S(1)}, f32[384]{0:T(512)S(1)}, f32[384]{0:T(512)S(1)}, f32[384]{0:T(512)S(1)}, f32[384]{0:T(512)S(1)}, /*index=5*/f32[384]{0:T(51...) fusion(bf16[38,38,384]{2,1,0:T(8,128)(2,1)S(1)} %fusion.97, ...), kind=kLoop, calls=%fused_computation.196 | loop fusion | flops 21619968 | bytes 14969856 | tf_op jit(solution)/shard_map/reduce_sum | solution.py:585
  86.9 4.0 %fusion.78 = (f32[384]{0:T(512)S(1)}, f32[384]{0:T(512)S(1)}, f32[384]{0:T(512)S(1)}, f32[384]{0:T(512)S(1)}, f32[384]{0:T(512)S(1)}, /*index=5*/f32[384]{0:T(51...) fusion(bf16[38,38,384]{2,1,0:T(8,128)(2,1)S(1)} %fusion.97, ...), kind=kLoop, calls=%fused_computation.178 | loop fusion | flops 21619968 | bytes 14969856 | tf_op jit(solution)/shard_map/reduce_sum | solution.py:585
  91.1 2.8 %fusion.60 = (f32[384]{0:T(512)S(1)}, f32[384]{0:T(512)S(1)}, f32[384]{0:T(512)S(1)}, f32[384]{0:T(512)S(1)}, f32[384]{0:T(512)S(1)}, /*index=5*/f32[384]{0:T(51...) fusion(bf16[38,38,384]{2,1,0:T(8,128)(2,1)S(1)} %fusion.97, ...), kind=kLoop, calls=%fused_computation.160 | loop fusion | flops 15723648 | bytes 11030016 | tf_op jit(solution)/shard_map/reduce_sum | solution.py:585
  94.1 5.0 %stack.211 = f32[64,384]{1,0:T(8,128)} concatenate(f32[1,384]{1,0:T(1,128)S(1)} %stack.159, f32[1,384]{1,0:T(1,128)S(1)} %stack.160, f32[1,384]{1,0:T(1,128)S(1)} %stack.161, f32[1,384]{1,0:T(1,128)S(1)} %stack.162, f32[1,384]{1,0:T(1,128)S(1)} %stack.163, f32[1,384]{1,0:T(1,128)S(1)} %stack.164, f32[1,384]{1,0:T(1,128)S(1)} %stack.165, f32[1,384]{1,0:T(1,128)S(1)} %stack.166, ...), dimensions={0} | concatenate | bytes 196608 | tf_op jit(solution)/shard_map/stack | solution.py:594
  99.0 0.8 fusion.100
  99.8 0.6 constant_dynamic-slice_fusion.4.refs_5_
  100.4 43.7 %sum_weights.1 = (f32[3,8,1536]{2,1,0:T(8,128)}, f32[12,8,384]{2,1,0:T(8,128)}, f32[8,8,384]{2,1,0:T(8,128)}, bf16[32,3,384]{2,1,0:T(4,128)(2,1)}, bf16[32,3,384...) custom-call(f32[48,8,1536]{2,1,0:T(8,128)} %bitcast.74, ...), custom_call_target="tpu_custom_call" | custom-call | tf_op jit(solution)/shard_map/sum_weights/pallas_call | solution.py:401
  144.2 1.0 maximum_select_fusion.2
  145.3 1.5 pad_maximum_fusion
  146.9 12.5 %broadcast_select_fusion = bf16[32,32,384]{2,1,0:T(8,128)(2,1)} fusion(pred[32]{0:T(512)(128)(4,1)S(1)} %iota_compare_fusion, f32[384]{0:T(512)S(1)} %get-tuple-element.151, bf16[38,38,384]{2,1,0:T(8,128)(2,1)S(1)} %fusion.98, f32[384]{0:T(512)S(1)} %get-tuple-element.152, f32[384]{0:T(512)S(1)} %get-tuple-element.105, f32[384]{0:T(512)S(1)} %get-tuple-element.106, ...), kind=kLoop, calls=%fused_computation.198 | loop fusion | flops 59375616 | bytes 40187424 | tf_op jit(solution)/shard_map/jit(_where)/select_n | solution.py:610
  159.4 0.6 reshape.88
  160.0 0.7 copy.21
  160.7 0.7 copy.22
  (96 shorter events, 0.7 us)
Async XLA Ops:
  8.2 38.2 %copy-start.5 = (bf16[7,7,384]{2,1,0:T(8,128)(2,1)S(1)}, bf16[7,7,384]{2,1,0:T(8,128)(2,1)}, u32[]{:S(2)}) copy-start(bf16[7,7,384]{2,1,0:T(8,128)(2,1)} %param.15) | copy-start | bytes 112900
  42.4 3.9 %copy-start.7 = (bf16[3,32,384]{2,1,0:T(8,128)(2,1)S(1)}, bf16[3,32,384]{2,1,0:T(8,128)(2,1)}, u32[]{:S(2)}) copy-start(bf16[3,32,384]{2,1,0:T(8,128)(2,1)} %get-tuple-element.36) | copy-start | bytes 221188
  42.4 3.9 %copy-start.9 = (bf16[3,3,384]{2,1,0:T(4,128)(2,1)S(1)}, bf16[3,3,384]{2,1,0:T(4,128)(2,1)}, u32[]{:S(2)}) copy-start(bf16[3,3,384]{2,1,0:T(4,128)(2,1)} %get-tuple-element.35) | copy-start | bytes 20740
  42.4 3.9 %copy-start.10 = (bf16[3,3,384]{2,1,0:T(4,128)(2,1)S(1)}, bf16[3,3,384]{2,1,0:T(4,128)(2,1)}, u32[]{:S(2)}) copy-start(bf16[3,3,384]{2,1,0:T(4,128)(2,1)} %get-tuple-element.37) | copy-start | bytes 20740
  46.7 13.1 %copy-start.13 = (f32[1536]{0:T(1024)S(1)}, f32[1536]{0:T(1024)}, u32[]{:S(2)}) copy-start(f32[1536]{0:T(1024)} %param.19) | copy-start | bytes 18436
  46.7 13.7 %copy-start.14 = (f32[384]{0:T(512)S(1)}, f32[384]{0:T(512)}, u32[]{:S(2)}) copy-start(f32[384]{0:T(512)} %param.16) | copy-start | bytes 4612
  46.7 14.2 %copy-start.15 = (f32[384]{0:T(512)S(1)}, f32[384]{0:T(512)}, u32[]{:S(2)}) copy-start(f32[384]{0:T(512)} %param.17) | copy-start | bytes 4612
  46.7 14.8 %copy-start.16 = (f32[384]{0:T(512)S(1)}, f32[384]{0:T(512)}, u32[]{:S(2)}) copy-start(f32[384]{0:T(512)} %param.21) | copy-start | bytes 4612
  46.7 15.4 %copy-start.17 = (f32[384]{0:T(512)S(1)}, f32[384]{0:T(512)}, u32[]{:S(2)}) copy-start(f32[384]{0:T(512)} %param.22) | copy-start | bytes 4612
  80.3 6.4 %copy-start.2 = (bf16[96,384]{1,0:T(8,128)(2,1)}, bf16[96,384]{1,0:T(8,128)(2,1)S(1)}, u32[]{:S(2)}) copy-start(bf16[96,384]{1,0:T(8,128)(2,1)S(1)} %slice.696) | copy-start | bytes 221188
  81.7 5.2 %copy-start = (bf16[1024,384]{1,0:T(8,128)(2,1)S(1)}, bf16[1024,384]{1,0:T(8,128)(2,1)}, u32[]{:S(2)}) copy-start(bf16[1024,384]{1,0:T(8,128)(2,1)} %get-tuple-element.43) | copy-start | bytes 2359300
  144.2 2.6 %copy-start.8 = (bf16[3,32,384]{2,1,0:T(8,128)(2,1)S(1)}, bf16[3,32,384]{2,1,0:T(8,128)(2,1)}, u32[]{:S(2)}) copy-start(bf16[3,32,384]{2,1,0:T(8,128)(2,1)} %get-tuple-element.50) | copy-start | bytes 221188
  144.2 2.6 %copy-start.11 = (bf16[3,3,384]{2,1,0:T(4,128)(2,1)S(1)}, bf16[3,3,384]{2,1,0:T(4,128)(2,1)}, u32[]{:S(2)}) copy-start(bf16[3,3,384]{2,1,0:T(4,128)(2,1)} %get-tuple-element.49) | copy-start | bytes 20740
  144.2 2.6 %copy-start.12 = (bf16[3,3,384]{2,1,0:T(4,128)(2,1)S(1)}, bf16[3,3,384]{2,1,0:T(4,128)(2,1)}, u32[]{:S(2)}) copy-start(bf16[3,3,384]{2,1,0:T(4,128)(2,1)} %get-tuple-element.51) | copy-start | bytes 20740
  144.2 2.7 %copy-start.1 = (bf16[32,32,384]{2,1,0:T(8,128)(2,1)S(1)}, bf16[32,32,384]{2,1,0:T(8,128)(2,1)}, u32[]{:S(2)}) copy-start(bf16[32,32,384]{2,1,0:T(8,128)(2,1)} %param.23) | copy-start | bytes 2359300
  146.9 12.5 %copy-start.6 = (f32[8,8,384]{2,1,0:T(8,128)S(1)}, f32[8,8,384]{2,1,0:T(8,128)}, u32[]{:S(2)}) copy-start(f32[8,8,384]{2,1,0:T(8,128)} %get-tuple-element.54) | copy-start | bytes 294916
  146.9 13.2 %copy-start.4 = (f32[3,8,1536]{2,1,0:T(8,128)S(1)}, f32[3,8,1536]{2,1,0:T(8,128)}, u32[]{:S(2)}) copy-start(f32[3,8,1536]{2,1,0:T(8,128)} %get-tuple-element.52) | copy-start | bytes 442372
  146.9 13.8 %copy-start.3 = (f32[12,8,384]{2,1,0:T(8,128)S(1)}, f32[12,8,384]{2,1,0:T(8,128)}, u32[]{:S(2)}) copy-start(f32[12,8,384]{2,1,0:T(8,128)} %get-tuple-element.53) | copy-start | bytes 442372

commit v4 on v3

--- a/solution.py
+++ b/solution.py
@@ -206,16 +206,53 @@
     return full_up.reshape(384, 1536), full_down.reshape(1536, 384), arrivals
 
 
+def tap_sums(framed_ref, back_ref, framed, shifted, back, taps_ref):
+    f32 = jnp.float32
+
+    @pl.loop(0, 38)
+    def _(row):
+        framed[row] = framed_ref[row].astype(f32)
+
+    @pl.loop(0, 32)
+    def _(row):
+        back[row] = back_ref[row].astype(f32)
+
+    taps_ref[6:8] = jnp.zeros((2, 8, 384), f32)
+    for col_off in range(7):
+
+        @pl.loop(0, 38)
+        def _(row):
+            shifted[row] = framed[row, col_off : col_off + 32]
+
+        for group in range(3):
+            lanes = slice(group * 128, group * 128 + 128)
+
+            def add_row(row, sums):
+                gradient = back[row, :, lanes]
+                return tuple(
+                    sums[off]
+                    + jnp.sum((shifted[row + off, :, lanes] * gradient).reshape(4, 8, 128), axis=0)
+                    for off in range(7)
+                )
+
+            sums = lax.fori_loop(0, 32, add_row, (jnp.zeros((8, 128), f32),) * 7)
+            for off in range(7):
+                tap = off * 7 + col_off
+                taps_ref[tap // 8, tap % 8 : tap % 8 + 1, lanes] = jnp.sum(
+                    sums[off], axis=0, keepdims=True
+                )
+
+
 def sum_kernel(rscale, *refs):
-    up_ref, down_ref, taps_ref = refs[:3]
-    edges = refs[3:11]
-    up_out, down_out, taps_out = refs[11:14]
-    arrivals = refs[14:22]
+    up_ref, down_ref, framed_ref, back_ref = refs[:4]
+    edges = refs[4:12]
+    up_out, down_out, taps_out = refs[12:15]
+    arrivals = refs[15:23]
     (
         twin_send, twin_recv, x_send, x_recv, d_send, d_recv, total, y_send, y_recv, z_send, z_recv,
         h_send, h_recv, pieces, others, tap_twin, tap_sum, tap_x, tap_ys, tap_yr, tap_z,
-        tap_hs, tap_hr, sends, recvs,
-    ) = refs[22:]
+        tap_hs, tap_hr, taps_ref, framed, shifted, back, sends, recvs,
+    ) = refs[23:]
     lat, lon, x, yh, c, yl, z = places()
     f32, bf16 = jnp.float32, jnp.bfloat16
     twin = (lat + 1 - 2 * c, lon)
@@ -233,9 +270,6 @@
         return copy
 
     halos = [launch(copy) for copy in halo_copies(edges, arrivals, sends, recvs, 50, around)]
-    tap_half = launch(
-        remote(taps_ref.at[pl.ds((1 - c) * 4, 4)], tap_twin, sends, recvs, 22, twin)
-    )
     order = (2, 1, 3, 0)
 
     def chunk_of(k):
@@ -284,14 +318,6 @@
             d_send[...] = total[...].astype(bf16)
             via_next = launch(remote(d_send.at[upper], d_recv.at[0], sends, recvs, 20, column[0]))
             via_last = launch(remote(d_send.at[lower], d_recv.at[1], sends, recvs, 21, column[2]))
-            tap_half.wait_recv()
-            tap_sum[...] = taps_ref[pl.ds(c * 4, 4)] + tap_twin[...]
-            for j in range(1, 4):
-                launch(
-                    remote(
-                        tap_sum.at[(x + j) % 4], tap_x.at[j - 1], sends, recvs, 22 + j, column[j - 1]
-                    )
-                )
         elif k == 1:
             x_send[0, lower] = total[lower].astype(bf16)
             launch(remote(x_send.at[0, lower], x_recv.at[0, lower], sends, recvs, 4, column[0]))
@@ -304,16 +330,10 @@
             via_last.wait_recv()
             x_send[1, lower] = (total[lower] + d_recv[1].astype(f32)).astype(bf16)
             launch(remote(x_send.at[1, lower], x_recv.at[1, lower], sends, recvs, 19, column[2]))
-    for j in (1, 3, 2):
-        remote(
-            tap_sum.at[x], tap_x.at[j - 1], sends, recvs, 22 + j, column[j - 1]
-        ).wait_recv()
-    tap_ys[...] = (tap_sum[x] + tap_x[0]) + (tap_x[1] + tap_x[2])
-    tap_y = launch(remote(tap_ys, tap_yr, sends, recvs, 26, across))
-    tap_y.wait_recv()
-    tap_z[z] = tap_ys[...] + tap_yr[...]
-    for k in (4, 3, 5, 2, 6, 1, 7):
-        launch(remote(tap_z.at[z], tap_z.at[z], sends, recvs, 26 + k, loop[k - 1]))
+    tap_sums(framed_ref, back_ref, framed, shifted, back, taps_ref)
+    tap_half = launch(
+        remote(taps_ref.at[pl.ds((1 - c) * 4, 4)], tap_twin, sends, recvs, 22, twin)
+    )
     remote(x_send.at[0, lower], x_recv.at[0, lower], sends, recvs, 4, column[0]).wait_recv()
     remote(x_send.at[0, upper], x_recv.at[0, upper], sends, recvs, 5, column[0]).wait_recv()
     remote(x_send.at[1, upper], x_recv.at[1, upper], sends, recvs, 6, column[2]).wait_recv()
@@ -326,14 +346,13 @@
 
     y_send[...] = summed(far_half).astype(bf16)
     y_copy = launch(remote(y_send, y_recv, sends, recvs, 7, across))
+    tap_half.wait_recv()
+    tap_sum[...] = taps_ref[pl.ds(c * 4, 4)] + tap_twin[...]
+    for j in range(1, 4):
+        launch(
+            remote(tap_sum.at[(x + j) % 4], tap_x.at[j - 1], sends, recvs, 22 + j, column[j - 1])
+        )
     total[near_half] = summed(near_half)
-    for k in (1, 7, 2, 6, 3, 5, 4):
-        owner = (z + 8 - k) % 8
-        remote(tap_z.at[owner], tap_z.at[owner], sends, recvs, 26 + k, loop[k - 1]).wait_recv()
-    tap_hs[...] = ((tap_z[0] + tap_z[1]) + (tap_z[2] + tap_z[3])) + (
-        (tap_z[4] + tap_z[5]) + (tap_z[6] + tap_z[7])
-    )
-    tap_h = launch(remote(tap_hs, tap_hr, sends, recvs, 34, far))
     y_copy.wait_recv()
     for k in (4, 3, 5, 2, 6, 1, 7):
         zk = (z + k) % 8
@@ -342,6 +361,36 @@
         ).astype(bf16)
         launch(remote(z_send.at[k - 1], z_recv.at[k - 1], sends, recvs, 7 + k, loop[k - 1]))
     piece = total[pl.ds(yl * 24 + z * 3, 3)] + y_recv[pl.ds(z * 3, 3)].astype(f32)
+    for j in (1, 3, 2):
+        remote(tap_sum.at[x], tap_x.at[j - 1], sends, recvs, 22 + j, column[j - 1]).wait_recv()
+    tap_ys[...] = (tap_sum[x] + tap_x[0]) + (tap_x[1] + tap_x[2])
+    tap_y = launch(remote(tap_ys, tap_yr, sends, recvs, 26, across))
+    for k in (1, 7, 2, 6, 3, 5, 4):
+        remote(z_send.at[k - 1], z_recv.at[k - 1], sends, recvs, 7 + k, loop[k - 1]).wait_recv()
+        piece = piece + z_recv[k - 1].astype(f32)
+    h_send[...] = piece
+    far_copy = launch(remote(h_send, h_recv, sends, recvs, 15, far))
+    tap_y.wait_recv()
+    tap_z[z] = tap_ys[...] + tap_yr[...]
+    for k in (4, 3, 5, 2, 6, 1, 7):
+        launch(remote(tap_z.at[z], tap_z.at[z], sends, recvs, 26 + k, loop[k - 1]))
+    far_copy.wait_recv()
+    pieces[x] = (h_send[...] + h_recv[...]) * rscale
+    for k in range(1, 4):
+        launch(remote(pieces.at[x], pieces.at[x], sends, recvs, 15 + k, column[k - 1]))
+    for k in (1, 7, 2, 6, 3, 5, 4):
+        owner = (z + 8 - k) % 8
+        remote(tap_z.at[owner], tap_z.at[owner], sends, recvs, 26 + k, loop[k - 1]).wait_recv()
+    tap_hs[...] = ((tap_z[0] + tap_z[1]) + (tap_z[2] + tap_z[3])) + (
+        (tap_z[4] + tap_z[5]) + (tap_z[6] + tap_z[7])
+    )
+    tap_h = launch(remote(tap_hs, tap_hr, sends, recvs, 34, far))
+    for k in range(1, 4):
+        owner = (x + 4 - k) % 4
+        remote(
+            pieces.at[owner], pieces.at[owner], sends, recvs, 15 + k, column[k - 1]
+        ).wait_recv()
+    last = launch(remote(pieces, others, sends, recvs, 39, twin))
     tap_h.wait_recv()
     taps_out[c * 4 + x] = (tap_hs[...] + tap_hr[...]) * rscale
     for k in range(1, 4):
@@ -350,11 +399,6 @@
                 taps_out.at[c * 4 + x], taps_out.at[c * 4 + x], sends, recvs, 34 + k, column[k - 1]
             )
         )
-    for k in (1, 7, 2, 6, 3, 5, 4):
-        remote(z_send.at[k - 1], z_recv.at[k - 1], sends, recvs, 7 + k, loop[k - 1]).wait_recv()
-        piece = piece + z_recv[k - 1].astype(f32)
-    h_send[...] = piece
-    far_copy = launch(remote(h_send, h_recv, sends, recvs, 15, far))
     for k in range(1, 4):
         owner = c * 4 + (x + 4 - k) % 4
         remote(
@@ -362,19 +406,6 @@
         ).wait_recv()
     here, there = pl.ds(c * 4, 4), pl.ds((1 - c) * 4, 4)
     launch(remote(taps_out.at[here], taps_out.at[here], sends, recvs, 38, twin))
-    far_copy.wait_recv()
-    pieces[x] = (h_send[...] + h_recv[...]) * rscale
-    for k in range(1, 4):
-        launch(remote(pieces.at[x], pieces.at[x], sends, recvs, 15 + k, column[k - 1]))
-    for k in range(1, 4):
-        owner = (x + 4 - k) % 4
-        remote(
-            pieces.at[owner], pieces.at[owner], sends, recvs, 15 + k, column[k - 1]
-        ).wait_recv()
-    last = launch(remote(pieces, others, sends, recvs, 39, twin))
-    remote(taps_out.at[there], taps_out.at[there], sends, recvs, 38, twin).wait_recv()
-    for copy in halos:
-        copy.wait_recv()
     last.wait_recv()
 
     def place(ups, downs):
@@ -390,11 +421,14 @@
     def _():
         place(others, pieces)
 
+    for copy in halos:
+        copy.wait_recv()
+    remote(taps_out.at[there], taps_out.at[there], sends, recvs, 38, twin).wait_recv()
     for copy in started:
         copy.wait_send()
 
 
-def sum_weights(sum_up, sum_down, taps, edges, rscale):
+def sum_weights(sum_up, sum_down, framed, back_depth, edges, rscale):
     vmem = pl.BlockSpec(memory_space=pltpu.VMEM)
     f32, bf16 = jnp.float32, jnp.bfloat16
     rows, cols, channels = edges[0].shape[0], edges[2].shape[1], edges[0].shape[2]
@@ -406,7 +440,7 @@
             jax.ShapeDtypeStruct((8, 8, 384), f32),
             *halo_shapes(rows, cols, channels),
         ),
-        in_specs=[vmem] * 11,
+        in_specs=[vmem] * 12,
         out_specs=(vmem,) * 11,
         scratch_shapes=[
             pltpu.VMEM((4, 48, 8, 384), bf16),
@@ -432,18 +466,22 @@
             pltpu.VMEM((8, 8, 384), f32),
             pltpu.VMEM((8, 384), f32),
             pltpu.VMEM((8, 384), f32),
+            pltpu.VMEM((8, 8, 384), f32),
+            pltpu.VMEM((38, 38, 384), f32),
+            pltpu.VMEM((38, 32, 384), f32),
+            pltpu.VMEM((32, 32, 384), f32),
             pltpu.SemaphoreType.DMA((58,)),
             pltpu.SemaphoreType.DMA((58,)),
         ],
         compiler_params=pltpu.CompilerParams(collective_id=2, has_side_effects=True),
         name="sum_weights",
-    )(sum_up.reshape(48, 8, 1536), sum_down.reshape(192, 8, 384), taps, *edges)
+    )(sum_up.reshape(48, 8, 1536), sum_down.reshape(192, 8, 384), framed, back_depth, *edges)
     return up_part.reshape(24, 1536), down_part.reshape(96, 384), taps, arrivals
 
 
 def token_kernel(
-    live_ref, depth_ref, feature_ref, cot_ref, gain_ref, shift_ref, up_ref, up_bias_ref,
-    down_ref, down_bias_ref, scale_ref, out_ref, back_ref, sum_up_ref, sum_down_ref,
+    live_ref, depth_ref, feature_ref, cot_ref, vector_ref, up_ref, up_bias_ref, down_ref,
+    out_ref, back_ref, sum_up_ref, sum_down_ref,
 ):
     step = pl.program_id(0)
     f32, bf16 = jnp.float32, jnp.bfloat16
@@ -460,11 +498,11 @@
     index = step * rows + lax.broadcasted_iota(jnp.int32, (rows, 1), 0)
     inside = index < live_ref[0]
     depth = depth_ref[...]
-    gain, layer_scale = gain_ref[...], scale_ref[...]
+    gain, shift, down_bias, layer_scale = (vector_ref[i : i + 1, :] for i in range(4))
     offset = depth - jnp.mean(depth, axis=-1, keepdims=True)
     scale_inv = lax.rsqrt(jnp.mean(offset * offset, axis=-1, keepdims=True) + EPSILON)
     standard = offset * scale_inv
-    normed = (standard * gain + shift_ref[...]).astype(bf16)
+    normed = (standard * gain + shift).astype(bf16)
     upstream = jnp.where(inside, layer_scale * cot_ref[...].astype(f32), 0.0).astype(bf16)
     before = dot(normed, up_ref[...], (1, 0)) + up_bias_ref[...]
     square = before * before
@@ -476,7 +514,7 @@
     )
     back_active = dot(upstream, down_ref[...], (1, 1))
     back_before = (back_active * slope).astype(bf16)
-    branch = dot(active, down_ref[...], (1, 0)) + down_bias_ref[...]
+    branch = dot(active, down_ref[...], (1, 0)) + down_bias
     result = feature_ref[...].astype(f32) + layer_scale * branch
     out_ref[...] = jnp.where(inside, result, 0.0).astype(bf16)
     back_unit = dot(back_before, up_ref[...], (1, 1)) * gain
@@ -518,19 +556,16 @@
             per_tile(),
             per_tile(),
             per_tile(),
-            whole(1, channels),
-            whole(1, channels),
+            whole(4, channels),
             whole(channels, hidden),
             whole(1, hidden),
             whole(hidden, channels),
-            whole(1, channels),
-            whole(1, channels),
         ],
         out_specs=(per_tile(), per_tile(), whole(channels, hidden), whole(hidden, channels)),
         name="token_block",
     )(
-        live, depth_rows, feature_rows, cot_rows, gain[None], shift[None], up, up_bias[None],
-        down, down_bias[None], scale[None],
+        live, depth_rows, feature_rows, cot_rows, jnp.stack([gain, shift, down_bias, scale]),
+        up, up_bias[None], down,
     )
 
 
@@ -578,23 +613,9 @@
         layer_scale,
     )
     back_depth = back_rows.reshape(rows_max, tile_cols, channels)
-    tap_list = []
-    for row_off in range(kernel):
-        for col_off in range(kernel):
-            tap_list.append(
-                jnp.sum(
-                    framed[row_off : row_off + rows_max, col_off : col_off + tile_cols].astype(
-                        jnp.float32
-                    )
-                    * back_depth.astype(jnp.float32),
-                    axis=(0, 1),
-                )
-            )
-    tap_list.extend([jnp.zeros_like(tap_list[0])] * (64 - kernel * kernel))
-    tap_terms = jnp.stack(tap_list, axis=0).reshape(8, 8, channels)
     rscale = 1.0 / math.sqrt(BAND_MEAN * lax.axis_size("lat") * tile_cols * lax.axis_size("lon"))
     up_part, down_part, grad_depth, arrivals = sum_weights(
-        sum_up, sum_down, tap_terms, halo_edges(back_depth, live_rows), rscale
+        sum_up, sum_down, framed, back_depth, halo_edges(back_depth, live_rows), rscale
     )
     grad_depth = grad_depth.reshape(64, channels)[: kernel * kernel]
     framed_back = framed_by(back_depth, arrivals, live_rows)

time: 162 us -> 161 us (level)
  Pallas kernels: 94.6 us -> 105 us
  other arithmetic: 44.8 us -> 36.3 us
  local copies, waits for them, and re-layouts: 17.1 us -> 15 us
    reduce_sum x3 -> x0, other arithmetic: 11.7 us -> none  [shards(): jnp.sum(framed[row_off:row_off + rows_max, col_off:col_off + tile_cols].a...]
    pallas_call x1, Pallas kernels: 43.7 us -> 54.1 us  [sum_weights(): pl.pallas_call(functools.partial(sum_kernel, rscale), out_shape=(jax.Shap...]
    mul x3, other arithmetic: 0.27 us -> 3.11 us  [shards(): framed[row_off:row_off + rows_max, col_off:col_off + tile_cols]]
    another operation x55 -> x5, local copies, waits for them, and re-layouts: 5.14 us -> 2.74 us  [the longest x4 2.73 us: token_block(): jnp.stack([gain, shift, down_bias, scale])]
    broadcast_in_dim x4 -> x0, local copies, waits for them, and re-layouts: 2.26 us -> none  [the longest x1 0.59 us: token_block(): down_bias[None]]
where the time goes in v4:
time: 161 us; the launch traced here: 160 us
  Pallas kernels  105 us (65%)
  other arithmetic  36.3 us (23%)
  local copies, waits for them, and re-layouts  15 us (9%)
  between operations  4.12 us (3%)
    pallas_call x1, Pallas kernels, sum_weights(): pl.pallas_call(functools.partial(sum_kernel, rscale), out_shape=(jax.Shap...  54.1 us
    pallas_call x1, Pallas kernels, gather_weights(): pl.pallas_call(gather_kernel, out_shape=(jax.ShapeDtypeStruct((48, 8, 153...  34.1 us
    pallas_call x1, Pallas kernels, token_block(): pl.pallas_call(token_kernel, grid=(pixels // tile,), out_shape=(jax.Shape...  16.7 us
    select_n x1, other arithmetic, shards(): jnp.where(inside[:, None, None], grad_local, jnp.zeros_like(grad_local))  12.5 us
    add x1, other arithmetic, shards(): depth_out + framed[row_off:row_off + rows_max, col_off:col_off + tile_col...  12.1 us

profile of v4, /device:TPU:1, one launch (start us, length us, event | category | flops | bytes accessed | tf_op | source)
XLA Modules:
  0.0 160.3 jit_solution(14382832329240112320)
XLA Ops:
  0.6 1.2 dynamic_slice.10
  5.1 0.7 iota_compare_fusion
  5.8 0.7 stack.15
  6.5 0.7 stack.16
  7.1 0.7 stack.17
  7.8 0.7 stack.18
  8.5 0.6 pad_maximum_fusion.2.vector_ref
  9.1 1.3 broadcast_in_dim.23.up_bias_ref
  10.4 0.9 convert_reduce_fusion.46
  11.4 0.8 fusion.2
  12.2 1.1 convert_reduce_fusion.48
  13.2 1.1 convert_reduce_fusion.47
  14.3 1.3 broadcast_multiply_fusion
  15.7 0.6 fusion.4
  16.3 0.7 fusion.5
  17.0 0.8 fusion.6
  17.7 34.1 %gather_weights.1 = (bf16[48,8,1536]{2,1,0:T(8,128)(2,1)}, bf16[192,8,384]{2,1,0:T(8,128)(2,1)}, bf16[32,3,384]{2,1,0:T(4,128)(2,1)}, bf16[32,3,384]{2,1,0:T(4,1...) custom-call(bf16[3,8,1536]{2,1,0:T(8,128)(2,1)} %bitcast.34, ...), custom_call_target="tpu_custom_call" | custom-call | tf_op jit(solution)/shard_map/gather_weights/pallas_call | solution.py:193
  51.9 1.0 maximum_select_fusion
  52.9 1.5 pad_maximum_fusion.1
  54.5 12.1 %multiply_add_fusion = f32[32,32,384]{2,1,0:T(8,128)} fusion(bf16[38,38,384]{2,1,0:T(8,128)(2,1)S(1)} %fusion.refs_2_, f32[384]{0:T(512)S(1)} %get-tuple-element.102, f32[384]{0:T(512)S(1)} %get-tuple-element.103, f32[384]{0:T(512)S(1)} %get-tuple-element.56, f32[384]{0:T(512)S(1)} %get-tuple-element.57, f32[384]{0:T(512)S(1)} %get-tuple-element.58, ...), kind=kLoop, calls=%fused_computation.3 | loop fusion | flops 57409536 | bytes 40183296 | tf_op jit(solution)/shard_map/add | solution.py:599
  66.7 16.7 %token_block.1 = (bf16[1024,384]{1,0:T(8,128)(2,1)}, bf16[1024,384]{1,0:T(8,128)(2,1)}, f32[384,1536]{1,0:T(8,128)}, f32[1536,384]{1,0:T(8,128)}) custom-call(s32[1]{0:T(128)} %bitcast.1.live_ref, f32[1024,384]{1,0:T(8,128)} %bitcast.17, bf16[1024,384]{1,0:T(8,128)(2,1)} %bitcast.23, bf16[1024,384]{1,0:T(8,128)(2,1)} %bitcast.24, ...), custom_call_target="tpu_custom_call" | custom-call | tf_op jit(solution)/shard_map/token_block/pallas_call | solution.py:545
  83.4 1.5 constant_dynamic-slice_fusion.4.refs_6_
  84.9 0.9 slice.647
  85.8 1.4 constant_dynamic-slice_fusion.1
  87.2 1.8 %fusion.3 = (bf16[32,3,384]{2,1,0:T(4,128)(2,1)}, bf16[32,3,384]{2,1,0:T(4,128)(2,1)}) fusion(bf16[32,32,384]{2,1,0:T(8,128)(2,1)} %bitcast.20), kind=kLoop, calls=%fused_computation.71 | loop fusion | bytes 294912 | tf_op jit(solution)/shard_map/slice | solution.py:62
  89.0 54.1 %sum_weights.1 = (f32[3,8,1536]{2,1,0:T(8,128)}, f32[12,8,384]{2,1,0:T(8,128)}, f32[8,8,384]{2,1,0:T(8,128)}, bf16[32,3,384]{2,1,0:T(4,128)(2,1)}, bf16[32,3,384...) custom-call(f32[48,8,1536]{2,1,0:T(8,128)} %bitcast.25, ...), custom_call_target="tpu_custom_call" | custom-call | tf_op jit(solution)/shard_map/sum_weights/pallas_call | solution.py:435
  143.2 1.0 maximum_select_fusion.2
  144.2 1.5 pad_maximum_fusion
  145.8 12.5 %broadcast_select_fusion = bf16[32,32,384]{2,1,0:T(8,128)(2,1)} fusion(pred[32]{0:T(512)(128)(4,1)S(1)} %iota_compare_fusion, f32[384]{0:T(512)S(1)} %get-tuple-element.102, bf16[38,38,384]{2,1,0:T(8,128)(2,1)S(1)} %fusion.1, f32[384]{0:T(512)S(1)} %get-tuple-element.103, f32[384]{0:T(512)S(1)} %get-tuple-element.56, f32[384]{0:T(512)S(1)} %get-tuple-element.57, ...), kind=kLoop, calls=%fused_computation.4 | loop fusion | flops 59375616 | bytes 40187424 | tf_op jit(solution)/shard_map/jit(_where)/select_n | solution.py:631
  158.3 0.6 reshape.84
  159.0 0.7 copy.21
  159.7 0.7 copy.22
  (30 shorter events, 0.2 us)
Async XLA Ops:
  51.9 2.6 %copy-start.8 = (bf16[3,32,384]{2,1,0:T(8,128)(2,1)S(1)}, bf16[3,32,384]{2,1,0:T(8,128)(2,1)}, u32[]{:S(2)}) copy-start(bf16[3,32,384]{2,1,0:T(8,128)(2,1)} %get-tuple-element.36) | copy-start | bytes 221188
  51.9 2.6 %copy-start.11 = (bf16[3,3,384]{2,1,0:T(4,128)(2,1)S(1)}, bf16[3,3,384]{2,1,0:T(4,128)(2,1)}, u32[]{:S(2)}) copy-start(bf16[3,3,384]{2,1,0:T(4,128)(2,1)} %get-tuple-element.35) | copy-start | bytes 20740
  51.9 2.6 %copy-start.12 = (bf16[3,3,384]{2,1,0:T(4,128)(2,1)S(1)}, bf16[3,3,384]{2,1,0:T(4,128)(2,1)}, u32[]{:S(2)}) copy-start(bf16[3,3,384]{2,1,0:T(4,128)(2,1)} %get-tuple-element.37) | copy-start | bytes 20740
  54.5 12.2 %copy-start = (bf16[38,38,384]{2,1,0:T(8,128)(2,1)}, bf16[38,38,384]{2,1,0:T(8,128)(2,1)S(1)}, u32[]{:S(2)}) copy-start(bf16[38,38,384]{2,1,0:T(8,128)(2,1)S(1)} %fusion.refs_2_) | copy-start | bytes 3326980
  85.8 3.2 %copy-start.3 = (bf16[96,384]{1,0:T(8,128)(2,1)}, bf16[96,384]{1,0:T(8,128)(2,1)S(1)}, u32[]{:S(2)}) copy-start(bf16[96,384]{1,0:T(8,128)(2,1)S(1)} %slice.647) | copy-start | bytes 221188
  89.0 55.2 %copy-start.1 = (bf16[1024,384]{1,0:T(8,128)(2,1)S(1)}, bf16[1024,384]{1,0:T(8,128)(2,1)}, u32[]{:S(2)}) copy-start(bf16[1024,384]{1,0:T(8,128)(2,1)} %get-tuple-element.43) | copy-start | bytes 2359300
  143.1 2.6 %copy-start.7 = (bf16[3,32,384]{2,1,0:T(8,128)(2,1)S(1)}, bf16[3,32,384]{2,1,0:T(8,128)(2,1)}, u32[]{:S(2)}) copy-start(bf16[3,32,384]{2,1,0:T(8,128)(2,1)} %get-tuple-element.50) | copy-start | bytes 221188
  143.1 2.6 %copy-start.9 = (bf16[3,3,384]{2,1,0:T(4,128)(2,1)S(1)}, bf16[3,3,384]{2,1,0:T(4,128)(2,1)}, u32[]{:S(2)}) copy-start(bf16[3,3,384]{2,1,0:T(4,128)(2,1)} %get-tuple-element.49) | copy-start | bytes 20740
  143.1 2.6 %copy-start.10 = (bf16[3,3,384]{2,1,0:T(4,128)(2,1)S(1)}, bf16[3,3,384]{2,1,0:T(4,128)(2,1)}, u32[]{:S(2)}) copy-start(bf16[3,3,384]{2,1,0:T(4,128)(2,1)} %get-tuple-element.51) | copy-start | bytes 20740
  143.1 2.6 %copy-start.2 = (bf16[32,32,384]{2,1,0:T(8,128)(2,1)S(1)}, bf16[32,32,384]{2,1,0:T(8,128)(2,1)}, u32[]{:S(2)}) copy-start(bf16[32,32,384]{2,1,0:T(8,128)(2,1)} %param.23) | copy-start | bytes 2359300
  145.8 12.5 %copy-start.6 = (f32[8,8,384]{2,1,0:T(8,128)S(1)}, f32[8,8,384]{2,1,0:T(8,128)}, u32[]{:S(2)}) copy-start(f32[8,8,384]{2,1,0:T(8,128)} %get-tuple-element.54) | copy-start | bytes 294916
  145.8 13.2 %copy-start.5 = (f32[3,8,1536]{2,1,0:T(8,128)S(1)}, f32[3,8,1536]{2,1,0:T(8,128)}, u32[]{:S(2)}) copy-start(f32[3,8,1536]{2,1,0:T(8,128)} %get-tuple-element.52) | copy-start | bytes 442372
  145.8 13.8 %copy-start.4 = (f32[12,8,384]{2,1,0:T(8,128)S(1)}, f32[12,8,384]{2,1,0:T(8,128)}, u32[]{:S(2)}) copy-start(f32[12,8,384]{2,1,0:T(8,128)} %get-tuple-element.53) | copy-start | bytes 442372

commit v5 on v4

--- a/solution.py
+++ b/solution.py
@@ -569,6 +569,58 @@
     )
 
 
+def depthwise_kernel(framed_ref, weight_ref, out_ref, framed, shifted):
+    f32 = jnp.float32
+
+    @pl.loop(0, 38)
+    def _(row):
+        framed[row] = framed_ref[row].astype(f32)
+
+    for col_off in range(7):
+
+        @pl.loop(0, 38)
+        def _(row):
+            shifted[row] = framed[row, col_off : col_off + 32]
+
+        for group in range(3):
+            lanes = slice(group * 128, group * 128 + 128)
+            taps = [
+                jnp.broadcast_to(
+                    weight_ref[off * 7 + col_off : off * 7 + col_off + 1, lanes], (8, 128)
+                )[None]
+                for off in range(7)
+            ]
+
+            @pl.loop(0, 16)
+            def _(pair):
+                rows = [
+                    shifted[pair * 2 + off, :, lanes].reshape(4, 8, 128) for off in range(8)
+                ]
+                for side in range(2):
+                    value = rows[side] * taps[0]
+                    for off in range(1, 7):
+                        value = value + rows[side + off] * taps[off]
+                    value = value.reshape(32, 128)
+                    if col_off:
+                        value = value + out_ref[pair * 2 + side, :, lanes]
+                    out_ref[pair * 2 + side, :, lanes] = value
+
+
+def depthwise(framed, weights):
+    vmem = pl.BlockSpec(memory_space=pltpu.VMEM)
+    return pl.pallas_call(
+        depthwise_kernel,
+        out_shape=jax.ShapeDtypeStruct((32, 32, 384), jnp.float32),
+        in_specs=[vmem, vmem],
+        out_specs=vmem,
+        scratch_shapes=[
+            pltpu.VMEM((38, 38, 384), jnp.float32),
+            pltpu.VMEM((38, 32, 384), jnp.float32),
+        ],
+        name="depthwise",
+    )(framed, weights)
+
+
 def shards(
     feature,
     coverage,
@@ -593,12 +645,8 @@
         up_weight, down_weight, halo_edges(masked, live_rows)
     )
     framed = framed_by(masked, arrivals, live_rows)
-    depth_out = jnp.zeros((rows_max, tile_cols, channels), jnp.float32)
-    for row_off in range(kernel):
-        for col_off in range(kernel):
-            depth_out = depth_out + framed[
-                row_off : row_off + rows_max, col_off : col_off + tile_cols
-            ].astype(jnp.float32) * depth_weight[row_off, col_off].astype(jnp.float32)
+    weights = depth_weight.astype(jnp.float32).reshape(kernel * kernel, channels)
+    depth_out = depthwise(framed, weights)
     block_rows, back_rows, sum_up, sum_down = token_block(
         (live_rows * tile_cols).reshape(1),
         depth_out.reshape(-1, channels),
@@ -619,12 +667,7 @@
     )
     grad_depth = grad_depth.reshape(64, channels)[: kernel * kernel]
     framed_back = framed_by(back_depth, arrivals, live_rows)
-    spread = jnp.zeros((rows_max, tile_cols, channels), jnp.float32)
-    for row_off in range(kernel):
-        for col_off in range(kernel):
-            spread = spread + framed_back[
-                6 - row_off : 6 - row_off + rows_max, 6 - col_off : 6 - col_off + tile_cols
-            ].astype(jnp.float32) * depth_weight[row_off, col_off].astype(jnp.float32)
+    spread = depthwise(framed_back, weights[::-1])
     grad_local = (
         cotangent.astype(jnp.float32) + covered.astype(jnp.float32)[:, :, None] * spread
     ).astype(jnp.bfloat16)

time: 161 us -> 164 us (1.019)
  other arithmetic: 36.3 us -> 11.2 us
  Pallas kernels: 105 us -> 130 us
  local copies, waits for them, and re-layouts: 15 us -> 18.4 us
    pallas_call x0 -> x2, Pallas kernels: none -> 24.7 us  [depthwise(): pl.pallas_call(depthwise_kernel, out_shape=jax.ShapeDtypeStruct((32, 32,...]
    add x1 -> x0, other arithmetic: 12.1 us -> none  [shards(): depth_out + framed[row_off:row_off + rows_max, col_off:col_off + tile_col...]
    select_n x1, other arithmetic: 12.5 us -> 2.71 us  [shards(): jnp.where(inside[:, None, None], grad_local, jnp.zeros_like(grad_local))]
    mul x3 -> x0, other arithmetic: 3.11 us -> none  [shards(): framed[row_off:row_off + rows_max, col_off:col_off + tile_cols]]
where the time goes in v5:
time: 164 us; the launch traced here: 163 us
  Pallas kernels  130 us (79%)
  local copies, waits for them, and re-layouts  18.4 us (11%)
  other arithmetic  11.2 us (7%)
  between operations  4.12 us (3%)
    pallas_call x1, Pallas kernels, sum_weights(): pl.pallas_call(functools.partial(sum_kernel, rscale), out_shape=(jax.Shap...  54.1 us
    pallas_call x1, Pallas kernels, gather_weights(): pl.pallas_call(gather_kernel, out_shape=(jax.ShapeDtypeStruct((48, 8, 153...  34.1 us
    pallas_call x2, Pallas kernels, depthwise(): pl.pallas_call(depthwise_kernel, out_shape=jax.ShapeDtypeStruct((32, 32,...  24.7 us
    pallas_call x1, Pallas kernels, token_block(): pl.pallas_call(token_kernel, grid=(pixels // tile,), out_shape=(jax.Shape...  16.7 us

profile of v5, /device:TPU:1, one launch (start us, length us, event | category | flops | bytes accessed | tf_op | source)
XLA Modules:
  0.0 163.4 jit_solution(11526423771514796726)
XLA Ops:
  0.6 1.2 dynamic_slice.10
  5.1 0.7 iota_compare_fusion
  5.8 0.7 stack.15
  6.5 0.7 stack.16
  7.1 0.7 stack.17
  7.8 0.7 stack.18
  9.1 1.3 broadcast_in_dim.32.up_bias_ref
  10.4 0.8 fusion.3
  11.2 0.8 reshape.93.weight_ref
  12.0 1.3 rev.3.weight_ref
  13.3 1.3 broadcast_multiply_fusion
  14.6 0.6 fusion.5
  15.3 0.7 fusion.6
  15.9 0.8 fusion.7
  16.7 34.1 %gather_weights.1 = (bf16[48,8,1536]{2,1,0:T(8,128)(2,1)}, bf16[192,8,384]{2,1,0:T(8,128)(2,1)}, bf16[32,3,384]{2,1,0:T(4,128)(2,1)}, bf16[32,3,384]{2,1,0:T(4,1...) custom-call(bf16[3,8,1536]{2,1,0:T(8,128)(2,1)} %bitcast.34, ...), custom_call_target="tpu_custom_call" | custom-call | tf_op jit(solution)/shard_map/gather_weights/pallas_call | solution.py:193
  50.9 1.0 maximum_select_fusion
  51.9 1.5 pad_maximum_fusion.1
  53.5 1.0 copy-done
  54.5 12.4 %depthwise.2 = f32[32,32,384]{2,1,0:T(8,128)} custom-call(bf16[38,38,384]{2,1,0:T(8,128)(2,1)} %copy-done, f32[49,384]{1,0:T(8,128)} %copy-done.4), custom_call_target="tpu_custom_call" | custom-call | tf_op jit(solution)/shard_map/depthwise/pallas_call | solution.py:611
  66.9 16.7 %token_block.1 = (bf16[1024,384]{1,0:T(8,128)(2,1)}, bf16[1024,384]{1,0:T(8,128)(2,1)}, f32[384,1536]{1,0:T(8,128)}, f32[1536,384]{1,0:T(8,128)}) custom-call(s32[1]{0:T(128)} %bitcast.1.live_ref, f32[1024,384]{1,0:T(8,128)} %bitcast.17, bf16[1024,384]{1,0:T(8,128)(2,1)} %bitcast.23, bf16[1024,384]{1,0:T(8,128)(2,1)} %bitcast.24, ...), custom_call_target="tpu_custom_call" | custom-call | tf_op jit(solution)/shard_map/token_block/pallas_call | solution.py:545
  83.6 1.5 constant_dynamic-slice_fusion.4.refs_6_
  85.1 0.9 slice.59
  86.0 1.4 constant_dynamic-slice_fusion.1
  87.4 1.8 %fusion.4 = (bf16[32,3,384]{2,1,0:T(4,128)(2,1)}, bf16[32,3,384]{2,1,0:T(4,128)(2,1)}) fusion(bf16[32,32,384]{2,1,0:T(8,128)(2,1)} %bitcast.20), kind=kLoop, calls=%fused_computation.21 | loop fusion | bytes 294912 | tf_op jit(solution)/shard_map/slice | solution.py:62
  89.2 54.1 %sum_weights.1 = (f32[3,8,1536]{2,1,0:T(8,128)}, f32[12,8,384]{2,1,0:T(8,128)}, f32[8,8,384]{2,1,0:T(8,128)}, bf16[32,3,384]{2,1,0:T(4,128)(2,1)}, bf16[32,3,384...) custom-call(f32[48,8,1536]{2,1,0:T(8,128)} %bitcast.25, ...), custom_call_target="tpu_custom_call" | custom-call | tf_op jit(solution)/shard_map/sum_weights/pallas_call | solution.py:435
  143.3 1.0 maximum_select_fusion.2
  144.3 1.5 pad_maximum_fusion
  146.0 0.6 reshape.91
  147.0 12.3 %depthwise.3 = f32[32,32,384]{2,1,0:T(8,128)} custom-call(bf16[38,38,384]{2,1,0:T(8,128)(2,1)} %copy-done.2, f32[49,384]{1,0:T(8,128)} %rev.3.weight_ref), custom_call_target="tpu_custom_call" | custom-call | tf_op jit(solution)/shard_map/depthwise/pallas_call | solution.py:611
  159.3 2.7 %fusion = bf16[32,32,384]{2,1,0:T(8,128)(2,1)} fusion(f32[32,32,384]{2,1,0:T(8,128)} %depthwise.3, bf16[32,32,384]{2,1,0:T(8,128)(2,1)S(1)} %copy-done.3, f32[32,32]{1,0:T(8,128)S(1)} %get-tuple-element.55, pred[32]{0:T(512)(128)(4,1)S(1)} %iota_compare_fusion), kind=kLoop, calls=%fused_computation.3 | loop fusion | flops 1966080 | bytes 3149856 | tf_op jit(solution)/shard_map/jit(_where)/select_n | solution.py:674
  162.0 0.7 copy.21
  162.7 0.7 copy.22
  (34 shorter events, 1.2 us)
Async XLA Ops:
  12.0 39.9 %copy-start.4 = (f32[49,384]{1,0:T(8,128)}, f32[49,384]{1,0:T(8,128)S(1)}, u32[]{:S(2)}) copy-start(f32[49,384]{1,0:T(8,128)S(1)} %reshape.93.weight_ref) | copy-start | bytes 225796
  50.8 2.6 %copy-start.10 = (bf16[3,32,384]{2,1,0:T(8,128)(2,1)S(1)}, bf16[3,32,384]{2,1,0:T(8,128)(2,1)}, u32[]{:S(2)}) copy-start(bf16[3,32,384]{2,1,0:T(8,128)(2,1)} %get-tuple-element.36) | copy-start | bytes 221188
  50.9 2.6 %copy-start.13 = (bf16[3,3,384]{2,1,0:T(4,128)(2,1)S(1)}, bf16[3,3,384]{2,1,0:T(4,128)(2,1)}, u32[]{:S(2)}) copy-start(bf16[3,3,384]{2,1,0:T(4,128)(2,1)} %get-tuple-element.35) | copy-start | bytes 20740
  50.9 2.6 %copy-start.14 = (bf16[3,3,384]{2,1,0:T(4,128)(2,1)S(1)}, bf16[3,3,384]{2,1,0:T(4,128)(2,1)}, u32[]{:S(2)}) copy-start(bf16[3,3,384]{2,1,0:T(4,128)(2,1)} %get-tuple-element.37) | copy-start | bytes 20740
  53.5 1.0 copy-start
  86.0 3.2 %copy-start.5 = (bf16[96,384]{1,0:T(8,128)(2,1)}, bf16[96,384]{1,0:T(8,128)(2,1)S(1)}, u32[]{:S(2)}) copy-start(bf16[96,384]{1,0:T(8,128)(2,1)S(1)} %slice.59) | copy-start | bytes 221188
  89.2 55.1 %copy-start.1 = (bf16[1024,384]{1,0:T(8,128)(2,1)S(1)}, bf16[1024,384]{1,0:T(8,128)(2,1)}, u32[]{:S(2)}) copy-start(bf16[1024,384]{1,0:T(8,128)(2,1)} %get-tuple-element.43) | copy-start | bytes 2359300
  143.3 2.6 %copy-start.9 = (bf16[3,32,384]{2,1,0:T(8,128)(2,1)S(1)}, bf16[3,32,384]{2,1,0:T(8,128)(2,1)}, u32[]{:S(2)}) copy-start(bf16[3,32,384]{2,1,0:T(8,128)(2,1)} %get-tuple-element.50) | copy-start | bytes 221188
  143.3 2.6 %copy-start.11 = (bf16[3,3,384]{2,1,0:T(4,128)(2,1)S(1)}, bf16[3,3,384]{2,1,0:T(4,128)(2,1)}, u32[]{:S(2)}) copy-start(bf16[3,3,384]{2,1,0:T(4,128)(2,1)} %get-tuple-element.49) | copy-start | bytes 20740
  143.3 2.6 %copy-start.12 = (bf16[3,3,384]{2,1,0:T(4,128)(2,1)S(1)}, bf16[3,3,384]{2,1,0:T(4,128)(2,1)}, u32[]{:S(2)}) copy-start(bf16[3,3,384]{2,1,0:T(4,128)(2,1)} %get-tuple-element.51) | copy-start | bytes 20740
  143.3 2.6 %copy-start.8 = (f32[8,8,384]{2,1,0:T(8,128)S(1)}, f32[8,8,384]{2,1,0:T(8,128)}, u32[]{:S(2)}) copy-start(f32[8,8,384]{2,1,0:T(8,128)} %get-tuple-element.54) | copy-start | bytes 294916
  145.9 1.1 copy-start.2
  146.0 13.4 %copy-start.3 = (bf16[32,32,384]{2,1,0:T(8,128)(2,1)S(1)}, bf16[32,32,384]{2,1,0:T(8,128)(2,1)}, u32[]{:S(2)}) copy-start(bf16[32,32,384]{2,1,0:T(8,128)(2,1)} %param.23) | copy-start | bytes 2359300
  159.3 2.7 %copy-start.7 = (f32[3,8,1536]{2,1,0:T(8,128)S(1)}, f32[3,8,1536]{2,1,0:T(8,128)}, u32[]{:S(2)}) copy-start(f32[3,8,1536]{2,1,0:T(8,128)} %get-tuple-element.52) | copy-start | bytes 442372
  159.3 3.4 %copy-start.6 = (f32[12,8,384]{2,1,0:T(8,128)S(1)}, f32[12,8,384]{2,1,0:T(8,128)}, u32[]{:S(2)}) copy-start(f32[12,8,384]{2,1,0:T(8,128)} %get-tuple-element.53) | copy-start | bytes 442372

commit v6 on v5

--- a/solution.py
+++ b/solution.py
@@ -480,7 +480,7 @@
 
 
 def token_kernel(
-    live_ref, depth_ref, feature_ref, cot_ref, vector_ref, up_ref, up_bias_ref, down_ref,
+    live_ref, depth_ref, feature_ref, cot_ref, gain_ref, shift_ref, down_bias_ref, scale_ref, up_ref, up_bias_ref, down_ref,
     out_ref, back_ref, sum_up_ref, sum_down_ref,
 ):
     step = pl.program_id(0)
@@ -498,13 +498,15 @@
     index = step * rows + lax.broadcasted_iota(jnp.int32, (rows, 1), 0)
     inside = index < live_ref[0]
     depth = depth_ref[...]
-    gain, shift, down_bias, layer_scale = (vector_ref[i : i + 1, :] for i in range(4))
+    gain, shift, down_bias, layer_scale = (
+        ref[...].reshape(1, -1) for ref in (gain_ref, shift_ref, down_bias_ref, scale_ref)
+    )
     offset = depth - jnp.mean(depth, axis=-1, keepdims=True)
     scale_inv = lax.rsqrt(jnp.mean(offset * offset, axis=-1, keepdims=True) + EPSILON)
     standard = offset * scale_inv
     normed = (standard * gain + shift).astype(bf16)
     upstream = jnp.where(inside, layer_scale * cot_ref[...].astype(f32), 0.0).astype(bf16)
-    before = dot(normed, up_ref[...], (1, 0)) + up_bias_ref[...]
+    before = dot(normed, up_ref[...], (1, 0)) + up_bias_ref[...].reshape(1, -1)
     square = before * before
     tangent = jnp.tanh(SQRT_TWO_PI * (before + CUBIC * square * before))
     half = 0.5 * (1.0 + tangent)
@@ -556,20 +558,19 @@
             per_tile(),
             per_tile(),
             per_tile(),
-            whole(4, channels),
+            *[pl.BlockSpec((channels,), lambda i: (0,))] * 4,
             whole(channels, hidden),
-            whole(1, hidden),
+            pl.BlockSpec((hidden,), lambda i: (0,)),
             whole(hidden, channels),
         ],
         out_specs=(per_tile(), per_tile(), whole(channels, hidden), whole(hidden, channels)),
         name="token_block",
     )(
-        live, depth_rows, feature_rows, cot_rows, jnp.stack([gain, shift, down_bias, scale]),
-        up, up_bias[None], down,
-    )
-
-
-def depthwise_kernel(framed_ref, weight_ref, out_ref, framed, shifted):
+        live, depth_rows, feature_rows, cot_rows, gain, shift, down_bias, scale, up, up_bias, down,
+    )
+
+
+def depthwise_kernel(flip, framed_ref, weight_ref, out_ref, framed, shifted):
     f32 = jnp.float32
 
     @pl.loop(0, 38)
@@ -586,7 +587,12 @@
             lanes = slice(group * 128, group * 128 + 128)
             taps = [
                 jnp.broadcast_to(
-                    weight_ref[off * 7 + col_off : off * 7 + col_off + 1, lanes], (8, 128)
+                    weight_ref[
+                        6 - off if flip else off,
+                        6 - col_off if flip else col_off : 7 - col_off if flip else col_off + 1,
+                        lanes,
+                    ].astype(f32),
+                    (8, 128),
                 )[None]
                 for off in range(7)
             ]
@@ -606,10 +612,10 @@
                     out_ref[pair * 2 + side, :, lanes] = value
 
 
-def depthwise(framed, weights):
+def depthwise(framed, weights, flip):
     vmem = pl.BlockSpec(memory_space=pltpu.VMEM)
     return pl.pallas_call(
-        depthwise_kernel,
+        functools.partial(depthwise_kernel, flip),
         out_shape=jax.ShapeDtypeStruct((32, 32, 384), jnp.float32),
         in_specs=[vmem, vmem],
         out_specs=vmem,
@@ -645,8 +651,7 @@
         up_weight, down_weight, halo_edges(masked, live_rows)
     )
     framed = framed_by(masked, arrivals, live_rows)
-    weights = depth_weight.astype(jnp.float32).reshape(kernel * kernel, channels)
-    depth_out = depthwise(framed, weights)
+    depth_out = depthwise(framed, depth_weight, False)
     block_rows, back_rows, sum_up, sum_down = token_block(
         (live_rows * tile_cols).reshape(1),
         depth_out.reshape(-1, channels),
@@ -667,7 +672,7 @@
     )
     grad_depth = grad_depth.reshape(64, channels)[: kernel * kernel]
     framed_back = framed_by(back_depth, arrivals, live_rows)
-    spread = depthwise(framed_back, weights[::-1])
+    spread = depthwise(framed_back, depth_weight, True)
     grad_local = (
         cotangent.astype(jnp.float32) + covered.astype(jnp.float32)[:, :, None] * spread
     ).astype(jnp.bfloat16)

time: 164 us -> 158 us (0.963)
  local copies, waits for them, and re-layouts: 18.4 us -> 12.3 us
    another operation x5 -> x1, local copies, waits for them, and re-layouts: 2.74 us -> 0.01 us  [the longest x4 2.73 us: token_block(): jnp.stack([gain, shift, down_bias, scale])]
where the time goes in v6:
time: 158 us; the launch traced here: 157 us
  Pallas kernels  130 us (82%)
  local copies, waits for them, and re-layouts  12.3 us (8%)
  other arithmetic  10.6 us (7%)
  between operations  4.1 us (3%)
    pallas_call x1, Pallas kernels, sum_weights(): pl.pallas_call(functools.partial(sum_kernel, rscale), out_shape=(jax.Shap...  54.1 us
    pallas_call x1, Pallas kernels, gather_weights(): pl.pallas_call(gather_kernel, out_shape=(jax.ShapeDtypeStruct((48, 8, 153...  34.1 us
    pallas_call x2, Pallas kernels, depthwise(): pl.pallas_call(functools.partial(depthwise_kernel, flip), out_shape=jax.S...  25.1 us
    pallas_call x1, Pallas kernels, token_block(): pl.pallas_call(token_kernel, grid=(pixels // tile,), out_shape=(jax.Shape...  16.8 us

profile of v6, /device:TPU:1, one launch (start us, length us, event | category | flops | bytes accessed | tf_op | source)
XLA Modules:
  0.0 157.1 jit_solution(9953544459539096975)
XLA Ops:
  0.6 1.2 dynamic_slice.10
  5.1 0.7 iota_compare_fusion
  5.8 0.8 fusion.3
  6.6 1.3 broadcast_multiply_fusion
  7.9 0.6 fusion.5
  8.5 0.7 fusion.6
  9.2 0.8 fusion.7
  10.0 34.1 %gather_weights.1 = (bf16[48,8,1536]{2,1,0:T(8,128)(2,1)}, bf16[192,8,384]{2,1,0:T(8,128)(2,1)}, bf16[32,3,384]{2,1,0:T(4,128)(2,1)}, bf16[32,3,384]{2,1,0:T(4,1...) custom-call(bf16[3,8,1536]{2,1,0:T(8,128)(2,1)} %bitcast.34, ...), custom_call_target="tpu_custom_call" | custom-call | tf_op jit(solution)/shard_map/gather_weights/pallas_call | solution.py:193
  44.1 0.0 copy-start.9
  44.1 0.0 copy-start.12
  44.1 0.0 copy-start.13
  44.1 1.0 maximum_select_fusion
  45.1 1.5 pad_maximum_fusion.1
  46.7 0.1 fusion.1.framed_ref.refs_2_
  46.8 1.0 copy-done
  47.8 12.6 %depthwise.2 = f32[32,32,384]{2,1,0:T(8,128)} custom-call(bf16[38,38,384]{2,1,0:T(8,128)(2,1)} %copy-done, bf16[7,7,384]{2,1,0:T(8,128)(2,1)} %weight_ref.3), custom_call_target="tpu_custom_call" | custom-call | tf_op jit(solution)/shard_map/depthwise/pallas_call | solution.py:617
  60.3 16.8 %token_block.1 = (bf16[1024,384]{1,0:T(8,128)(2,1)}, bf16[1024,384]{1,0:T(8,128)(2,1)}, f32[384,1536]{1,0:T(8,128)}, f32[1536,384]{1,0:T(8,128)}) custom-call(s32[1]{0:T(128)} %bitcast.1.live_ref, f32[1024,384]{1,0:T(8,128)} %bitcast.17, bf16[1024,384]{1,0:T(8,128)(2,1)} %bitcast.23, bf16[1024,384]{1,0:T(8,128)(2,1)} %bitcast.24, f32[384]{0:T(512)} %gain_ref.1, ...), custom_call_target="tpu_custom_call" | custom-call | tf_op jit(solution)/shard_map/token_block/pallas_call | solution.py:547
  77.1 1.5 constant_dynamic-slice_fusion.4.refs_6_
  78.7 0.9 slice.59
  79.6 1.4 constant_dynamic-slice_fusion.1
  81.0 1.8 %fusion.4 = (bf16[32,3,384]{2,1,0:T(4,128)(2,1)}, bf16[32,3,384]{2,1,0:T(4,128)(2,1)}) fusion(bf16[32,32,384]{2,1,0:T(8,128)(2,1)} %bitcast.20), kind=kLoop, calls=%fused_computation.20 | loop fusion | bytes 294912 | tf_op jit(solution)/shard_map/slice | solution.py:62
  82.8 54.1 %sum_weights.1 = (f32[3,8,1536]{2,1,0:T(8,128)}, f32[12,8,384]{2,1,0:T(8,128)}, f32[8,8,384]{2,1,0:T(8,128)}, bf16[32,3,384]{2,1,0:T(4,128)(2,1)}, bf16[32,3,384...) custom-call(f32[48,8,1536]{2,1,0:T(8,128)} %bitcast.25, ...), custom_call_target="tpu_custom_call" | custom-call | tf_op jit(solution)/shard_map/sum_weights/pallas_call | solution.py:435
  136.9 1.0 maximum_select_fusion.2
  137.9 1.5 pad_maximum_fusion
  139.4 0.1 fusion.2.framed_ref
  139.5 0.0 copy-start.3
  139.5 0.6 reshape.84
  140.2 0.4 copy-done.2
  140.6 12.5 %depthwise.3 = f32[32,32,384]{2,1,0:T(8,128)} custom-call(bf16[38,38,384]{2,1,0:T(8,128)(2,1)} %copy-done.2, bf16[7,7,384]{2,1,0:T(8,128)(2,1)} %weight_ref.3), custom_call_target="tpu_custom_call" | custom-call | tf_op jit(solution)/shard_map/depthwise/pallas_call | solution.py:617
  153.1 2.7 %fusion = bf16[32,32,384]{2,1,0:T(8,128)(2,1)} fusion(f32[32,32,384]{2,1,0:T(8,128)} %depthwise.3, bf16[32,32,384]{2,1,0:T(8,128)(2,1)S(1)} %copy-done.3, f32[32,32]{1,0:T(8,128)S(1)} %get-tuple-element.55, pred[32]{0:T(512)(128)(4,1)S(1)} %iota_compare_fusion), kind=kLoop, calls=%fused_computation.3 | loop fusion | flops 1966080 | bytes 3149856 | tf_op jit(solution)/shard_map/jit(_where)/select_n | solution.py:679
  155.8 0.7 copy.21
  156.5 0.7 copy.22
  (24 shorter events, 0.1 us)
Async XLA Ops:
  44.1 2.6 %copy-start.9 = (bf16[3,32,384]{2,1,0:T(8,128)(2,1)S(1)}, bf16[3,32,384]{2,1,0:T(8,128)(2,1)}, u32[]{:S(2)}) copy-start(bf16[3,32,384]{2,1,0:T(8,128)(2,1)} %get-tuple-element.36) | copy-start | bytes 221188
  44.1 2.6 %copy-start.12 = (bf16[3,3,384]{2,1,0:T(4,128)(2,1)S(1)}, bf16[3,3,384]{2,1,0:T(4,128)(2,1)}, u32[]{:S(2)}) copy-start(bf16[3,3,384]{2,1,0:T(4,128)(2,1)} %get-tuple-element.35) | copy-start | bytes 20740
  44.1 2.6 %copy-start.13 = (bf16[3,3,384]{2,1,0:T(4,128)(2,1)S(1)}, bf16[3,3,384]{2,1,0:T(4,128)(2,1)}, u32[]{:S(2)}) copy-start(bf16[3,3,384]{2,1,0:T(4,128)(2,1)} %get-tuple-element.37) | copy-start | bytes 20740
  46.8 1.0 copy-start
  79.6 3.2 %copy-start.4 = (bf16[96,384]{1,0:T(8,128)(2,1)}, bf16[96,384]{1,0:T(8,128)(2,1)S(1)}, u32[]{:S(2)}) copy-start(bf16[96,384]{1,0:T(8,128)(2,1)S(1)} %slice.59) | copy-start | bytes 221188
  82.7 55.1 %copy-start.1 = (bf16[1024,384]{1,0:T(8,128)(2,1)S(1)}, bf16[1024,384]{1,0:T(8,128)(2,1)}, u32[]{:S(2)}) copy-start(bf16[1024,384]{1,0:T(8,128)(2,1)} %get-tuple-element.43) | copy-start | bytes 2359300
  136.8 2.6 %copy-start.8 = (bf16[3,32,384]{2,1,0:T(8,128)(2,1)S(1)}, bf16[3,32,384]{2,1,0:T(8,128)(2,1)}, u32[]{:S(2)}) copy-start(bf16[3,32,384]{2,1,0:T(8,128)(2,1)} %get-tuple-element.50) | copy-start | bytes 221188
  136.8 2.6 %copy-start.10 = (bf16[3,3,384]{2,1,0:T(4,128)(2,1)S(1)}, bf16[3,3,384]{2,1,0:T(4,128)(2,1)}, u32[]{:S(2)}) copy-start(bf16[3,3,384]{2,1,0:T(4,128)(2,1)} %get-tuple-element.49) | copy-start | bytes 20740
  136.8 2.6 %copy-start.11 = (bf16[3,3,384]{2,1,0:T(4,128)(2,1)S(1)}, bf16[3,3,384]{2,1,0:T(4,128)(2,1)}, u32[]{:S(2)}) copy-start(bf16[3,3,384]{2,1,0:T(4,128)(2,1)} %get-tuple-element.51) | copy-start | bytes 20740
  136.9 2.6 %copy-start.7 = (f32[8,8,384]{2,1,0:T(8,128)S(1)}, f32[8,8,384]{2,1,0:T(8,128)}, u32[]{:S(2)}) copy-start(f32[8,8,384]{2,1,0:T(8,128)} %get-tuple-element.54) | copy-start | bytes 294916
  139.5 1.1 copy-start.2
  139.5 13.6 %copy-start.3 = (bf16[32,32,384]{2,1,0:T(8,128)(2,1)S(1)}, bf16[32,32,384]{2,1,0:T(8,128)(2,1)}, u32[]{:S(2)}) copy-start(bf16[32,32,384]{2,1,0:T(8,128)(2,1)} %param.23) | copy-start | bytes 2359300
  153.1 2.7 %copy-start.6 = (f32[3,8,1536]{2,1,0:T(8,128)S(1)}, f32[3,8,1536]{2,1,0:T(8,128)}, u32[]{:S(2)}) copy-start(f32[3,8,1536]{2,1,0:T(8,128)} %get-tuple-element.52) | copy-start | bytes 442372
  153.1 3.4 %copy-start.5 = (f32[12,8,384]{2,1,0:T(8,128)S(1)}, f32[12,8,384]{2,1,0:T(8,128)}, u32[]{:S(2)}) copy-start(f32[12,8,384]{2,1,0:T(8,128)} %get-tuple-element.53) | copy-start | bytes 442372
